TPU v7x, 32 devices: a whole 2x2x4 slice. The times are simulated.
32 devices in a mesh: dp: 8 (over z, x), tensor: 4 (over y, core).
Axes of the slice: x: 2, y: 2, z: 4, core: 2. Of those that a mesh axis runs over, the one named last changes fastest.
Arguments:
- hidden_in: bfloat16 [4096, 1024], P(('dp', 'tensor')), may hold values from -8 to 8
- cotangent: bfloat16 [4096, 1024], P(('dp', 'tensor')), may hold values from -6 to 6
- lengths: int32 [8], P('dp'), may hold values from 128 to 512, as said below
- query_weight: bfloat16 [1024, 1024], P('dp', 'tensor'), as said below
- key_weight: bfloat16 [1024, 1024], P('dp', 'tensor'), as said below
- value_weight: bfloat16 [1024, 1024], P('dp', 'tensor'), may hold values from -0.1875 to 0.1875
- output_weight: bfloat16 [1024, 1024], P('tensor', 'dp'), may hold values from -1 to 1
- up_weight: bfloat16 [1024, 4096], P('dp', 'tensor'), may hold values from -0.1875 to 0.1875
- down_weight: bfloat16 [4096, 1024], P('tensor', 'dp'), may hold values from -0.09375 to 0.09375
- query_bias: float32 [1024], P('tensor'), may hold values from -3 to 3
- value_bias: float32 [1024], P('tensor'), may hold values from -3 to 3
- output_bias: float32 [1024], replicated, may hold values from -3 to 3
- up_bias: float32 [4096], P('tensor'), may hold values from -3 to 3
- down_bias: float32 [1024], replicated, may hold values from -3 to 3
- first_gain: float32 [1024], replicated, may hold values from 0.5 to 1.5
- first_shift: float32 [1024], replicated, may hold values from -3 to 3
- second_gain: float32 [1024], replicated, may hold values from 0.5 to 1.5
- second_shift: float32 [1024], replicated, may hold values from -3 to 3
Outputs:
- hidden_out: bfloat16 [4096, 1024], P(('dp', 'tensor'))
- grad_in: bfloat16 [4096, 1024], P(('dp', 'tensor'))
- grad_query_weight: float32 [1024, 1024], P('dp', 'tensor')
- grad_key_weight: float32 [1024, 1024], P('dp', 'tensor')
- grad_value_weight: float32 [1024, 1024], P('dp', 'tensor')
- grad_output_weight: float32 [1024, 1024], P('tensor', 'dp')
- grad_up_weight: float32 [1024, 4096], P('dp', 'tensor')
- grad_down_weight: float32 [4096, 1024], P('tensor', 'dp')
- grad_query_bias: float32 [1024], P('tensor')
- grad_value_bias: float32 [1024], P('tensor')
- grad_output_bias: float32 [1024], replicated
- grad_up_bias: float32 [4096], P('tensor')
- grad_down_bias: float32 [1024], replicated
- grad_first_gain: float32 [1024], replicated
- grad_first_shift: float32 [1024], replicated
- grad_second_gain: float32 [1024], replicated
- grad_second_shift: float32 [1024], replicated
Inputs may be any that keep to these rules, and one draw needn't show every extreme that they name: `lengths`: positions of a sequence at or past its entry are padding keys. Some sequence is full. `query_weight`: A projection scaled by its fan-in. `key_weight`: A projection scaled by its fan-in.
All inputs are finite; a program needn't handle non-finite values.
Results may differ from a plain program's by a relative error of at most 0.02.
Values may be sent and summed in bfloat16 or wider, within the bound.
No kernel may reach another device: no remote copies, remote signals or barrier semaphores. Data moves between devices by JAX's collectives and lax.ppermute only.
A program may use at most 128 MiB of HBM per device.

v0:
```python
import functools

import jax
import jax.numpy as jnp
from jax import lax
from jax.experimental import pallas as pl
from jax.experimental.layout import Layout, with_layout_constraint
from jax.experimental.pallas import tpu as pltpu
from jax.sharding import PartitionSpec as P


HD = 64


EPSILON = 1e-12
ROOT_HALF = 0.7071067811865476
INV_ROOT_TWO_PI = 0.3989422804014327
MASKED = -1e30
BF16 = jnp.bfloat16
F32 = jnp.float32
KERNEL_VMEM = 16 << 20


def matmul(left_side, right_side):
    return jnp.dot(left_side, right_side, preferred_element_type=F32)


def matmul_nt(left_side, right_side):
    return lax.dot_general(left_side, right_side, (((1,), (1,)), ((), ())), preferred_element_type=F32)


def matmul_tn(left_side, right_side):
    return lax.dot_general(left_side, right_side, (((0,), (0,)), ((), ())), preferred_element_type=F32)


def gelu_value(pre_act):
    return pre_act * 0.5 * (1.0 + lax.erf(pre_act * ROOT_HALF))


def gelu_slope(pre_act):
    cumulative = 0.5 * (1.0 + lax.erf(pre_act * ROOT_HALF))
    density = jnp.exp(-0.5 * pre_act * pre_act) * INV_ROOT_TWO_PI
    return cumulative + pre_act * density


def norm_forward(summed, gain_vector, shift_vector):
    centre = summed - jnp.mean(summed, axis=-1, keepdims=True)
    spread = jnp.mean(centre * centre, axis=-1, keepdims=True)
    inverse = lax.rsqrt(spread + EPSILON)
    normed = centre * inverse
    return (normed * gain_vector + shift_vector, normed, inverse)


def norm_backward(upstream, gain_vector, normed, inverse):
    scaled = upstream * gain_vector
    return inverse * (
        scaled
        - jnp.mean(scaled, axis=-1, keepdims=True)
        - normed * jnp.mean(scaled * normed, axis=-1, keepdims=True)
    )


def swap(array, axis, bit):
    size = lax.axis_size(axis)
    return lax.ppermute(array, axis, [(i, i ^ bit) for i in range(size)])


def gather_rows(block):
    far = swap(block, "tensor", 2)
    other_core = swap(block, "tensor", 1)
    far_core = swap(far, "tensor", 1)
    return jnp.concatenate([block, other_core, far, far_core], axis=0)


def scatter_rows(partial):
    rows = partial.shape[0] // 4
    own, other_core, far, far_core = (partial[i * rows : (i + 1) * rows] for i in range(4))
    far_sum = (far.astype(F32) + swap(far_core, "tensor", 1).astype(F32)).astype(BF16)
    from_far = swap(far_sum, "tensor", 2)
    from_core = swap(other_core, "tensor", 1)
    return own.astype(F32) + from_core.astype(F32) + from_far.astype(F32)


class Ring:
    def __init__(self):
        self.size = lax.axis_size("dp")
        half = self.size // 2
        order = [2 * i for i in range(half)] + [2 * (self.size - 1 - i) + 1 for i in range(half, self.size)]
        self.up = [(order[i], order[(i + 1) % self.size]) for i in range(self.size)]
        self.down = [(b, a) for a, b in self.up]
        index = lax.axis_index("dp")
        row, column = index // 2, index % 2
        self.place = jnp.where(column == 0, row, self.size - 1 - row)
        self.small = self.size <= 16 and self.size % 2 == 0

    def owner(self, distance):
        place = (self.place + distance + 2 * self.size) % self.size
        return jnp.where(place < self.size // 2, 2 * place, 2 * (self.size - 1 - place) + 1)

    def step(self, going_up, going_down):
        going_up = lax.ppermute(going_up, "dp", self.up)
        going_down = lax.ppermute(going_down, "dp", self.down)
        return going_up, going_down

    def gather(self, block, splits):
        if not self.small:
            whole = lax.all_gather(block.reshape(1, *block.shape), "dp", axis=0, tiled=True)
            parts, start = [], 0
            for rows in splits:
                part = whole[:, start : start + rows]
                parts.append(part.reshape(self.size * rows, block.shape[1]))
                start += rows
            return parts
        total = block.shape[0]
        wholes = [jnp.zeros((self.size * rows, block.shape[1]), block.dtype) for rows in splits]

        def put(part, first, distance):
            start = 0
            for i, rows in enumerate(splits):
                low, high = max(start, first), min(start + rows, first + part.shape[0])
                if low < high:
                    wholes[i] = lax.dynamic_update_slice_in_dim(
                        wholes[i],
                        part[low - first : high - first],
                        self.owner(distance) * rows + (low - start),
                        0,
                    )
                start += rows

        put(block, 0, 0)
        going_up = going_down = block
        middle = self.size // 2
        for step in range(1, middle):
            going_up, going_down = self.step(going_up, going_down)
            put(going_up, 0, -step)
            put(going_down, 0, step)
        cut = total // 2
        first, second = self.step(going_up[:cut], going_down[cut:])
        put(first, 0, middle)
        put(second, cut, middle)
        return wholes

    def scatter(self, layout, shapes, vectors=()):
        if not self.small:
            owned = []
            for row in layout:
                for left, right in row:
                    whole = matmul_tn(left, right).astype(BF16)
                    owned.append(lax.psum_scatter(whole, "dp", scatter_dimension=0, tiled=True).astype(F32))
            outs = []
            for term, start, stop, turned in shapes:
                piece = owned[term][:, start:stop]
                outs.append(piece.T if turned else piece)
            if vectors:
                partial, other, *singles = vectors
                rows = [(partial + other)[i : i + 1] for i in range(partial.shape[0])] + singles
                outs.extend(lax.psum(rows, "dp"))
            return outs
        middle = self.size // 2
        arrived = list(ring_sum(layout, [self.owner(middle)] * 2, (), FIRST, (), vectors))
        for step in range(1, middle + 1):
            arrived[:2] = self.step(arrived[0], arrived[1])
            distance = middle - step
            stage = STEP if distance else LAST
            arrived = list(
                ring_sum(layout, [self.owner(distance), self.owner(-distance)], arrived, stage, shapes, vectors)
            )
        return arrived


FIRST, STEP, LAST = range(3)
VECTOR_ROWS = 8


def split_low(value):
    high = value.astype(BF16)
    return high, (value - high.astype(F32)).astype(BF16)


def ring_sum_kernel(places, stage, shapes, has_vectors, owners_ref, *refs):
    count = len(places)
    lefts, rights, rest = refs[:count], refs[count : 2 * count], refs[2 * count :]
    rows = places[0][2]
    total = max(place[0] for place in places) + rows
    half = total // 2
    extra = 2 * VECTOR_ROWS if has_vectors else 0

    def term(i, direction):
        start = pl.multiple_of(owners_ref[direction] * rows, rows)
        return matmul_tn(lefts[i][:, pl.ds(start, rows)], rights[i][...])

    def vectors_in(ref):
        first = ref.shape[0] - extra
        high = ref[first : first + VECTOR_ROWS].astype(F32)
        return high + ref[first + VECTOR_ROWS : first + extra].astype(F32)

    if has_vectors and stage == FIRST:
        partial_ref, other_ref, *single_refs = rest[:5]
        rest = rest[5:]
        sum_ref = rest[2]
        row, column = partial_ref.shape[0], 0
        sum_ref[...] = jnp.zeros_like(sum_ref)
        sum_ref[:row] = partial_ref[...] + other_ref[...]
        for ref in single_refs:
            width = ref.shape[1]
            if column + width > sum_ref.shape[1]:
                row, column = row + 1, 0
            sum_ref[row : row + 1, column : column + width] = ref[...]
            column += width
        high, low = split_low(sum_ref[...])
        for target in rest[:2]:
            first = target.shape[0] - extra
            target[first : first + VECTOR_ROWS] = high
            target[first + VECTOR_ROWS : first + extra] = low
    elif has_vectors and stage == STEP:
        rest[5][...] = rest[2][...] + vectors_in(rest[0]) + vectors_in(rest[1])
        for arrived, target in zip(rest[:2], rest[3:5]):
            target[target.shape[0] - extra :] = arrived[arrived.shape[0] - extra :]
        rest = (rest[0], rest[1], rest[3], rest[4])
    elif has_vectors:
        sums = rest[2][...] + vectors_in(rest[0])
        rest = rest[:2] + rest[3:]
        for target, (row, column) in zip(rest[2 + len(shapes) :], vector_places(rest[2 + len(shapes) :])):
            target[...] = sums[row : row + 1, column : column + target.shape[1]]

    for i, (row, column, _, width) in enumerate(places):
        columns = slice(column, column + width)
        if stage == FIRST:
            value = term(i, 0).astype(BF16)
            if row < half:
                rest[0][row : min(row + rows, half), columns] = value[: half - row]
            if row + rows > half:
                first = max(row, half)
                rest[1][first - half : row + rows - half, columns] = value[first - row :]
        elif stage == STEP:
            whole = rest[0].shape[0] == total + extra
            for direction, (low, high) in enumerate(((0, half), (half, total))):
                if whole:
                    low, high = 0, total
                value, arrived, target = term(i, direction), rest[direction], rest[2 + direction]
                first, last = max(row, low), min(row + rows, high)
                if first < last:
                    added = value[first - row : last - row] + arrived[first - low : last - low, columns].astype(F32)
                    target[first:last, columns] = added.astype(BF16)
                for begin, end in ((row, min(low, row + rows)), (max(high, row), row + rows)):
                    if begin < end:
                        target[begin:end, columns] = value[begin - row : end - row].astype(BF16)
        else:
            value = term(i, 0) + rest[0][row : row + rows, columns].astype(F32)
            value = value + rest[1][row : row + rows, columns].astype(F32)
            for target, (source, start, stop, turned) in zip(rest[2 : 2 + len(shapes)], shapes):
                if source == i:
                    target[...] = value[:, start:stop].T if turned else value[:, start:stop]


def vector_places(arrays):
    places, row, column, full = [], 0, 0, arrays[0].shape[1]
    for array in arrays:
        if column + array.shape[1] > full:
            row, column = row + 1, 0
        places.append((row, column))
        column += array.shape[1]
    return places


def ring_sum(layout, owners, arrived, stage, shapes, vectors):
    size = lax.axis_size("dp")
    places, lefts, rights, row = [], [], [], 0
    for terms in layout:
        column = 0
        for left, right in terms:
            rows = left.shape[1] // size
            places.append((row, column, rows, right.shape[1]))
            lefts.append(left)
            rights.append(right)
            column += right.shape[1]
        row += rows
    extra = 2 * VECTOR_ROWS if vectors else 0
    operands = [*lefts, *rights, *arrived]
    out_shape = []
    if stage == LAST:
        for term, start, stop, turned in shapes:
            shape = (places[term][2], stop - start)
            out_shape.append(jax.ShapeDtypeStruct(shape[::-1] if turned else shape, F32))
        if vectors:
            out_shape += [jax.ShapeDtypeStruct((1, column), F32)] * vectors[0].shape[0]
            out_shape += [jax.ShapeDtypeStruct(single.shape, F32) for single in vectors[2:]]
    else:
        travels = (row // 2 if stage == FIRST else row) + extra
        out_shape = [jax.ShapeDtypeStruct((travels, column), BF16)] * 2
        if vectors:
            out_shape.append(jax.ShapeDtypeStruct((VECTOR_ROWS, column), F32))
        if stage == FIRST:
            operands += vectors
    vmem = pl.BlockSpec(memory_space=pltpu.VMEM)
    return pl.pallas_call(
        functools.partial(ring_sum_kernel, places, stage, shapes, bool(vectors)),
        in_specs=[pl.BlockSpec(memory_space=pltpu.SMEM)] + [vmem] * len(operands),
        out_specs=[vmem] * len(out_shape),
        out_shape=out_shape,
        cost_estimate=pl.CostEstimate(
            flops=4 * row * column * lefts[0].shape[0],
            bytes_accessed=12 * row * column,
            transcendentals=0,
        ),
        compiler_params=pltpu.CompilerParams(vmem_limit_bytes=KERNEL_VMEM),
        name="ring_sum",
    )(jnp.stack(owners), *operands)


def row_major(array):
    return with_layout_constraint(array, Layout(major_to_minor=(0, 1)))


LANES = 128
QUERY_TILE = 256


def head_lanes(shape, head):
    lane = lax.broadcasted_iota(jnp.int32, shape, 1)
    return (lane >= head * HD) & (lane < (head + 1) * HD)


def keep_head(block, head):
    return jnp.where(head_lanes(block.shape, head), block, jnp.zeros_like(block))


def scores_of(key_block, query_block, counts_ref, score_scale):
    scores = matmul_nt(key_block, query_block) * score_scale
    rows = scores.shape[0] // counts_ref.shape[0]
    valid = [
        lax.broadcasted_iota(jnp.int32, (rows, scores.shape[1]), 0) < counts_ref[r]
        for r in range(counts_ref.shape[0])
    ]
    return jnp.where(jnp.concatenate(valid, axis=0), scores, MASKED)


def attention_kernel(score_scale, counts_ref, query_ref, key_ref, value_ref, context_ref, log_total_ref):
    keys, values = key_ref[...], value_ref[...]
    pieces = []
    for head in range(LANES // HD):
        scores = scores_of(keys, keep_head(query_ref[...], head), counts_ref, score_scale)
        row_peak = jnp.max(scores, axis=0, keepdims=True)
        raised = jnp.exp(scores - row_peak)
        total = jnp.sum(raised, axis=0, keepdims=True)
        log_total_ref[0, head : head + 1, :] = row_peak + jnp.log(total)
        probs_low = (raised * (1.0 / total)).astype(BF16)
        both = matmul_tn(values, probs_low)
        pieces.append(both[head * HD : (head + 1) * HD])
    context_ref[...] = jnp.concatenate(pieces, axis=0).T.astype(BF16)


def attention(qkv_low, counts, local_width, score_scale):
    seq_len = qkv_low.shape[0]
    pairs = local_width // LANES
    tiles = seq_len // QUERY_TILE
    return pl.pallas_call(
        functools.partial(attention_kernel, score_scale),
        grid=(pairs, tiles),
        in_specs=[
            pl.BlockSpec(memory_space=pltpu.SMEM),
            pl.BlockSpec((QUERY_TILE, LANES), lambda j, i: (i, j)),
            pl.BlockSpec((seq_len, LANES), lambda j, i: (0, pairs + j)),
            pl.BlockSpec((seq_len, LANES), lambda j, i: (0, 2 * pairs + j)),
        ],
        out_specs=[
            pl.BlockSpec((QUERY_TILE, LANES), lambda j, i: (i, j)),
            pl.BlockSpec((1, LANES // HD, QUERY_TILE), lambda j, i: (j, 0, i)),
        ],
        out_shape=[
            jax.ShapeDtypeStruct((seq_len, local_width), BF16),
            jax.ShapeDtypeStruct((pairs, LANES // HD, seq_len), F32),
        ],
        cost_estimate=pl.CostEstimate(
            flops=4 * seq_len * seq_len * local_width,
            bytes_accessed=8 * seq_len * local_width,
            transcendentals=seq_len * seq_len * local_width // HD,
        ),
        compiler_params=pltpu.CompilerParams(vmem_limit_bytes=KERNEL_VMEM),
        name="attention",
    )(counts, qkv_low, qkv_low, qkv_low)


def attention_grad_kernel(
    score_scale,
    counts_ref,
    query_ref,
    key_ref,
    value_ref,
    upstream_ref,
    log_total_ref,
    low_ref,
    query_sum_ref,
    value_sum_ref,
    key_total,
    value_total,
):
    pair, step = pl.program_id(0), pl.program_id(1)
    width = low_ref.shape[1] // 3

    @pl.when(step == 0)
    def _():
        key_total[...] = jnp.zeros_like(key_total)
        value_total[...] = jnp.zeros_like(value_total)
        query_sum_ref[...] = jnp.zeros_like(query_sum_ref)

    keys, values = key_ref[...], value_ref[...]
    pieces = []
    for head in range(LANES // HD):
        queries = keep_head(query_ref[...], head)
        upstream = keep_head(upstream_ref[...], head)
        scores = scores_of(keys, queries, counts_ref, score_scale)
        probs = jnp.exp(scores - log_total_ref[0, head : head + 1, :])
        prob_grad = matmul_nt(values, upstream)
        row_inner = jnp.sum(probs * prob_grad, axis=0, keepdims=True)
        score_grad = (probs * (prob_grad - row_inner) * score_scale).astype(BF16)
        value_total[...] += matmul(probs.astype(BF16), upstream)
        key_total[...] += matmul(score_grad, queries)
        both = matmul_tn(keys, score_grad)
        pieces.append(both[head * HD : (head + 1) * HD])
    query_grad = jnp.concatenate(pieces, axis=0).T
    rows = pl.ds(pl.multiple_of(step * QUERY_TILE, QUERY_TILE), QUERY_TILE)
    start = pl.multiple_of(pair * LANES, LANES)
    low_ref[rows, pl.ds(start, LANES)] = query_grad.astype(BF16)
    query_sum_ref[...] += jnp.sum(query_grad, axis=0, keepdims=True)

    @pl.when(step == pl.num_programs(1) - 1)
    def _():
        low_ref[:, pl.ds(start + width, LANES)] = key_total[...].astype(BF16)
        low_ref[:, pl.ds(start + 2 * width, LANES)] = value_total[...].astype(BF16)
        value_sum_ref[...] = jnp.sum(value_total[...], axis=0, keepdims=True)


def attention_grad(qkv_low, upstream, log_total, counts, local_width, score_scale):
    seq_len = qkv_low.shape[0]
    pairs = local_width // LANES
    tiles = seq_len // QUERY_TILE
    tile_spec = pl.BlockSpec((QUERY_TILE, LANES), lambda j, i: (i, j))
    sum_spec = pl.BlockSpec((1, LANES), lambda j, i: (0, j))
    sums = jax.ShapeDtypeStruct((1, local_width), F32)
    return pl.pallas_call(
        functools.partial(attention_grad_kernel, score_scale),
        grid=(pairs, tiles),
        in_specs=[
            pl.BlockSpec(memory_space=pltpu.SMEM),
            tile_spec,
            pl.BlockSpec((seq_len, LANES), lambda j, i: (0, pairs + j)),
            pl.BlockSpec((seq_len, LANES), lambda j, i: (0, 2 * pairs + j)),
            tile_spec,
            pl.BlockSpec((1, LANES // HD, QUERY_TILE), lambda j, i: (j, 0, i)),
        ],
        out_specs=[pl.BlockSpec((seq_len, 3 * local_width), lambda j, i: (0, 0)), sum_spec, sum_spec],
        out_shape=[jax.ShapeDtypeStruct((seq_len, 3 * local_width), BF16), sums, sums],
        scratch_shapes=[pltpu.VMEM((seq_len, LANES), F32), pltpu.VMEM((seq_len, LANES), F32)],
        cost_estimate=pl.CostEstimate(
            flops=10 * seq_len * seq_len * local_width,
            bytes_accessed=16 * seq_len * local_width,
            transcendentals=seq_len * seq_len * local_width // HD,
        ),
        compiler_params=pltpu.CompilerParams(vmem_limit_bytes=KERNEL_VMEM),
        name="attention_grad",
    )(counts, qkv_low, qkv_low, qkv_low, upstream, log_total)


def layer(
    hidden_in,
    cotangent,
    lengths,
    query_weight,
    key_weight,
    value_weight,
    output_weight,
    up_weight,
    down_weight,
    query_bias,
    value_bias,
    output_bias,
    up_bias,
    down_bias,
    first_gain,
    first_shift,
    second_gain,
    second_shift,
):
    n_tensor = lax.axis_size("tensor")
    tensor_index = lax.axis_index("tensor")
    local_rows = hidden_in.shape[0]
    local_width = query_weight.shape[1]
    score_scale = HD ** (-0.5)
    ring = Ring()
    blocks = jnp.arange(n_tensor, dtype=jnp.int32) ^ tensor_index
    counts = lengths[0] - blocks * local_rows

    packed = row_major(jnp.concatenate([query_weight, key_weight, value_weight, output_weight.T], axis=1))
    (packed_full,) = ring.gather(packed, (packed.shape[0],))
    hidden_full = gather_rows(hidden_in)
    stacked = row_major(jnp.concatenate([up_weight, down_weight.T], axis=0))
    up_full, down_turned = ring.gather(stacked, (up_weight.shape[0], down_weight.shape[1]))
    qkv_full = packed_full[:, : 3 * local_width]
    output_turned = packed_full[:, 3 * local_width :]

    qkv_bias = jnp.concatenate([query_bias, jnp.zeros_like(query_bias), value_bias])
    qkv_low = (matmul(hidden_full, qkv_full) + qkv_bias).astype(BF16)
    context, log_total = attention(qkv_low, counts, local_width, score_scale)
    attn_rows = scatter_rows(matmul_nt(context, output_turned).astype(BF16))
    first_sum = hidden_in.astype(F32) + attn_rows + output_bias
    first_out, first_normed, first_inverse = norm_forward(first_sum, first_gain, first_shift)
    normed_full = gather_rows(first_out.astype(BF16))
    pre_act = matmul(normed_full, up_full) + up_bias
    activated, slope = lax.optimization_barrier((gelu_value(pre_act).astype(BF16), gelu_slope(pre_act)))
    mlp_rows = scatter_rows(matmul_nt(activated, down_turned).astype(BF16))
    second_sum = first_out + mlp_rows + down_bias
    second_out, second_normed, second_inverse = norm_forward(second_sum, second_gain, second_shift)
    hidden_out = second_out.astype(BF16)

    upstream = cotangent.astype(F32)
    grad_second_gain = jnp.sum(upstream * second_normed, axis=0)
    grad_second_shift = jnp.sum(upstream, axis=0)
    second_grad = norm_backward(upstream, second_gain, second_normed, second_inverse)
    grad_down_bias = jnp.sum(second_grad, axis=0)
    second_full = gather_rows(second_grad.astype(BF16))
    pre_grad = matmul(second_full, down_turned) * slope
    grad_up_bias, pre_low = lax.optimization_barrier((jnp.sum(pre_grad, axis=0), pre_grad.astype(BF16)))
    partial = matmul_nt(pre_low, up_full).astype(BF16)
    up_owned, down_owned = ring.scatter(
        [[(normed_full, pre_low)], [(second_full, activated)]],
        ((0, 0, up_weight.shape[1], False), (1, 0, down_weight.shape[0], True)),
    )
    first_grad_in = second_grad + scatter_rows(partial)
    grad_first_gain = jnp.sum(first_grad_in * first_normed, axis=0)
    grad_first_shift = jnp.sum(first_grad_in, axis=0)
    first_grad = norm_backward(first_grad_in, first_gain, first_normed, first_inverse)
    grad_output_bias = jnp.sum(first_grad, axis=0)
    attn_grad_full = lax.optimization_barrier(gather_rows(first_grad.astype(BF16)))
    context_grad = matmul(attn_grad_full, output_turned).astype(BF16)

    everywhere = jnp.stack(
        [grad_second_gain, grad_second_shift, grad_down_bias, grad_first_gain, grad_first_shift, grad_output_bias]
    )
    everywhere = everywhere + swap(everywhere, "tensor", 1)
    everywhere_far = swap(everywhere, "tensor", 2)

    low, query_sum, value_sum = attention_grad(
        qkv_low, context_grad, log_total, counts, local_width, score_scale
    )
    query_owned, key_owned, value_owned, output_owned, *sums = ring.scatter(
        [[(hidden_full, low), (attn_grad_full, context)]],
        tuple((0, i * local_width, (i + 1) * local_width, False) for i in range(3)) + ((1, 0, local_width, True),),
        (everywhere, everywhere_far, grad_up_bias.reshape(1, -1), query_sum, value_sum),
    )
    sums = [vector.reshape(-1) for vector in sums]
    back = matmul_nt(low, qkv_full).astype(BF16)
    back = scatter_rows(back)
    grad_in = (first_grad + back).astype(BF16)
    return (
        hidden_out,
        grad_in,
        query_owned,
        key_owned,
        value_owned,
        output_owned,
        up_owned,
        down_owned,
        sums[7],
        sums[8],
        sums[5],
        sums[6],
        sums[2],
        sums[3],
        sums[4],
        sums[0],
        sums[1],
    )


def solution(mesh):
    in_specs = (
        P(("dp", "tensor"), None),
        P(("dp", "tensor"), None),
        P("dp"),
        P("dp", "tensor"),
        P("dp", "tensor"),
        P("dp", "tensor"),
        P("tensor", "dp"),
        P("dp", "tensor"),
        P("tensor", "dp"),
        P("tensor"),
        P("tensor"),
        P(),
        P("tensor"),
        P(),
        P(),
        P(),
        P(),
        P(),
    )
    out_specs = (
        P(("dp", "tensor"), None),
        P(("dp", "tensor"), None),
        P("dp", "tensor"),
        P("dp", "tensor"),
        P("dp", "tensor"),
        P("tensor", "dp"),
        P("dp", "tensor"),
        P("tensor", "dp"),
        P("tensor"),
        P("tensor"),
        P(),
        P("tensor"),
        P(),
        P(),
        P(),
        P(),
        P(),
    )
    return jax.shard_map(layer, mesh=mesh, in_specs=in_specs, out_specs=out_specs, check_vma=False)
```

profile of v0, /device:TPU:0, one launch (start us, length us, event | category | flops | bytes accessed | tf_op | source)
XLA Modules:
  0.0 206.2 jit_solution(12280514074937439465)
XLA Ops:
  1.3 2.6 %collective-permute-start.1 = (bf16[128,1024]{1,0:T(8,128)(2,1)}, bf16[128,1024]{1,0:T(8,128)(2,1)}, u32[]{:S(2)}, u32[]{:S(2)}) collective-permute-start(bf16[128,1024]{1,0:T(8,128)(2,1)} %param.18), channel_id=1, source_target_pairs={{0,2},{1,3},{2,0},{3,1},{4,6},{5,7},{6,4},{7,5},{8,10},{9,11},{10,... | collective-permute-start | bytes 786440 | tf_op jit(solution)/shard_map/ppermute | solution.py:65
  21.4 6.8 %collective-permute-done.18 = bf16[256,1024]{1,0:T(8,128)(2,1)} collective-permute-done((bf16[256,1024]{1,0:T(8,128)(2,1)}, bf16[256,1024]{1,0:T(8,128)(2,1)}, u32[]{:S(2)}, u32[]{:S(2)}) %collective-permute-start.18) | collective-permute-done | bytes 524320 | tf_op jit(solution)/shard_map/ppermute | solution.py:102
  30.2 4.5 %collective-permute-done.5 = bf16[128,1024]{1,0:T(8,128)(2,1)S(1)} collective-permute-done((bf16[128,1024]{1,0:T(8,128)(2,1)}, bf16[128,1024]{1,0:T(8,128)(2,1)S(1)}, u32[]{:S(2)}, u32[]{:S(2)}) %collective-permute-start.5) | collective-permute-done | bytes 262176 | tf_op jit(solution)/shard_map/ppermute | solution.py:101
  36.8 13.1 %collective-permute-done.7 = bf16[128,1024]{1,0:T(8,128)(2,1)S(1)} collective-permute-done((bf16[128,1024]{1,0:T(8,128)(2,1)S(1)}, bf16[128,1024]{1,0:T(8,128)(2,1)S(1)}, u32[]{:S(2)}, u32[]{:S(2)}) %collective-permute-start.7) | collective-permute-done | bytes 262176 | tf_op jit(solution)/shard_map/ppermute | solution.py:101
  52.1 2.8 %collective-permute-done.9 = bf16[64,1024]{1,0:T(8,128)(2,1)S(1)} collective-permute-done((bf16[64,1024]{1,0:T(8,128)(2,1)S(1)}, bf16[64,1024]{1,0:T(8,128)(2,1)S(1)}, u32[]{:S(2)}, u32[]{:S(2)}) %collective-permute-start.9) | collective-permute-done | bytes 131104 | tf_op jit(solution)/shard_map/ppermute | solution.py:101
  56.6 5.7 %attention.1 = (bf16[512,256]{1,0:T(8,128)(2,1)S(1)}, f32[2,2,512]{2,1,0:T(2,128)S(1)}) custom-call(s32[4]{0:T(128)S(1)} %multiply_subtract_fusion.counts_ref, bf16[512,768]{1,0:T(8,128)(2,1)S(1)} %add_convert_fusion.query_ref.key_ref.value_ref, bf16[512,768]{1,0:T(8,128)(2,1)S(1)} %add_convert_fusion.query_ref.key_ref.value_ref, ...), custom_call_target="tpu_custom_call" | custom-call | flops 268435456 | bytes 1048576 | tf_op jit(solution)/shard_map/attention/pallas_call | solution.py:357
  68.3 7.3 %collective-permute-done.13 = bf16[128,1024]{1,0:T(8,128)(2,1)S(1)} collective-permute-done((bf16[128,1024]{1,0:T(8,128)(2,1)S(1)}, bf16[128,1024]{1,0:T(8,128)(2,1)S(1)}, u32[]{:S(2)}, u32[]{:S(2)}) %collective-permute-start.13) | collective-permute-done | bytes 262176 | tf_op jit(solution)/shard_map/ppermute | solution.py:65
  76.7 4.1 %collective-permute-done.21 = bf16[256,1024]{1,0:T(8,128)(2,1)S(1)} collective-permute-done((bf16[256,1024]{1,0:T(8,128)(2,1)S(1)}, bf16[256,1024]{1,0:T(8,128)(2,1)S(1)}, u32[]{:S(2)}, u32[]{:S(2)}) %collective-permute-start.21) | collective-permute-done | bytes 524320 | tf_op jit(solution)/shard_map/ppermute | solution.py:101
  81.0 1.6 collective-permute-start.24
  83.6 4.6 %collective-permute-done.24 = bf16[128,1024]{1,0:T(8,128)(2,1)S(1)} collective-permute-done((bf16[128,1024]{1,0:T(8,128)(2,1)S(1)}, bf16[128,1024]{1,0:T(8,128)(2,1)S(1)}, u32[]{:S(2)}, u32[]{:S(2)}) %collective-permute-start.24) | collective-permute-done | bytes 262176 | tf_op jit(solution)/shard_map/ppermute | solution.py:102
  89.5 2.0 fusion.3
  95.2 7.8 %collective-permute-done.27 = bf16[128,1024]{1,0:T(8,128)(2,1)S(1)} collective-permute-done((bf16[128,1024]{1,0:T(8,128)(2,1)S(1)}, bf16[128,1024]{1,0:T(8,128)(2,1)S(1)}, u32[]{:S(2)}, u32[]{:S(2)}) %collective-permute-start.27) | collective-permute-done | bytes 262176 | tf_op jit(solution)/shard_map/ppermute | solution.py:65
  105.5 7.0 %collective-permute-done.29 = bf16[128,1024]{1,0:T(8,128)(2,1)S(1)} collective-permute-done((bf16[128,1024]{1,0:T(8,128)(2,1)S(1)}, bf16[128,1024]{1,0:T(8,128)(2,1)S(1)}, u32[]{:S(2)}, u32[]{:S(2)}) %collective-permute-start.29) | collective-permute-done | bytes 262176 | tf_op jit(solution)/shard_map/ppermute | solution.py:65
  119.0 1.6 collective-permute-start.51
  121.3 5.6 %collective-permute-done.50.refs_4_ = bf16[128,1024]{1,0:T(8,128)(2,1)S(1)} collective-permute-done((bf16[128,1024]{1,0:T(8,128)(2,1)S(1)}, bf16[128,1024]{1,0:T(8,128)(2,1)S(1)}, u32[]{:S(2)}, u32[]{:S(2)}) %collective-permute-start.50) | collective-permute-done | bytes 262176 | tf_op jit(solution)/shard_map/ppermute | solution.py:101
  127.1 2.2 %ring_sum.16 = (bf16[256,1024]{1,0:T(8,128)(2,1)}, bf16[256,1024]{1,0:T(8,128)(2,1)}) custom-call(s32[2]{0:T(128)S(1)} %pad_add_fusion.3.owners_ref, bf16[512,1024]{1,0:T(8,128)(2,1)S(1)} %pad_maximum_fusion.refs_0_, bf16[512,1024]{1,0:T(8,128)(2,1)S(1)} %pad_maximum_fusion.1.refs_1_, bf16[512,1024]{1,0:T(8,128)(2,1)S(1)} %get-tuple-element.64.refs_2_, ...), custom_call_target="tpu_custom_call" | custom-call | flops 536870912 | bytes 3145728 | tf_op jit(solution)/shard_map/ring_sum/pallas_call | solution.py:296
  134.0 6.6 %collective-permute-done.35 = bf16[128,1024]{1,0:T(8,128)(2,1)} collective-permute-done((bf16[128,1024]{1,0:T(8,128)(2,1)}, bf16[128,1024]{1,0:T(8,128)(2,1)}, u32[]{:S(2)}, u32[]{:S(2)}) %collective-permute-start.35) | collective-permute-done | bytes 262176 | tf_op jit(solution)/shard_map/ppermute | solution.py:65
  145.4 2.0 ring_sum.17
  151.3 6.2 %attention_grad.1 = (bf16[512,768]{1,0:T(8,128)(2,1)S(1)}, f32[1,256]{1,0:T(1,128)S(1)}, f32[1,256]{1,0:T(1,128)S(1)}) custom-call(s32[4]{0:T(128)S(1)} %multiply_subtract_fusion.counts_ref, bf16[512,768]{1,0:T(8,128)(2,1)S(1)} %copy-done.1, bf16[512,768]{1,0:T(8,128)(2,1)S(1)} %copy-done.1, bf16[512,768]{1,0:T(8,128)(2,1)S(1)} %copy-done.1, ...), custom_call_target="tpu_custom_call" | custom-call | flops 671088640 | bytes 2097152 | tf_op jit(solution)/shard_map/attention_grad/pallas_call | solution.py:441
  161.5 3.1 %collective-permute-done.42.refs_4_ = bf16[80,1024]{1,0:T(8,128)(2,1)S(1)} collective-permute-done((bf16[80,1024]{1,0:T(8,128)(2,1)S(1)}, bf16[80,1024]{1,0:T(8,128)(2,1)S(1)}, u32[]{:S(2)}, u32[]{:S(2)}) %collective-permute-start.42) | collective-permute-done | bytes 163872 | tf_op jit(solution)/shard_map/ppermute | solution.py:101
  166.2 1.7 collective-permute-start.44
  168.4 5.5 %collective-permute-done.44.refs_4_ = bf16[144,1024]{1,0:T(8,128)(2,1)S(1)} collective-permute-done((bf16[144,1024]{1,0:T(8,128)(2,1)S(1)}, bf16[144,1024]{1,0:T(8,128)(2,1)S(1)}, u32[]{:S(2)}, u32[]{:S(2)}) %collective-permute-start.44) | collective-permute-done | bytes 294944 | tf_op jit(solution)/shard_map/ppermute | solution.py:101
  175.7 1.6 collective-permute-start.46
  178.0 2.2 %collective-permute-start.39 = (bf16[128,1024]{1,0:T(8,128)(2,1)S(1)}, bf16[128,1024]{1,0:T(8,128)(2,1)S(1)}, u32[]{:S(2)}, u32[]{:S(2)}) collective-permute-start(bf16[128,1024]{1,0:T(8,128)(2,1)S(1)} %add_convert_fusion.2), channel_id=1, source_target_pairs={{0,2},{1,3},{2,0},{3,1},{4,6},{5,7},{6,4},{7,5},{8,10},{9,11},{10,... | collective-permute-start | bytes 786440 | tf_op jit(solution)/shard_map/ppermute | solution.py:65
  181.5 1.6 collective-permute-start.56
  184.0 3.3 %collective-permute-done.47.refs_5_ = bf16[144,1024]{1,0:T(8,128)(2,1)S(1)} collective-permute-done((bf16[144,1024]{1,0:T(8,128)(2,1)S(1)}, bf16[144,1024]{1,0:T(8,128)(2,1)S(1)}, u32[]{:S(2)}, u32[]{:S(2)}) %collective-permute-start.47) | collective-permute-done | bytes 294944 | tf_op jit(solution)/shard_map/ppermute | solution.py:102
  188.4 1.8 collective-permute-start.48
  191.3 5.1 %collective-permute-done.56.refs_4_ = bf16[256,1024]{1,0:T(8,128)(2,1)S(1)} collective-permute-done((bf16[256,1024]{1,0:T(8,128)(2,1)S(1)}, bf16[256,1024]{1,0:T(8,128)(2,1)S(1)}, u32[]{:S(2)}, u32[]{:S(2)}) %collective-permute-start.56) | collective-permute-done | bytes 524320 | tf_op jit(solution)/shard_map/ppermute | solution.py:101
  196.3 2.2 %collective-permute-done.57.refs_5_ = bf16[256,1024]{1,0:T(8,128)(2,1)S(1)} collective-permute-done((bf16[256,1024]{1,0:T(8,128)(2,1)S(1)}, bf16[256,1024]{1,0:T(8,128)(2,1)S(1)}, u32[]{:S(2)}, u32[]{:S(2)}) %collective-permute-start.57) | collective-permute-done | bytes 524320 | tf_op jit(solution)/shard_map/ppermute | solution.py:102
  198.5 2.0 ring_sum.19
  201.6 2.8 %collective-permute-done.49.refs_5_ = bf16[144,1024]{1,0:T(8,128)(2,1)S(1)} collective-permute-done((bf16[144,1024]{1,0:T(8,128)(2,1)S(1)}, bf16[144,1024]{1,0:T(8,128)(2,1)S(1)}, u32[]{:S(2)}, u32[]{:S(2)}) %collective-permute-start.49) | collective-permute-done | bytes 294944 | tf_op jit(solution)/shard_map/ppermute | solution.py:102
  204.4 1.7 ring_sum.14
  (239 shorter events, 75.1 us)
Async XLA Ops:
  0.7 13.3 %collective-permute-start = (bf16[128,1024]{1,0:T(8,128)(2,1)}, bf16[128,1024]{1,0:T(8,128)(2,1)}, u32[]{:S(2)}, u32[]{:S(2)}) collective-permute-start(bf16[128,1024]{1,0:T(8,128)(2,1)} %param.18), channel_id=1, source_target_pairs={{0,1},{1,0},{2,3},{3,2},{4,5},{5,4},{6,7},{7,6},{8,9},{9,8},{10,11... | collective-permute-start | bytes 786440 | tf_op jit(solution)/shard_map/ppermute | solution.py:65
  1.3 14.1 %collective-permute-start.1 = (bf16[128,1024]{1,0:T(8,128)(2,1)}, bf16[128,1024]{1,0:T(8,128)(2,1)}, u32[]{:S(2)}, u32[]{:S(2)}) collective-permute-start(bf16[128,1024]{1,0:T(8,128)(2,1)} %param.18), channel_id=1, source_target_pairs={{0,2},{1,3},{2,0},{3,1},{4,6},{5,7},{6,4},{7,5},{8,10},{9,11},{10,... | collective-permute-start | bytes 786440 | tf_op jit(solution)/shard_map/ppermute | solution.py:65
  5.9 9.5 %collective-permute-start.3 = (bf16[128,1024]{1,0:T(8,128)(2,1)}, bf16[128,1024]{1,0:T(8,128)(2,1)}, u32[]{:S(2)}, u32[]{:S(2)}) collective-permute-start(bf16[128,1024]{1,0:T(8,128)(2,1)} %get-tuple-element.149), channel_id=1, source_target_pairs={{0,8},{8,16},{16,24},{24,28},{28,20},{20,12},{12,4},{4,0},{1,9},{9... | collective-permute-start | bytes 786440 | tf_op jit(solution)/shard_map/ppermute | solution.py:101
  7.4 9.5 %collective-permute-start.4 = (bf16[128,1024]{1,0:T(8,128)(2,1)}, bf16[128,1024]{1,0:T(8,128)(2,1)}, u32[]{:S(2)}, u32[]{:S(2)}) collective-permute-start(bf16[128,1024]{1,0:T(8,128)(2,1)} %get-tuple-element.149), channel_id=1, source_target_pairs={{8,0},{16,8},{24,16},{28,24},{20,28},{12,20},{4,12},{0,4},{9,1},{1... | collective-permute-start | bytes 786440 | tf_op jit(solution)/shard_map/ppermute | solution.py:102
  8.9 19.3 %collective-permute-start.18 = (bf16[256,1024]{1,0:T(8,128)(2,1)}, bf16[256,1024]{1,0:T(8,128)(2,1)}, u32[]{:S(2)}, u32[]{:S(2)}) collective-permute-start(bf16[256,1024]{1,0:T(8,128)(2,1)} %pad_maximum_fusion.3), channel_id=1, source_target_pairs={{8,0},{16,8},{24,16},{28,24},{20,28},{12,20},{4,12},{0,4},{9,1},{1... | collective-permute-start | bytes 1572872 | tf_op jit(solution)/shard_map/ppermute | solution.py:102
  14.0 15.2 %collective-permute-start.17 = (bf16[256,1024]{1,0:T(8,128)(2,1)}, bf16[256,1024]{1,0:T(8,128)(2,1)}, u32[]{:S(2)}, u32[]{:S(2)}) collective-permute-start(bf16[256,1024]{1,0:T(8,128)(2,1)} %pad_maximum_fusion.3), channel_id=1, source_target_pairs={{0,8},{8,16},{16,24},{24,28},{28,20},{20,12},{12,4},{4,0},{1,9},{9... | collective-permute-start | bytes 1572872 | tf_op jit(solution)/shard_map/ppermute | solution.py:101
  15.4 21.4 %collective-permute-start.2 = (bf16[128,1024]{1,0:T(8,128)(2,1)}, bf16[128,1024]{1,0:T(8,128)(2,1)S(1)}, u32[]{:S(2)}, u32[]{:S(2)}) collective-permute-start(bf16[128,1024]{1,0:T(8,128)(2,1)} %collective-permute-done.1), channel_id=1, source_target_pairs={{0,1},{1,0},{2,3},{3,2},{4,5},{5,4},{6,7},{7,6},{8,9},{9,8},{10,11... | collective-permute-start | bytes 786440 | tf_op jit(solution)/shard_map/ppermute | solution.py:65
  15.4 19.3 %collective-permute-start.5 = (bf16[128,1024]{1,0:T(8,128)(2,1)}, bf16[128,1024]{1,0:T(8,128)(2,1)S(1)}, u32[]{:S(2)}, u32[]{:S(2)}) collective-permute-start(bf16[128,1024]{1,0:T(8,128)(2,1)} %collective-permute-done.3), channel_id=1, source_target_pairs={{0,8},{8,16},{16,24},{24,28},{28,20},{20,12},{12,4},{4,0},{1,9},{9... | collective-permute-start | bytes 786440 | tf_op jit(solution)/shard_map/ppermute | solution.py:101
  16.9 18.3 %collective-permute-start.6 = (bf16[128,1024]{1,0:T(8,128)(2,1)}, bf16[128,1024]{1,0:T(8,128)(2,1)S(1)}, u32[]{:S(2)}, u32[]{:S(2)}) collective-permute-start(bf16[128,1024]{1,0:T(8,128)(2,1)} %collective-permute-done.4), channel_id=1, source_target_pairs={{8,0},{16,8},{24,16},{28,24},{20,28},{12,20},{4,12},{0,4},{9,1},{1... | collective-permute-start | bytes 786440 | tf_op jit(solution)/shard_map/ppermute | solution.py:102
  28.2 37.5 %collective-permute-start.20 = (bf16[256,1024]{1,0:T(8,128)(2,1)}, bf16[256,1024]{1,0:T(8,128)(2,1)S(1)}, u32[]{:S(2)}, u32[]{:S(2)}) collective-permute-start(bf16[256,1024]{1,0:T(8,128)(2,1)} %collective-permute-done.18), channel_id=1, source_target_pairs={{8,0},{16,8},{24,16},{28,24},{20,28},{12,20},{4,12},{0,4},{9,1},{1... | collective-permute-start | bytes 1572872 | tf_op jit(solution)/shard_map/ppermute | solution.py:102
  29.2 38.0 %collective-permute-start.19 = (bf16[256,1024]{1,0:T(8,128)(2,1)}, bf16[256,1024]{1,0:T(8,128)(2,1)S(1)}, u32[]{:S(2)}, u32[]{:S(2)}) collective-permute-start(bf16[256,1024]{1,0:T(8,128)(2,1)} %collective-permute-done.17), channel_id=1, source_target_pairs={{0,8},{8,16},{16,24},{24,28},{28,20},{20,12},{12,4},{4,0},{1,9},{9... | collective-permute-start | bytes 1572872 | tf_op jit(solution)/shard_map/ppermute | solution.py:101
  34.7 15.2 %collective-permute-start.7 = (bf16[128,1024]{1,0:T(8,128)(2,1)S(1)}, bf16[128,1024]{1,0:T(8,128)(2,1)S(1)}, u32[]{:S(2)}, u32[]{:S(2)}) collective-permute-start(bf16[128,1024]{1,0:T(8,128)(2,1)S(1)} %collective-permute-done.5), channel_id=1, source_target_pairs={{0,8},{8,16},{16,24},{24,28},{28,20},{20,12},{12,4},{4,0},{1,9},{9... | collective-permute-start | bytes 786440 | tf_op jit(solution)/shard_map/ppermute | solution.py:101
  35.2 15.3 %collective-permute-start.8 = (bf16[128,1024]{1,0:T(8,128)(2,1)S(1)}, bf16[128,1024]{1,0:T(8,128)(2,1)S(1)}, u32[]{:S(2)}, u32[]{:S(2)}) collective-permute-start(bf16[128,1024]{1,0:T(8,128)(2,1)S(1)} %collective-permute-done.6), channel_id=1, source_target_pairs={{8,0},{16,8},{24,16},{28,24},{20,28},{12,20},{4,12},{0,4},{9,1},{1... | collective-permute-start | bytes 786440 | tf_op jit(solution)/shard_map/ppermute | solution.py:102
  65.7 15.2 %collective-permute-start.22 = (bf16[256,1024]{1,0:T(8,128)(2,1)S(1)}, bf16[256,1024]{1,0:T(8,128)(2,1)S(1)}, u32[]{:S(2)}, u32[]{:S(2)}) collective-permute-start(bf16[256,1024]{1,0:T(8,128)(2,1)S(1)} %collective-permute-done.20), channel_id=1, source_target_pairs={{8,0},{16,8},{24,16},{28,24},{20,28},{12,20},{4,12},{0,4},{9,1},{1... | collective-permute-start | bytes 1572872 | tf_op jit(solution)/shard_map/ppermute | solution.py:102
  67.2 13.6 %collective-permute-start.21 = (bf16[256,1024]{1,0:T(8,128)(2,1)S(1)}, bf16[256,1024]{1,0:T(8,128)(2,1)S(1)}, u32[]{:S(2)}, u32[]{:S(2)}) collective-permute-start(bf16[256,1024]{1,0:T(8,128)(2,1)S(1)} %collective-permute-done.19), channel_id=1, source_target_pairs={{0,8},{8,16},{16,24},{24,28},{28,20},{20,12},{12,4},{4,0},{1,9},{9... | collective-permute-start | bytes 1572872 | tf_op jit(solution)/shard_map/ppermute | solution.py:101
  117.0 14.3 %collective-permute-start.31 = (bf16[128,1024]{1,0:T(8,128)(2,1)S(1)}, bf16[128,1024]{1,0:T(8,128)(2,1)S(1)}, u32[]{:S(2)}, u32[]{:S(2)}) collective-permute-start(bf16[128,1024]{1,0:T(8,128)(2,1)S(1)} %get-tuple-element.128), channel_id=1, source_target_pairs={{0,1},{1,0},{2,3},{3,2},{4,5},{5,4},{6,7},{7,6},{8,9},{9,8},{10,11... | collective-permute-start | bytes 786440 | tf_op jit(solution)/shard_map/ppermute | solution.py:65
  120.7 10.6 %collective-permute-start.33 = (bf16[128,1024]{1,0:T(8,128)(2,1)S(1)}, bf16[128,1024]{1,0:T(8,128)(2,1)S(1)}, u32[]{:S(2)}, u32[]{:S(2)}) collective-permute-start(bf16[128,1024]{1,0:T(8,128)(2,1)S(1)} %add_convert_fusion.3), channel_id=1, source_target_pairs={{0,2},{1,3},{2,0},{3,1},{4,6},{5,7},{6,4},{7,5},{8,10},{9,11},{10,... | collective-permute-start | bytes 786440 | tf_op jit(solution)/shard_map/ppermute | solution.py:65
  129.3 13.7 %collective-permute-start.52 = (bf16[256,1024]{1,0:T(8,128)(2,1)}, bf16[256,1024]{1,0:T(8,128)(2,1)}, u32[]{:S(2)}, u32[]{:S(2)}) collective-permute-start(bf16[256,1024]{1,0:T(8,128)(2,1)} %get-tuple-element.88), channel_id=1, source_target_pairs={{0,8},{8,16},{16,24},{24,28},{28,20},{20,12},{12,4},{4,0},{1,9},{9... | collective-permute-start | bytes 1572872 | tf_op jit(solution)/shard_map/ppermute | solution.py:101
  129.9 13.0 %collective-permute-start.53 = (bf16[256,1024]{1,0:T(8,128)(2,1)}, bf16[256,1024]{1,0:T(8,128)(2,1)}, u32[]{:S(2)}, u32[]{:S(2)}) collective-permute-start(bf16[256,1024]{1,0:T(8,128)(2,1)} %get-tuple-element.89), channel_id=1, source_target_pairs={{8,0},{16,8},{24,16},{28,24},{20,28},{12,20},{4,12},{0,4},{9,1},{1... | collective-permute-start | bytes 1572872 | tf_op jit(solution)/shard_map/ppermute | solution.py:102
  134.0 15.5 %collective-permute-start.34 = (bf16[128,1024]{1,0:T(8,128)(2,1)}, bf16[128,1024]{1,0:T(8,128)(2,1)}, u32[]{:S(2)}, u32[]{:S(2)}) collective-permute-start(bf16[128,1024]{1,0:T(8,128)(2,1)} %convert_element_type.146), channel_id=1, source_target_pairs={{0,1},{1,0},{2,3},{3,2},{4,5},{5,4},{6,7},{7,6},{8,9},{9,8},{10,11... | collective-permute-start | bytes 786440 | tf_op jit(solution)/shard_map/ppermute | solution.py:65
  140.5 9.0 %collective-permute-start.36 = (bf16[128,1024]{1,0:T(8,128)(2,1)}, bf16[128,1024]{1,0:T(8,128)(2,1)}, u32[]{:S(2)}, u32[]{:S(2)}) collective-permute-start(bf16[128,1024]{1,0:T(8,128)(2,1)} %collective-permute-done.35), channel_id=1, source_target_pairs={{0,1},{1,0},{2,3},{3,2},{4,5},{5,4},{6,7},{7,6},{8,9},{9,8},{10,11... | collective-permute-start | bytes 786440 | tf_op jit(solution)/shard_map/ppermute | solution.py:65
  142.4 15.1 %collective-permute-start.41 = (f32[6,1024]{1,0:T(8,128)S(1)}, f32[6,1024]{1,0:T(8,128)S(1)}, u32[]{:S(2)}, u32[]{:S(2)}) collective-permute-start(f32[6,1024]{1,0:T(8,128)S(1)} %add.469.refs_4_), channel_id=1, source_target_pairs={{0,2},{1,3},{2,0},{3,1},{4,6},{5,7},{6,4},{7,5},{8,10},{9,11},{10,... | collective-permute-start | bytes 73736 | tf_op jit(solution)/shard_map/ppermute | solution.py:65
  147.4 30.5 %collective-permute-start.54 = (bf16[256,1024]{1,0:T(8,128)(2,1)S(1)}, bf16[256,1024]{1,0:T(8,128)(2,1)S(1)}, u32[]{:S(2)}, u32[]{:S(2)}) collective-permute-start(bf16[256,1024]{1,0:T(8,128)(2,1)S(1)} %get-tuple-element.90), channel_id=1, source_target_pairs={{0,8},{8,16},{16,24},{24,28},{28,20},{20,12},{12,4},{4,0},{1,9},{9... | collective-permute-start | bytes 1572872 | tf_op jit(solution)/shard_map/ppermute | solution.py:101
  148.8 31.3 %collective-permute-start.55 = (bf16[256,1024]{1,0:T(8,128)(2,1)S(1)}, bf16[256,1024]{1,0:T(8,128)(2,1)S(1)}, u32[]{:S(2)}, u32[]{:S(2)}) collective-permute-start(bf16[256,1024]{1,0:T(8,128)(2,1)S(1)} %get-tuple-element.91), channel_id=1, source_target_pairs={{8,0},{16,8},{24,16},{28,24},{20,28},{12,20},{4,12},{0,4},{9,1},{1... | collective-permute-start | bytes 1572872 | tf_op jit(solution)/shard_map/ppermute | solution.py:102
  168.3 9.0 %collective-permute-start.38 = (bf16[128,1024]{1,0:T(8,128)(2,1)S(1)}, bf16[128,1024]{1,0:T(8,128)(2,1)S(1)}, u32[]{:S(2)}, u32[]{:S(2)}) collective-permute-start(bf16[128,1024]{1,0:T(8,128)(2,1)S(1)} %get-tuple-element.127), channel_id=1, source_target_pairs={{0,1},{1,0},{2,3},{3,2},{4,5},{5,4},{6,7},{7,6},{8,9},{9,8},{10,11... | collective-permute-start | bytes 786440 | tf_op jit(solution)/shard_map/ppermute | solution.py:65
  177.4 12.8 %collective-permute-start.37 = (bf16[128,1024]{1,0:T(8,128)(2,1)S(1)}, bf16[128,1024]{1,0:T(8,128)(2,1)S(1)}, u32[]{:S(2)}, u32[]{:S(2)}) collective-permute-start(bf16[128,1024]{1,0:T(8,128)(2,1)S(1)} %get-tuple-element.126), channel_id=1, source_target_pairs={{0,1},{1,0},{2,3},{3,2},{4,5},{5,4},{6,7},{7,6},{8,9},{9,8},{10,11... | collective-permute-start | bytes 786440 | tf_op jit(solution)/shard_map/ppermute | solution.py:65
  177.4 9.9 %collective-permute-start.47 = (bf16[144,1024]{1,0:T(8,128)(2,1)S(1)}, bf16[144,1024]{1,0:T(8,128)(2,1)S(1)}, u32[]{:S(2)}, u32[]{:S(2)}) collective-permute-start(bf16[144,1024]{1,0:T(8,128)(2,1)S(1)} %get-tuple-element.77), channel_id=1, source_target_pairs={{8,0},{16,8},{24,16},{28,24},{20,28},{12,20},{4,12},{0,4},{9,1},{1... | collective-permute-start | bytes 884744 | tf_op jit(solution)/shard_map/ppermute | solution.py:102
  178.0 12.5 %collective-permute-start.39 = (bf16[128,1024]{1,0:T(8,128)(2,1)S(1)}, bf16[128,1024]{1,0:T(8,128)(2,1)S(1)}, u32[]{:S(2)}, u32[]{:S(2)}) collective-permute-start(bf16[128,1024]{1,0:T(8,128)(2,1)S(1)} %add_convert_fusion.2), channel_id=1, source_target_pairs={{0,2},{1,3},{2,0},{3,1},{4,6},{5,7},{6,4},{7,5},{8,10},{9,11},{10,... | collective-permute-start | bytes 786440 | tf_op jit(solution)/shard_map/ppermute | solution.py:65
  181.5 14.9 %collective-permute-start.56 = (bf16[256,1024]{1,0:T(8,128)(2,1)S(1)}, bf16[256,1024]{1,0:T(8,128)(2,1)S(1)}, u32[]{:S(2)}, u32[]{:S(2)}) collective-permute-start(bf16[256,1024]{1,0:T(8,128)(2,1)S(1)} %get-tuple-element.92), channel_id=1, source_target_pairs={{0,8},{8,16},{16,24},{24,28},{28,20},{20,12},{12,4},{4,0},{1,9},{9... | collective-permute-start | bytes 1572872 | tf_op jit(solution)/shard_map/ppermute | solution.py:101
  183.1 15.4 %collective-permute-start.57 = (bf16[256,1024]{1,0:T(8,128)(2,1)S(1)}, bf16[256,1024]{1,0:T(8,128)(2,1)S(1)}, u32[]{:S(2)}, u32[]{:S(2)}) collective-permute-start(bf16[256,1024]{1,0:T(8,128)(2,1)S(1)} %get-tuple-element.93), channel_id=1, source_target_pairs={{8,0},{16,8},{24,16},{28,24},{20,28},{12,20},{4,12},{0,4},{9,1},{1... | collective-permute-start | bytes 1572872 | tf_op jit(solution)/shard_map/ppermute | solution.py:102
  188.4 13.2 %collective-permute-start.48 = (bf16[144,1024]{1,0:T(8,128)(2,1)S(1)}, bf16[144,1024]{1,0:T(8,128)(2,1)S(1)}, u32[]{:S(2)}, u32[]{:S(2)}) collective-permute-start(bf16[144,1024]{1,0:T(8,128)(2,1)S(1)} %get-tuple-element.79), channel_id=1, source_target_pairs={{0,8},{8,16},{16,24},{24,28},{28,20},{20,12},{12,4},{4,0},{1,9},{9... | collective-permute-start | bytes 884744 | tf_op jit(solution)/shard_map/ppermute | solution.py:101
  190.2 14.2 %collective-permute-start.49 = (bf16[144,1024]{1,0:T(8,128)(2,1)S(1)}, bf16[144,1024]{1,0:T(8,128)(2,1)S(1)}, u32[]{:S(2)}, u32[]{:S(2)}) collective-permute-start(bf16[144,1024]{1,0:T(8,128)(2,1)S(1)} %get-tuple-element.80), channel_id=1, source_target_pairs={{8,0},{16,8},{24,16},{28,24},{20,28},{12,20},{4,12},{0,4},{9,1},{1... | collective-permute-start | bytes 884744 | tf_op jit(solution)/shard_map/ppermute | solution.py:102
  (58 other events, 389.4 us)
where the time goes:
time: 207 us; the launch traced here: 206 us
  waiting for transfers between devices  101 us (49%)
  starting transfers between devices  44.1 us (21%)
  Pallas kernels  26.3 us (13%)
  local copies, waits for them, and re-layouts  15 us (7%)
  matrix products  8.84 us (4%)
  other arithmetic  8.29 us (4%)
  between operations  2.38 us (1%)
    ppermute x16, waiting for transfers between devices, step(): going_up = lax.ppermute(going_up, 'dp', self.up)  46.6 us
    ppermute x26, waiting for transfers between devices, swap(): return lax.ppermute(array, axis, [(i, i ^ bit) for i in range(size)])  32.5 us
    ppermute x16, waiting for transfers between devices, step(): going_down = lax.ppermute(going_down, 'dp', self.down)  22.2 us
    ppermute x16, starting transfers between devices, step(): going_up = lax.ppermute(going_up, 'dp', self.up)  17 us
    ppermute x16, starting transfers between devices, step(): going_down = lax.ppermute(going_down, 'dp', self.down)  15.4 us
    pallas_call x10, Pallas kernels, ring_sum(): pl.pallas_call(functools.partial(ring_sum_kernel, places, stage, shapes,...  14.4 us
    ppermute x26, starting transfers between devices, swap(): return lax.ppermute(array, axis, [(i, i ^ bit) for i in range(size)])  11.8 us
    unnamed x69, local copies, waits for them, and re-layouts  9.46 us
  transfers between devices with their start and end apart: 58, of which 29 were waited for; matrix products, arithmetic and copies ran while one was open for 9% of the time, Pallas kernels for 12%

commit v1 on v0

--- a/solution.py
+++ b/solution.py
@@ -316,37 +316,42 @@
 QUERY_TILE = 256
 
 
-def head_lanes(shape, head):
-    lane = lax.broadcasted_iota(jnp.int32, shape, 1)
-    return (lane >= head * HD) & (lane < (head + 1) * HD)
-
-
-def keep_head(block, head):
-    return jnp.where(head_lanes(block.shape, head), block, jnp.zeros_like(block))
-
-
-def scores_of(key_block, query_block, counts_ref, score_scale):
-    scores = matmul_nt(key_block, query_block) * score_scale
-    rows = scores.shape[0] // counts_ref.shape[0]
-    valid = [
-        lax.broadcasted_iota(jnp.int32, (rows, scores.shape[1]), 0) < counts_ref[r]
-        for r in range(counts_ref.shape[0])
-    ]
-    return jnp.where(jnp.concatenate(valid, axis=0), scores, MASKED)
+def keep_head(block, head, other=None):
+    lane = lax.broadcasted_iota(jnp.int32, block.shape, 1)
+    kept = (lane >= head * HD) & (lane < (head + 1) * HD)
+    rest = jnp.zeros_like(block)
+    if other is not None:
+        spare = HD * (1 - head)
+        rest = jnp.where(lane == spare, other, rest)
+    return jnp.where(kept, block, rest)
+
+
+def key_offsets(shape, counts_ref):
+    rows = shape[0] // counts_ref.shape[0]
+    row = lax.broadcasted_iota(jnp.int32, (rows, shape[1]), 0)
+    parts = [jnp.where(row < counts_ref[r], 0.0, MASKED) for r in range(counts_ref.shape[0])]
+    return jnp.concatenate(parts, axis=0).astype(BF16)
+
+
+def scores_of(keys, offsets, scaled_queries, head):
+    with_offsets = keep_head(keys, head, offsets)
+    with_ones = keep_head(scaled_queries, head, jnp.ones_like(scaled_queries))
+    return matmul_nt(with_offsets, with_ones)
 
 
 def attention_kernel(score_scale, counts_ref, query_ref, key_ref, value_ref, context_ref, log_total_ref):
     keys, values = key_ref[...], value_ref[...]
+    offsets = key_offsets(keys.shape, counts_ref)
+    queries = query_ref[...] * jnp.asarray(score_scale, BF16)
     pieces = []
     for head in range(LANES // HD):
-        scores = scores_of(keys, keep_head(query_ref[...], head), counts_ref, score_scale)
+        scores = scores_of(keys, offsets, queries, head)
         row_peak = jnp.max(scores, axis=0, keepdims=True)
         raised = jnp.exp(scores - row_peak)
         total = jnp.sum(raised, axis=0, keepdims=True)
         log_total_ref[0, head : head + 1, :] = row_peak + jnp.log(total)
-        probs_low = (raised * (1.0 / total)).astype(BF16)
-        both = matmul_tn(values, probs_low)
-        pieces.append(both[head * HD : (head + 1) * HD])
+        both = matmul_tn(values, raised.astype(BF16))
+        pieces.append(both[head * HD : (head + 1) * HD] * (1.0 / total))
     context_ref[...] = jnp.concatenate(pieces, axis=0).T.astype(BF16)
 
 
@@ -405,18 +410,20 @@
         query_sum_ref[...] = jnp.zeros_like(query_sum_ref)
 
     keys, values = key_ref[...], value_ref[...]
+    offsets = key_offsets(keys.shape, counts_ref)
+    scale = jnp.asarray(score_scale, BF16)
+    queries, scaled_keys = query_ref[...] * scale, keys * scale
     pieces = []
     for head in range(LANES // HD):
-        queries = keep_head(query_ref[...], head)
         upstream = keep_head(upstream_ref[...], head)
-        scores = scores_of(keys, queries, counts_ref, score_scale)
+        scores = scores_of(keys, offsets, queries, head)
         probs = jnp.exp(scores - log_total_ref[0, head : head + 1, :])
         prob_grad = matmul_nt(values, upstream)
         row_inner = jnp.sum(probs * prob_grad, axis=0, keepdims=True)
-        score_grad = (probs * (prob_grad - row_inner) * score_scale).astype(BF16)
+        score_grad = (probs * (prob_grad - row_inner)).astype(BF16)
         value_total[...] += matmul(probs.astype(BF16), upstream)
-        key_total[...] += matmul(score_grad, queries)
-        both = matmul_tn(keys, score_grad)
+        key_total[...] += matmul(score_grad, keep_head(queries, head))
+        both = matmul_tn(scaled_keys, score_grad)
         pieces.append(both[head * HD : (head + 1) * HD])
     query_grad = jnp.concatenate(pieces, axis=0).T
     rows = pl.ds(pl.multiple_of(step * QUERY_TILE, QUERY_TILE), QUERY_TILE)
@@ -494,8 +501,8 @@
     packed = row_major(jnp.concatenate([query_weight, key_weight, value_weight, output_weight.T], axis=1))
     (packed_full,) = ring.gather(packed, (packed.shape[0],))
     hidden_full = gather_rows(hidden_in)
-    stacked = row_major(jnp.concatenate([up_weight, down_weight.T], axis=0))
-    up_full, down_turned = ring.gather(stacked, (up_weight.shape[0], down_weight.shape[1]))
+    (up_full,) = ring.gather(up_weight, (up_weight.shape[0],))
+    (down_turned,) = ring.gather(row_major(down_weight.T), (down_weight.shape[1],))
     qkv_full = packed_full[:, : 3 * local_width]
     output_turned = packed_full[:, 3 * local_width :]
 

time: 207 us -> 215 us (1.039)
  waiting for transfers between devices: 101 us -> 84.6 us
  local copies, waits for them, and re-layouts: 15 us -> 26.9 us
  starting transfers between devices: 44.1 us -> 51.9 us
  matrix products: 8.84 us -> 16 us
    ppermute x16 -> x20, waiting for transfers between devices: 46.6 us -> 34.8 us  [step(): going_up = lax.ppermute(going_up, 'dp', self.up)]
    dynamic_update_slice x17 -> x26, local copies, waits for them, and re-layouts: 4.49 us -> 15.8 us  [put(): lax.dynamic_update_slice_in_dim(wholes[i], part[low - first:high - first]...]
    ppermute x16 -> x20, starting transfers between devices: 17 us -> 25.4 us  [step(): going_up = lax.ppermute(going_up, 'dp', self.up)]
    ppermute x16 -> x20, waiting for transfers between devices: 22.2 us -> 18.2 us  [step(): going_down = lax.ppermute(going_down, 'dp', self.down)]
    dot_general x4, matrix products: 4.07 us -> 8 us  [matmul_nt(): lax.dot_general(left_side, right_side, (((1,), (1,)), ((), ())), preferre...]
    dot_general x4, matrix products: 4.78 us -> 7.96 us  [matmul(): return jnp.dot(left_side, right_side, preferred_element_type=F32)]
    another operation x3, local copies, waits for them, and re-layouts: 0.75 us -> 3.47 us
    unnamed x69 -> x61, local copies, waits for them, and re-layouts: 9.46 us -> 7.36 us
  transfers between devices with their start and end apart: 58 -> 66, of which waited for: 29 -> 27; matrix products, arithmetic and copies ran while one was open for 9% -> 14% of each run, Pallas kernels for 12% -> 11%
where the time goes in v1:
time: 215 us
  waiting for transfers between devices  84.6 us (39%)
  starting transfers between devices  51.9 us (24%)
  local copies, waits for them, and re-layouts  26.9 us (13%)
  Pallas kernels  25.7 us (12%)
  matrix products  16 us (7%)
  other arithmetic  7.44 us (3%)
  between operations  2.45 us (1%)
    ppermute x20, waiting for transfers between devices, step(): going_up = lax.ppermute(going_up, 'dp', self.up)  34.8 us
    ppermute x26, waiting for transfers between devices, swap(): return lax.ppermute(array, axis, [(i, i ^ bit) for i in range(size)])  31.5 us
    ppermute x20, starting transfers between devices, step(): going_up = lax.ppermute(going_up, 'dp', self.up)  25.4 us
    ppermute x20, waiting for transfers between devices, step(): going_down = lax.ppermute(going_down, 'dp', self.down)  18.2 us
    ppermute x20, starting transfers between devices, step(): going_down = lax.ppermute(going_down, 'dp', self.down)  16.6 us
    dynamic_update_slice x26, local copies, waits for them, and re-layouts, put(): lax.dynamic_update_slice_in_dim(wholes[i], part[low - first:high - first]...  15.8 us
    pallas_call x10, Pallas kernels, ring_sum(): pl.pallas_call(functools.partial(ring_sum_kernel, places, stage, shapes,...  14.4 us
    ppermute x26, starting transfers between devices, swap(): return lax.ppermute(array, axis, [(i, i ^ bit) for i in range(size)])  9.92 us
  transfers between devices with their start and end apart: 66, of which 27 were waited for; matrix products, arithmetic and copies ran while one was open for 14% of the time, Pallas kernels for 11%

profile of v1, /device:TPU:0, one launch (start us, length us, event | category | flops | bytes accessed | tf_op | source)
XLA Modules:
  0.0 214.8 jit_solution(14073530606762226900)
XLA Ops:
  1.8 3.1 %collective-permute-start.25 = (bf16[128,1024]{1,0:T(8,128)(2,1)S(1)}, bf16[128,1024]{1,0:T(8,128)(2,1)}, u32[]{:S(2)}, u32[]{:S(2)}) collective-permute-start(bf16[128,1024]{1,0:T(8,128)(2,1)S(1)} %bitcast.40), channel_id=1, source_target_pairs={{0,8},{8,16},{16,24},{24,28},{28,20},{20,12},{12,4},{4,0},{1,9},{9... | collective-permute-start | bytes 786440 | tf_op jit(solution)/shard_map/ppermute | solution.py:101
  4.9 2.0 collective-permute-start.1
  21.7 2.8 %collective-permute-done.17 = bf16[128,1024]{1,0:T(8,128)(2,1)S(1)} collective-permute-done((bf16[128,1024]{1,0:T(8,128)(2,1)}, bf16[128,1024]{1,0:T(8,128)(2,1)S(1)}, u32[]{:S(2)}, u32[]{:S(2)}) %collective-permute-start.17) | collective-permute-done | bytes 262176 | tf_op jit(solution)/shard_map/ppermute | solution.py:101
  25.3 2.9 %collective-permute-done.4 = bf16[128,1024]{1,0:T(8,128)(2,1)S(1)} collective-permute-done((bf16[128,1024]{1,0:T(8,128)(2,1)}, bf16[128,1024]{1,0:T(8,128)(2,1)S(1)}, u32[]{:S(2)}, u32[]{:S(2)}) %collective-permute-start.4) | collective-permute-done | bytes 262176 | tf_op jit(solution)/shard_map/ppermute | solution.py:102
  30.3 1.7 constant_dynamic-update-slice_fusion.11
  33.5 1.7 constant_dynamic-update-slice_fusion.10
  35.7 1.9 collective-permute-done.5
  40.8 5.3 %collective-permute-done.7 = bf16[128,1024]{1,0:T(8,128)(2,1)S(1)} collective-permute-done((bf16[128,1024]{1,0:T(8,128)(2,1)S(1)}, bf16[128,1024]{1,0:T(8,128)(2,1)S(1)}, u32[]{:S(2)}, u32[]{:S(2)}) %collective-permute-start.7) | collective-permute-done | bytes 262176 | tf_op jit(solution)/shard_map/ppermute | solution.py:101
  47.7 7.3 %collective-permute-done.8 = bf16[128,1024]{1,0:T(8,128)(2,1)S(1)} collective-permute-done((bf16[128,1024]{1,0:T(8,128)(2,1)S(1)}, bf16[128,1024]{1,0:T(8,128)(2,1)S(1)}, u32[]{:S(2)}, u32[]{:S(2)}) %collective-permute-start.8) | collective-permute-done | bytes 262176 | tf_op jit(solution)/shard_map/ppermute | solution.py:102
  59.7 1.7 collective-permute-done.9
  64.0 5.1 %attention.1 = (bf16[512,256]{1,0:T(8,128)(2,1)S(1)}, f32[2,2,512]{2,1,0:T(2,128)S(1)}) custom-call(s32[4]{0:T(128)S(1)} %multiply_subtract_fusion.counts_ref, bf16[512,768]{1,0:T(8,128)(2,1)S(1)} %add_convert_fusion.query_ref.key_ref.value_ref, bf16[512,768]{1,0:T(8,128)(2,1)S(1)} %add_convert_fusion.query_ref.key_ref.value_ref, ...), custom_call_target="tpu_custom_call" | custom-call | flops 268435456 | bytes 1048576 | tf_op jit(solution)/shard_map/attention/pallas_call | solution.py:362
  84.2 4.8 %collective-permute-done.15 = bf16[128,1024]{1,0:T(8,128)(2,1)S(1)} collective-permute-done((bf16[128,1024]{1,0:T(8,128)(2,1)S(1)}, bf16[128,1024]{1,0:T(8,128)(2,1)S(1)}, u32[]{:S(2)}, u32[]{:S(2)}) %collective-permute-start.15) | collective-permute-done | bytes 262176 | tf_op jit(solution)/shard_map/ppermute | solution.py:65
  90.9 3.6 %fusion.3 = (f32[512,1024]{1,0:T(8,128)S(1)}, bf16[512,1024]{1,0:T(8,128)(2,1)S(1)}) fusion(f32[1024]{0:T(1024)S(1)} %copy-done.27, bf16[1024,1024]{1,0:T(8,128)(2,1)} %constant_dynamic-update-slice_fusion.13, bf16[128,1024]{1,0:T(8,128)(2,1)S(1)} %collective-permute-done.16, bf16[128,1024]{1,0:T(8,128)(2,1)S(1)} %collective-permute-done.15, ...), kind=kOutput, calls=%fused_computation.4 | convolution fusion | flops 1084227584 | bytes 6295552 | tf_op jit(solution)/shard_map/dot_general | solution.py:25
  94.6 3.3 %convolution_convert_fusion.2 = bf16[512,1024]{1,0:T(8,128)(2,1)S(1)} fusion(bf16[512,1024]{1,0:T(8,128)(2,1)S(1)} %get-tuple-element.62.refs_3_, bf16[1024,1024]{1,0:T(8,128)(2,1)} %constant_dynamic-update-slice_fusion.4), kind=kOutput, calls=%fused_computation.11 | convolution fusion | flops 1074266112 | bytes 4194304 | tf_op jit(solution)/shard_map/dot_general | solution.py:29
  100.3 8.1 %collective-permute-done.35 = bf16[128,1024]{1,0:T(8,128)(2,1)S(1)} collective-permute-done((bf16[128,1024]{1,0:T(8,128)(2,1)S(1)}, bf16[128,1024]{1,0:T(8,128)(2,1)S(1)}, u32[]{:S(2)}, u32[]{:S(2)}) %collective-permute-start.35) | collective-permute-done | bytes 262176 | tf_op jit(solution)/shard_map/ppermute | solution.py:65
  110.8 7.2 %collective-permute-done.37 = bf16[128,1024]{1,0:T(8,128)(2,1)S(1)} collective-permute-done((bf16[128,1024]{1,0:T(8,128)(2,1)S(1)}, bf16[128,1024]{1,0:T(8,128)(2,1)S(1)}, u32[]{:S(2)}, u32[]{:S(2)}) %collective-permute-start.37) | collective-permute-done | bytes 262176 | tf_op jit(solution)/shard_map/ppermute | solution.py:65
  119.6 2.9 %fusion.22 = (bf16[512,1024]{1,0:T(8,128)(2,1)S(1)}, f32[1024]{0:T(1024)S(1)}) fusion(f32[512,1024]{1,0:T(8,128)S(1)} %get-tuple-element.63, bf16[1024,1024]{1,0:T(8,128)(2,1)} %constant_dynamic-update-slice_fusion.4, bf16[128,1024]{1,0:T(8,128)(2,1)S(1)} %collective-permute-done.38, bf16[128,1024]{1,0:T(8,128)(2,1)S(1)} %collective-permute-done.37, ...), kind=kOutput, calls=%fused_computation.102 | convolution fusion | flops 1079507968 | bytes 6295552 | tf_op jit(solution)/shard_map/dot_general | solution.py:25
  122.4 3.3 %convolution_convert_fusion.1 = bf16[512,1024]{1,0:T(8,128)(2,1)S(1)} fusion(bf16[512,1024]{1,0:T(8,128)(2,1)S(1)} %get-tuple-element.64.refs_2_, bf16[1024,1024]{1,0:T(8,128)(2,1)} %constant_dynamic-update-slice_fusion.13), kind=kOutput, calls=%fused_computation.10 | convolution fusion | flops 1074266112 | bytes 4194304 | tf_op jit(solution)/shard_map/dot_general | solution.py:29
  130.4 5.6 %collective-permute-done.58.refs_4_ = bf16[128,1024]{1,0:T(8,128)(2,1)S(1)} collective-permute-done((bf16[128,1024]{1,0:T(8,128)(2,1)S(1)}, bf16[128,1024]{1,0:T(8,128)(2,1)S(1)}, u32[]{:S(2)}, u32[]{:S(2)}) %collective-permute-start.58) | collective-permute-done | bytes 262176 | tf_op jit(solution)/shard_map/ppermute | solution.py:101
  137.2 2.2 %ring_sum.16 = (bf16[256,1024]{1,0:T(8,128)(2,1)}, bf16[256,1024]{1,0:T(8,128)(2,1)}) custom-call(s32[2]{0:T(128)S(1)} %pad_add_fusion.3.owners_ref, bf16[512,1024]{1,0:T(8,128)(2,1)S(1)} %pad_maximum_fusion.refs_0_, bf16[512,1024]{1,0:T(8,128)(2,1)S(1)} %pad_maximum_fusion.1.refs_1_, bf16[512,1024]{1,0:T(8,128)(2,1)S(1)} %get-tuple-element.64.refs_2_, ...), custom_call_target="tpu_custom_call" | custom-call | flops 536870912 | bytes 3145728 | tf_op jit(solution)/shard_map/ring_sum/pallas_call | solution.py:296
  144.1 6.4 %collective-permute-done.43 = bf16[128,1024]{1,0:T(8,128)(2,1)} collective-permute-done((bf16[128,1024]{1,0:T(8,128)(2,1)}, bf16[128,1024]{1,0:T(8,128)(2,1)}, u32[]{:S(2)}, u32[]{:S(2)}) %collective-permute-start.43) | collective-permute-done | bytes 262176 | tf_op jit(solution)/shard_map/ppermute | solution.py:65
  155.4 2.0 ring_sum.17
  161.3 6.2 %attention_grad.1 = (bf16[512,768]{1,0:T(8,128)(2,1)S(1)}, f32[1,256]{1,0:T(1,128)S(1)}, f32[1,256]{1,0:T(1,128)S(1)}) custom-call(s32[4]{0:T(128)S(1)} %multiply_subtract_fusion.counts_ref, bf16[512,768]{1,0:T(8,128)(2,1)S(1)} %copy-done.1, bf16[512,768]{1,0:T(8,128)(2,1)S(1)} %copy-done.1, bf16[512,768]{1,0:T(8,128)(2,1)S(1)} %copy-done.1, ...), custom_call_target="tpu_custom_call" | custom-call | flops 671088640 | bytes 2097152 | tf_op jit(solution)/shard_map/attention_grad/pallas_call | solution.py:448
  171.5 3.2 %collective-permute-done.50.refs_4_ = bf16[80,1024]{1,0:T(8,128)(2,1)S(1)} collective-permute-done((bf16[80,1024]{1,0:T(8,128)(2,1)S(1)}, bf16[80,1024]{1,0:T(8,128)(2,1)S(1)}, u32[]{:S(2)}, u32[]{:S(2)}) %collective-permute-start.50) | collective-permute-done | bytes 163872 | tf_op jit(solution)/shard_map/ppermute | solution.py:101
  178.2 5.8 %collective-permute-done.52.refs_4_ = bf16[144,1024]{1,0:T(8,128)(2,1)S(1)} collective-permute-done((bf16[144,1024]{1,0:T(8,128)(2,1)S(1)}, bf16[144,1024]{1,0:T(8,128)(2,1)S(1)}, u32[]{:S(2)}, u32[]{:S(2)}) %collective-permute-start.52) | collective-permute-done | bytes 294944 | tf_op jit(solution)/shard_map/ppermute | solution.py:101
  186.0 1.8 collective-permute-start.55
  193.8 2.1 collective-permute-done.55.refs_5_
  200.0 5.7 %collective-permute-done.64.refs_4_ = bf16[256,1024]{1,0:T(8,128)(2,1)S(1)} collective-permute-done((bf16[256,1024]{1,0:T(8,128)(2,1)S(1)}, bf16[256,1024]{1,0:T(8,128)(2,1)S(1)}, u32[]{:S(2)}, u32[]{:S(2)}) %collective-permute-start.64) | collective-permute-done | bytes 524320 | tf_op jit(solution)/shard_map/ppermute | solution.py:101
  205.6 1.7 collective-permute-done.65.refs_5_
  207.3 2.0 ring_sum.19
  210.9 2.1 collective-permute-done.57.refs_5_
  213.0 1.7 ring_sum.14
  (258 shorter events, 95.5 us)
Async XLA Ops:
  1.8 27.9 %collective-permute-start.25 = (bf16[128,1024]{1,0:T(8,128)(2,1)S(1)}, bf16[128,1024]{1,0:T(8,128)(2,1)}, u32[]{:S(2)}, u32[]{:S(2)}) collective-permute-start(bf16[128,1024]{1,0:T(8,128)(2,1)S(1)} %bitcast.40), channel_id=1, source_target_pairs={{0,8},{8,16},{16,24},{24,28},{28,20},{20,12},{12,4},{4,0},{1,9},{9... | collective-permute-start | bytes 786440 | tf_op jit(solution)/shard_map/ppermute | solution.py:101
  4.9 27.0 %collective-permute-start.26 = (bf16[128,1024]{1,0:T(8,128)(2,1)S(1)}, bf16[128,1024]{1,0:T(8,128)(2,1)}, u32[]{:S(2)}, u32[]{:S(2)}) collective-permute-start(bf16[128,1024]{1,0:T(8,128)(2,1)S(1)} %bitcast.41), channel_id=1, source_target_pairs={{8,0},{16,8},{24,16},{28,24},{20,28},{12,20},{4,12},{0,4},{9,1},{1... | collective-permute-start | bytes 786440 | tf_op jit(solution)/shard_map/ppermute | solution.py:102
  4.9 13.8 %collective-permute-start.1 = (bf16[128,1024]{1,0:T(8,128)(2,1)}, bf16[128,1024]{1,0:T(8,128)(2,1)}, u32[]{:S(2)}, u32[]{:S(2)}) collective-permute-start(bf16[128,1024]{1,0:T(8,128)(2,1)} %param.18), channel_id=1, source_target_pairs={{0,2},{1,3},{2,0},{3,1},{4,6},{5,7},{6,4},{7,5},{8,10},{9,11},{10,... | collective-permute-start | bytes 786440 | tf_op jit(solution)/shard_map/ppermute | solution.py:65
  8.9 11.3 %collective-permute-start.3 = (bf16[128,1024]{1,0:T(8,128)(2,1)}, bf16[128,1024]{1,0:T(8,128)(2,1)}, u32[]{:S(2)}, u32[]{:S(2)}) collective-permute-start(bf16[128,1024]{1,0:T(8,128)(2,1)} %get-tuple-element.135), channel_id=1, source_target_pairs={{0,8},{8,16},{16,24},{24,28},{28,20},{20,12},{12,4},{4,0},{1,9},{9... | collective-permute-start | bytes 786440 | tf_op jit(solution)/shard_map/ppermute | solution.py:101
  20.2 15.0 %collective-permute-start.18 = (bf16[128,1024]{1,0:T(8,128)(2,1)}, bf16[128,1024]{1,0:T(8,128)(2,1)S(1)}, u32[]{:S(2)}, u32[]{:S(2)}) collective-permute-start(bf16[128,1024]{1,0:T(8,128)(2,1)} %param.25), channel_id=1, source_target_pairs={{8,0},{16,8},{24,16},{28,24},{20,28},{12,20},{4,12},{0,4},{9,1},{1... | collective-permute-start | bytes 786440 | tf_op jit(solution)/shard_map/ppermute | solution.py:102
  24.5 15.3 %collective-permute-start.2 = (bf16[128,1024]{1,0:T(8,128)(2,1)}, bf16[128,1024]{1,0:T(8,128)(2,1)S(1)}, u32[]{:S(2)}, u32[]{:S(2)}) collective-permute-start(bf16[128,1024]{1,0:T(8,128)(2,1)} %collective-permute-done.1), channel_id=1, source_target_pairs={{0,1},{1,0},{2,3},{3,2},{4,5},{5,4},{6,7},{7,6},{8,9},{9,8},{10,11... | collective-permute-start | bytes 786440 | tf_op jit(solution)/shard_map/ppermute | solution.py:65
  32.0 24.6 %collective-permute-start.27 = (bf16[128,1024]{1,0:T(8,128)(2,1)}, bf16[128,1024]{1,0:T(8,128)(2,1)S(1)}, u32[]{:S(2)}, u32[]{:S(2)}) collective-permute-start(bf16[128,1024]{1,0:T(8,128)(2,1)} %collective-permute-done.25), channel_id=1, source_target_pairs={{0,8},{8,16},{16,24},{24,28},{28,20},{20,12},{12,4},{4,0},{1,9},{9... | collective-permute-start | bytes 786440 | tf_op jit(solution)/shard_map/ppermute | solution.py:101
  35.2 21.9 %collective-permute-start.28 = (bf16[128,1024]{1,0:T(8,128)(2,1)}, bf16[128,1024]{1,0:T(8,128)(2,1)S(1)}, u32[]{:S(2)}, u32[]{:S(2)}) collective-permute-start(bf16[128,1024]{1,0:T(8,128)(2,1)} %collective-permute-done.26), channel_id=1, source_target_pairs={{8,0},{16,8},{24,16},{28,24},{20,28},{12,20},{4,12},{0,4},{9,1},{1... | collective-permute-start | bytes 786440 | tf_op jit(solution)/shard_map/ppermute | solution.py:102
  39.8 18.9 %collective-permute-start.20 = (bf16[128,1024]{1,0:T(8,128)(2,1)S(1)}, bf16[128,1024]{1,0:T(8,128)(2,1)S(1)}, u32[]{:S(2)}, u32[]{:S(2)}) collective-permute-start(bf16[128,1024]{1,0:T(8,128)(2,1)S(1)} %collective-permute-done.18), channel_id=1, source_target_pairs={{8,0},{16,8},{24,16},{28,24},{20,28},{12,20},{4,12},{0,4},{9,1},{1... | collective-permute-start | bytes 786440 | tf_op jit(solution)/shard_map/ppermute | solution.py:102
  40.3 14.6 %collective-permute-start.8 = (bf16[128,1024]{1,0:T(8,128)(2,1)S(1)}, bf16[128,1024]{1,0:T(8,128)(2,1)S(1)}, u32[]{:S(2)}, u32[]{:S(2)}) collective-permute-start(bf16[128,1024]{1,0:T(8,128)(2,1)S(1)} %collective-permute-done.6), channel_id=1, source_target_pairs={{8,0},{16,8},{24,16},{28,24},{20,28},{12,20},{4,12},{0,4},{9,1},{1... | collective-permute-start | bytes 786440 | tf_op jit(solution)/shard_map/ppermute | solution.py:102
  46.1 13.1 %collective-permute-start.19 = (bf16[128,1024]{1,0:T(8,128)(2,1)S(1)}, bf16[128,1024]{1,0:T(8,128)(2,1)S(1)}, u32[]{:S(2)}, u32[]{:S(2)}) collective-permute-start(bf16[128,1024]{1,0:T(8,128)(2,1)S(1)} %collective-permute-done.17), channel_id=1, source_target_pairs={{0,8},{8,16},{16,24},{24,28},{28,20},{20,12},{12,4},{4,0},{1,9},{9... | collective-permute-start | bytes 786440 | tf_op jit(solution)/shard_map/ppermute | solution.py:101
  57.1 15.4 %collective-permute-start.29 = (bf16[128,1024]{1,0:T(8,128)(2,1)S(1)}, bf16[128,1024]{1,0:T(8,128)(2,1)S(1)}, u32[]{:S(2)}, u32[]{:S(2)}) collective-permute-start(bf16[128,1024]{1,0:T(8,128)(2,1)S(1)} %collective-permute-done.27), channel_id=1, source_target_pairs={{0,8},{8,16},{16,24},{24,28},{28,20},{20,12},{12,4},{4,0},{1,9},{9... | collective-permute-start | bytes 786440 | tf_op jit(solution)/shard_map/ppermute | solution.py:101
  58.7 15.1 %collective-permute-start.30 = (bf16[128,1024]{1,0:T(8,128)(2,1)S(1)}, bf16[128,1024]{1,0:T(8,128)(2,1)S(1)}, u32[]{:S(2)}, u32[]{:S(2)}) collective-permute-start(bf16[128,1024]{1,0:T(8,128)(2,1)S(1)} %collective-permute-done.28), channel_id=1, source_target_pairs={{8,0},{16,8},{24,16},{28,24},{20,28},{12,20},{4,12},{0,4},{9,1},{1... | collective-permute-start | bytes 786440 | tf_op jit(solution)/shard_map/ppermute | solution.py:102
  59.2 16.2 %collective-permute-start.22 = (bf16[128,1024]{1,0:T(8,128)(2,1)S(1)}, bf16[128,1024]{1,0:T(8,128)(2,1)S(1)}, u32[]{:S(2)}, u32[]{:S(2)}) collective-permute-start(bf16[128,1024]{1,0:T(8,128)(2,1)S(1)} %collective-permute-done.20), channel_id=1, source_target_pairs={{8,0},{16,8},{24,16},{28,24},{20,28},{12,20},{4,12},{0,4},{9,1},{1... | collective-permute-start | bytes 786440 | tf_op jit(solution)/shard_map/ppermute | solution.py:102
  61.3 14.7 %collective-permute-start.21 = (bf16[128,1024]{1,0:T(8,128)(2,1)S(1)}, bf16[128,1024]{1,0:T(8,128)(2,1)S(1)}, u32[]{:S(2)}, u32[]{:S(2)}) collective-permute-start(bf16[128,1024]{1,0:T(8,128)(2,1)S(1)} %collective-permute-done.19), channel_id=1, source_target_pairs={{0,8},{8,16},{16,24},{24,28},{28,20},{20,12},{12,4},{4,0},{1,9},{9... | collective-permute-start | bytes 786440 | tf_op jit(solution)/shard_map/ppermute | solution.py:101
  73.8 15.7 %collective-permute-start.31 = (bf16[64,1024]{1,0:T(8,128)(2,1)S(1)}, bf16[64,1024]{1,0:T(8,128)(2,1)S(1)}, u32[]{:S(2)}, u32[]{:S(2)}) collective-permute-start(bf16[64,1024]{1,0:T(8,128)(2,1)S(1)} %slice.106), channel_id=1, source_target_pairs={{0,8},{8,16},{16,24},{24,28},{28,20},{20,12},{12,4},{4,0},{1,9},{9... | collective-permute-start | bytes 393224 | tf_op jit(solution)/shard_map/ppermute | solution.py:101
  75.5 14.8 %collective-permute-start.32 = (bf16[64,1024]{1,0:T(8,128)(2,1)S(1)}, bf16[64,1024]{1,0:T(8,128)(2,1)S(1)}, u32[]{:S(2)}, u32[]{:S(2)}) collective-permute-start(bf16[64,1024]{1,0:T(8,128)(2,1)S(1)} %slice.107), channel_id=1, source_target_pairs={{8,0},{16,8},{24,16},{28,24},{20,28},{12,20},{4,12},{0,4},{9,1},{1... | collective-permute-start | bytes 393224 | tf_op jit(solution)/shard_map/ppermute | solution.py:102
  76.0 12.9 %collective-permute-start.24 = (bf16[64,1024]{1,0:T(8,128)(2,1)S(1)}, bf16[64,1024]{1,0:T(8,128)(2,1)S(1)}, u32[]{:S(2)}, u32[]{:S(2)}) collective-permute-start(bf16[64,1024]{1,0:T(8,128)(2,1)S(1)} %slice.105), channel_id=1, source_target_pairs={{8,0},{16,8},{24,16},{28,24},{20,28},{12,20},{4,12},{0,4},{9,1},{1... | collective-permute-start | bytes 393224 | tf_op jit(solution)/shard_map/ppermute | solution.py:102
  126.0 15.4 %collective-permute-start.39 = (bf16[128,1024]{1,0:T(8,128)(2,1)S(1)}, bf16[128,1024]{1,0:T(8,128)(2,1)S(1)}, u32[]{:S(2)}, u32[]{:S(2)}) collective-permute-start(bf16[128,1024]{1,0:T(8,128)(2,1)S(1)} %get-tuple-element.128), channel_id=1, source_target_pairs={{0,1},{1,0},{2,3},{3,2},{4,5},{5,4},{6,7},{7,6},{8,9},{9,8},{10,11... | collective-permute-start | bytes 786440 | tf_op jit(solution)/shard_map/ppermute | solution.py:65
  129.7 11.7 %collective-permute-start.41 = (bf16[128,1024]{1,0:T(8,128)(2,1)S(1)}, bf16[128,1024]{1,0:T(8,128)(2,1)S(1)}, u32[]{:S(2)}, u32[]{:S(2)}) collective-permute-start(bf16[128,1024]{1,0:T(8,128)(2,1)S(1)} %add_convert_fusion.3), channel_id=1, source_target_pairs={{0,2},{1,3},{2,0},{3,1},{4,6},{5,7},{6,4},{7,5},{8,10},{9,11},{10,... | collective-permute-start | bytes 786440 | tf_op jit(solution)/shard_map/ppermute | solution.py:65
  139.4 13.5 %collective-permute-start.60 = (bf16[256,1024]{1,0:T(8,128)(2,1)}, bf16[256,1024]{1,0:T(8,128)(2,1)}, u32[]{:S(2)}, u32[]{:S(2)}) collective-permute-start(bf16[256,1024]{1,0:T(8,128)(2,1)} %get-tuple-element.88), channel_id=1, source_target_pairs={{0,8},{8,16},{16,24},{24,28},{28,20},{20,12},{12,4},{4,0},{1,9},{9... | collective-permute-start | bytes 1572872 | tf_op jit(solution)/shard_map/ppermute | solution.py:101
  139.9 13.1 %collective-permute-start.61 = (bf16[256,1024]{1,0:T(8,128)(2,1)}, bf16[256,1024]{1,0:T(8,128)(2,1)}, u32[]{:S(2)}, u32[]{:S(2)}) collective-permute-start(bf16[256,1024]{1,0:T(8,128)(2,1)} %get-tuple-element.89), channel_id=1, source_target_pairs={{8,0},{16,8},{24,16},{28,24},{20,28},{12,20},{4,12},{0,4},{9,1},{1... | collective-permute-start | bytes 1572872 | tf_op jit(solution)/shard_map/ppermute | solution.py:102
  144.1 15.4 %collective-permute-start.42 = (bf16[128,1024]{1,0:T(8,128)(2,1)}, bf16[128,1024]{1,0:T(8,128)(2,1)}, u32[]{:S(2)}, u32[]{:S(2)}) collective-permute-start(bf16[128,1024]{1,0:T(8,128)(2,1)} %convert_element_type.146), channel_id=1, source_target_pairs={{0,1},{1,0},{2,3},{3,2},{4,5},{5,4},{6,7},{7,6},{8,9},{9,8},{10,11... | collective-permute-start | bytes 786440 | tf_op jit(solution)/shard_map/ppermute | solution.py:65
  152.4 15.0 %collective-permute-start.49 = (f32[6,1024]{1,0:T(8,128)S(1)}, f32[6,1024]{1,0:T(8,128)S(1)}, u32[]{:S(2)}, u32[]{:S(2)}) collective-permute-start(f32[6,1024]{1,0:T(8,128)S(1)} %add.481.refs_4_), channel_id=1, source_target_pairs={{0,2},{1,3},{2,0},{3,1},{4,6},{5,7},{6,4},{7,5},{8,10},{9,11},{10,... | collective-permute-start | bytes 73736 | tf_op jit(solution)/shard_map/ppermute | solution.py:65
  157.4 30.4 %collective-permute-start.62 = (bf16[256,1024]{1,0:T(8,128)(2,1)S(1)}, bf16[256,1024]{1,0:T(8,128)(2,1)S(1)}, u32[]{:S(2)}, u32[]{:S(2)}) collective-permute-start(bf16[256,1024]{1,0:T(8,128)(2,1)S(1)} %get-tuple-element.90), channel_id=1, source_target_pairs={{0,8},{8,16},{16,24},{24,28},{28,20},{20,12},{12,4},{4,0},{1,9},{9... | collective-permute-start | bytes 1572872 | tf_op jit(solution)/shard_map/ppermute | solution.py:101
  158.0 31.4 %collective-permute-start.63 = (bf16[256,1024]{1,0:T(8,128)(2,1)S(1)}, bf16[256,1024]{1,0:T(8,128)(2,1)S(1)}, u32[]{:S(2)}, u32[]{:S(2)}) collective-permute-start(bf16[256,1024]{1,0:T(8,128)(2,1)S(1)} %get-tuple-element.91), channel_id=1, source_target_pairs={{8,0},{16,8},{24,16},{28,24},{20,28},{12,20},{4,12},{0,4},{9,1},{1... | collective-permute-start | bytes 1572872 | tf_op jit(solution)/shard_map/ppermute | solution.py:102
  186.0 11.4 %collective-permute-start.45 = (bf16[128,1024]{1,0:T(8,128)(2,1)S(1)}, bf16[128,1024]{1,0:T(8,128)(2,1)S(1)}, u32[]{:S(2)}, u32[]{:S(2)}) collective-permute-start(bf16[128,1024]{1,0:T(8,128)(2,1)S(1)} %get-tuple-element.126), channel_id=1, source_target_pairs={{0,1},{1,0},{2,3},{3,2},{4,5},{5,4},{6,7},{7,6},{8,9},{9,8},{10,11... | collective-permute-start | bytes 786440 | tf_op jit(solution)/shard_map/ppermute | solution.py:65
  187.9 11.2 %collective-permute-start.47 = (bf16[128,1024]{1,0:T(8,128)(2,1)S(1)}, bf16[128,1024]{1,0:T(8,128)(2,1)S(1)}, u32[]{:S(2)}, u32[]{:S(2)}) collective-permute-start(bf16[128,1024]{1,0:T(8,128)(2,1)S(1)} %add_convert_fusion.2), channel_id=1, source_target_pairs={{0,2},{1,3},{2,0},{3,1},{4,6},{5,7},{6,4},{7,5},{8,10},{9,11},{10,... | collective-permute-start | bytes 786440 | tf_op jit(solution)/shard_map/ppermute | solution.py:65
  190.8 14.8 %collective-permute-start.64 = (bf16[256,1024]{1,0:T(8,128)(2,1)S(1)}, bf16[256,1024]{1,0:T(8,128)(2,1)S(1)}, u32[]{:S(2)}, u32[]{:S(2)}) collective-permute-start(bf16[256,1024]{1,0:T(8,128)(2,1)S(1)} %get-tuple-element.92), channel_id=1, source_target_pairs={{0,8},{8,16},{16,24},{24,28},{28,20},{20,12},{12,4},{4,0},{1,9},{9... | collective-permute-start | bytes 1572872 | tf_op jit(solution)/shard_map/ppermute | solution.py:101
  192.5 14.8 %collective-permute-start.65 = (bf16[256,1024]{1,0:T(8,128)(2,1)S(1)}, bf16[256,1024]{1,0:T(8,128)(2,1)S(1)}, u32[]{:S(2)}, u32[]{:S(2)}) collective-permute-start(bf16[256,1024]{1,0:T(8,128)(2,1)S(1)} %get-tuple-element.93), channel_id=1, source_target_pairs={{8,0},{16,8},{24,16},{28,24},{20,28},{12,20},{4,12},{0,4},{9,1},{1... | collective-permute-start | bytes 1572872 | tf_op jit(solution)/shard_map/ppermute | solution.py:102
  197.0 13.9 %collective-permute-start.56 = (bf16[144,1024]{1,0:T(8,128)(2,1)S(1)}, bf16[144,1024]{1,0:T(8,128)(2,1)S(1)}, u32[]{:S(2)}, u32[]{:S(2)}) collective-permute-start(bf16[144,1024]{1,0:T(8,128)(2,1)S(1)} %get-tuple-element.79), channel_id=1, source_target_pairs={{0,8},{8,16},{16,24},{24,28},{28,20},{20,12},{12,4},{4,0},{1,9},{9... | collective-permute-start | bytes 884744 | tf_op jit(solution)/shard_map/ppermute | solution.py:101
  197.4 15.6 %collective-permute-start.57 = (bf16[144,1024]{1,0:T(8,128)(2,1)S(1)}, bf16[144,1024]{1,0:T(8,128)(2,1)S(1)}, u32[]{:S(2)}, u32[]{:S(2)}) collective-permute-start(bf16[144,1024]{1,0:T(8,128)(2,1)S(1)} %get-tuple-element.80), channel_id=1, source_target_pairs={{8,0},{16,8},{24,16},{28,24},{20,28},{12,20},{4,12},{0,4},{9,1},{1... | collective-permute-start | bytes 884744 | tf_op jit(solution)/shard_map/ppermute | solution.py:102
  (62 other events, 452.3 us)

commit v2 on v1

--- a/solution.py
+++ b/solution.py
@@ -69,7 +69,11 @@
     far = swap(block, "tensor", 2)
     other_core = swap(block, "tensor", 1)
     far_core = swap(far, "tensor", 1)
-    return jnp.concatenate([block, other_core, far, far_core], axis=0)
+    rows = block.shape[0]
+    whole = jnp.zeros((4 * rows, block.shape[1]), block.dtype)
+    for i, part in enumerate((block, other_core, far, far_core)):
+        whole = lax.dynamic_update_slice_in_dim(whole, part, i * rows, 0)
+    return lax.optimization_barrier(whole)
 
 
 def scatter_rows(partial):
@@ -158,12 +162,23 @@
             return outs
         middle = self.size // 2
         arrived = list(ring_sum(layout, [self.owner(middle)] * 2, (), FIRST, (), vectors))
+        apart = len(layout) > 1 and middle > 2
         for step in range(1, middle + 1):
             arrived[:2] = self.step(arrived[0], arrived[1])
             distance = middle - step
+            if not distance and apart:
+                arrived[2:] = self.step(arrived[2], arrived[3])
             stage = STEP if distance else LAST
             arrived = list(
-                ring_sum(layout, [self.owner(distance), self.owner(-distance)], arrived, stage, shapes, vectors)
+                ring_sum(
+                    layout,
+                    [self.owner(distance), self.owner(-distance)],
+                    arrived,
+                    stage,
+                    shapes,
+                    vectors,
+                    distance == 1 and apart,
+                )
             )
         return arrived
 
@@ -188,6 +203,8 @@
     def term(i, direction):
         start = pl.multiple_of(owners_ref[direction] * rows, rows)
         return matmul_tn(lefts[i][:, pl.ds(start, rows)], rights[i][...])
+
+    by_row = stage != FIRST and not has_vectors and len(rest) == (4 + len(shapes) if stage == LAST else 6)
 
     def vectors_in(ref):
         first = ref.shape[0] - extra
@@ -237,7 +254,12 @@
             for direction, (low, high) in enumerate(((0, half), (half, total))):
                 if whole:
                     low, high = 0, total
-                value, arrived, target = term(i, direction), rest[direction], rest[2 + direction]
+                value, arrived = term(i, direction), rest[direction]
+                if by_row:
+                    added = value + arrived[row : row + rows, columns].astype(F32)
+                    rest[2 + 2 * (row // rows) + direction][:, columns] = added.astype(BF16)
+                    continue
+                target = rest[2 + direction]
                 first, last = max(row, low), min(row + rows, high)
                 if first < last:
                     added = value[first - row : last - row] + arrived[first - low : last - low, columns].astype(F32)
@@ -246,9 +268,11 @@
                     if begin < end:
                         target[begin:end, columns] = value[begin - row : end - row].astype(BF16)
         else:
-            value = term(i, 0) + rest[0][row : row + rows, columns].astype(F32)
-            value = value + rest[1][row : row + rows, columns].astype(F32)
-            for target, (source, start, stop, turned) in zip(rest[2 : 2 + len(shapes)], shapes):
+            pair, first = (2 * (row // rows), 0) if by_row else (0, row)
+            value = term(i, 0) + rest[pair][first : first + rows, columns].astype(F32)
+            value = value + rest[pair + 1][first : first + rows, columns].astype(F32)
+            targets = rest[4:] if by_row else rest[2 : 2 + len(shapes)]
+            for target, (source, start, stop, turned) in zip(targets, shapes):
                 if source == i:
                     target[...] = value[:, start:stop].T if turned else value[:, start:stop]
 
@@ -263,7 +287,7 @@
     return places
 
 
-def ring_sum(layout, owners, arrived, stage, shapes, vectors):
+def ring_sum(layout, owners, arrived, stage, shapes, vectors, apart=False):
     size = lax.axis_size("dp")
     places, lefts, rights, row = [], [], [], 0
     for terms in layout:
@@ -288,6 +312,8 @@
     else:
         travels = (row // 2 if stage == FIRST else row) + extra
         out_shape = [jax.ShapeDtypeStruct((travels, column), BF16)] * 2
+        if apart:
+            out_shape = [jax.ShapeDtypeStruct((row // len(layout), column), BF16)] * (2 * len(layout))
         if vectors:
             out_shape.append(jax.ShapeDtypeStruct((VECTOR_ROWS, column), F32))
         if stage == FIRST:
@@ -538,7 +564,7 @@
     grad_first_shift = jnp.sum(first_grad_in, axis=0)
     first_grad = norm_backward(first_grad_in, first_gain, first_normed, first_inverse)
     grad_output_bias = jnp.sum(first_grad, axis=0)
-    attn_grad_full = lax.optimization_barrier(gather_rows(first_grad.astype(BF16)))
+    attn_grad_full = gather_rows(first_grad.astype(BF16))
     context_grad = matmul(attn_grad_full, output_turned).astype(BF16)
 
     everywhere = jnp.stack(

time: 215 us -> 211 us (0.981)
  waiting for transfers between devices: 84.6 us -> 76.8 us
  local copies, waits for them, and re-layouts: 26.9 us -> 29.2 us
    dynamic_update_slice x0 -> x16, local copies, waits for them, and re-layouts: none -> 6.37 us  [gather_rows(): whole = lax.dynamic_update_slice_in_dim(whole, part, i * rows, 0)]
    unnamed x61 -> x54, local copies, waits for them, and re-layouts: 7.36 us -> 2.42 us
    ppermute x26, waiting for transfers between devices: 31.5 us -> 26.7 us  [swap(): return lax.ppermute(array, axis, [(i, i ^ bit) for i in range(size)])]
    ppermute x20 -> x21, starting transfers between devices: 25.4 us -> 27.9 us  [step(): going_up = lax.ppermute(going_up, 'dp', self.up)]
    ppermute x20 -> x21, waiting for transfers between devices: 18.2 us -> 15.8 us  [step(): going_down = lax.ppermute(going_down, 'dp', self.down)]
    ppermute x20 -> x21, starting transfers between devices: 16.6 us -> 15.8 us  [step(): going_down = lax.ppermute(going_down, 'dp', self.down)]
    ppermute x20 -> x21, waiting for transfers between devices: 34.8 us -> 34.4 us  [step(): going_up = lax.ppermute(going_up, 'dp', self.up)]
  transfers between devices with their start and end apart: 66 -> 68, of which waited for: 27 -> 30; matrix products, arithmetic and copies ran while one was open for 14% -> 17% of each run, Pallas kernels for 11% -> 11%
where the time goes in v2:
time: 211 us; the launch traced here: 210 us
  waiting for transfers between devices  76.8 us (36%)
  starting transfers between devices  54 us (26%)
  local copies, waits for them, and re-layouts  29.2 us (14%)
  Pallas kernels  25.8 us (12%)
  matrix products  15.8 us (7%)
  other arithmetic  6.14 us (3%)
  between operations  2.58 us (1%)
    ppermute x21, waiting for transfers between devices, step(): going_up = lax.ppermute(going_up, 'dp', self.up)  34.4 us
    ppermute x21, starting transfers between devices, step(): going_up = lax.ppermute(going_up, 'dp', self.up)  27.9 us
    ppermute x26, waiting for transfers between devices, swap(): return lax.ppermute(array, axis, [(i, i ^ bit) for i in range(size)])  26.7 us
    dynamic_update_slice x26, local copies, waits for them, and re-layouts, put(): lax.dynamic_update_slice_in_dim(wholes[i], part[low - first:high - first]...  16.7 us
    ppermute x21, starting transfers between devices, step(): going_down = lax.ppermute(going_down, 'dp', self.down)  15.8 us
    ppermute x21, waiting for transfers between devices, step(): going_down = lax.ppermute(going_down, 'dp', self.down)  15.8 us
    pallas_call x10, Pallas kernels, ring_sum(): pl.pallas_call(functools.partial(ring_sum_kernel, places, stage, shapes,...  14.5 us
    ppermute x26, starting transfers between devices, swap(): return lax.ppermute(array, axis, [(i, i ^ bit) for i in range(size)])  10.3 us
  transfers between devices with their start and end apart: 68, of which 30 were waited for; matrix products, arithmetic and copies ran while one was open for 17% of the time, Pallas kernels for 11%

profile of v2, /device:TPU:0, one launch (start us, length us, event | category | flops | bytes accessed | tf_op | source)
XLA Modules:
  0.0 210.3 jit_solution(4159599307348171374)
XLA Ops:
  1.3 2.6 %collective-permute-start.1 = (bf16[128,1024]{1,0:T(8,128)(2,1)}, bf16[128,1024]{1,0:T(8,128)(2,1)}, u32[]{:S(2)}, u32[]{:S(2)}) collective-permute-start(bf16[128,1024]{1,0:T(8,128)(2,1)} %param.18), channel_id=1, source_target_pairs={{0,2},{1,3},{2,0},{3,1},{4,6},{5,7},{6,4},{7,5},{8,10},{9,11},{10,... | collective-permute-start | bytes 786440 | tf_op jit(solution)/shard_map/ppermute | solution.py:65
  9.6 1.6 broadcast.107.clone.2
  13.6 1.7 constant_dynamic-update-slice_fusion.23
  18.7 1.6 collective-permute-start.25
  22.9 1.7 constant_dynamic-update-slice_fusion.22
  37.2 2.4 %collective-permute-done.19 = bf16[128,1024]{1,0:T(8,128)(2,1)S(1)} collective-permute-done((bf16[128,1024]{1,0:T(8,128)(2,1)}, bf16[128,1024]{1,0:T(8,128)(2,1)S(1)}, u32[]{:S(2)}, u32[]{:S(2)}) %collective-permute-start.19) | collective-permute-done | bytes 262176 | tf_op jit(solution)/shard_map/ppermute | solution.py:105
  44.6 6.2 %collective-permute-done.7 = bf16[128,1024]{1,0:T(8,128)(2,1)S(1)} collective-permute-done((bf16[128,1024]{1,0:T(8,128)(2,1)S(1)}, bf16[128,1024]{1,0:T(8,128)(2,1)S(1)}, u32[]{:S(2)}, u32[]{:S(2)}) %collective-permute-start.7) | collective-permute-done | bytes 262176 | tf_op jit(solution)/shard_map/ppermute | solution.py:105
  54.5 4.3 %collective-permute-done.9 = bf16[64,1024]{1,0:T(8,128)(2,1)S(1)} collective-permute-done((bf16[64,1024]{1,0:T(8,128)(2,1)S(1)}, bf16[64,1024]{1,0:T(8,128)(2,1)S(1)}, u32[]{:S(2)}, u32[]{:S(2)}) %collective-permute-start.9) | collective-permute-done | bytes 131104 | tf_op jit(solution)/shard_map/ppermute | solution.py:105
  61.4 5.1 %attention.1 = (bf16[512,256]{1,0:T(8,128)(2,1)S(1)}, f32[2,2,512]{2,1,0:T(2,128)S(1)}) custom-call(s32[4]{0:T(128)S(1)} %multiply_subtract_fusion.counts_ref, bf16[512,768]{1,0:T(8,128)(2,1)S(1)} %add_convert_fusion.query_ref.key_ref.value_ref, bf16[512,768]{1,0:T(8,128)(2,1)S(1)} %add_convert_fusion.query_ref.key_ref.value_ref, ...), custom_call_target="tpu_custom_call" | custom-call | flops 268435456 | bytes 1048576 | tf_op jit(solution)/shard_map/attention/pallas_call | solution.py:388
  73.1 4.0 %collective-permute-done.30 = bf16[128,1024]{1,0:T(8,128)(2,1)S(1)} collective-permute-done((bf16[128,1024]{1,0:T(8,128)(2,1)S(1)}, bf16[128,1024]{1,0:T(8,128)(2,1)S(1)}, u32[]{:S(2)}, u32[]{:S(2)}) %collective-permute-start.30) | collective-permute-done | bytes 262176 | tf_op jit(solution)/shard_map/ppermute | solution.py:106
  83.6 5.4 %collective-permute-done.15 = bf16[128,1024]{1,0:T(8,128)(2,1)S(1)} collective-permute-done((bf16[128,1024]{1,0:T(8,128)(2,1)S(1)}, bf16[128,1024]{1,0:T(8,128)(2,1)S(1)}, u32[]{:S(2)}, u32[]{:S(2)}) %collective-permute-start.15) | collective-permute-done | bytes 262176 | tf_op jit(solution)/shard_map/ppermute | solution.py:65
  90.5 3.4 %fusion.3 = (f32[512,1024]{1,0:T(8,128)S(1)}, bf16[512,1024]{1,0:T(8,128)(2,1)S(1)}) fusion(f32[1024]{0:T(1024)S(1)} %copy-done.25, bf16[512,1024]{1,0:T(8,128)(2,1)S(1)} %constant_dynamic-update-slice_fusion.24.refs_0_, bf16[1024,1024]{1,0:T(8,128)(2,1)} %constant_dynamic-update-slice_fusion.15), kind=kOutput, calls=%fused_computation.4 | convolution fusion | flops 1080033280 | bytes 6295552 | tf_op jit(solution)/shard_map/dot_general | solution.py:25
  93.9 3.3 %convolution_convert_fusion.2 = bf16[512,1024]{1,0:T(8,128)(2,1)S(1)} fusion(bf16[512,1024]{1,0:T(8,128)(2,1)S(1)} %get-tuple-element.64.refs_3_, bf16[1024,1024]{1,0:T(8,128)(2,1)} %constant_dynamic-update-slice_fusion.6), kind=kOutput, calls=%fused_computation.11 | convolution fusion | flops 1074266112 | bytes 4194304 | tf_op jit(solution)/shard_map/dot_general | solution.py:29
  99.5 7.8 %collective-permute-done.35 = bf16[128,1024]{1,0:T(8,128)(2,1)S(1)} collective-permute-done((bf16[128,1024]{1,0:T(8,128)(2,1)S(1)}, bf16[128,1024]{1,0:T(8,128)(2,1)S(1)}, u32[]{:S(2)}, u32[]{:S(2)}) %collective-permute-start.35) | collective-permute-done | bytes 262176 | tf_op jit(solution)/shard_map/ppermute | solution.py:65
  109.8 7.0 %collective-permute-done.37 = bf16[128,1024]{1,0:T(8,128)(2,1)S(1)} collective-permute-done((bf16[128,1024]{1,0:T(8,128)(2,1)S(1)}, bf16[128,1024]{1,0:T(8,128)(2,1)S(1)}, u32[]{:S(2)}, u32[]{:S(2)}) %collective-permute-start.37) | collective-permute-done | bytes 262176 | tf_op jit(solution)/shard_map/ppermute | solution.py:65
  118.3 2.9 %fusion.21 = (bf16[512,1024]{1,0:T(8,128)(2,1)S(1)}, f32[1024]{0:T(1024)S(1)}) fusion(f32[512,1024]{1,0:T(8,128)S(1)} %get-tuple-element.65, bf16[512,1024]{1,0:T(8,128)(2,1)S(1)} %constant_dynamic-update-slice_fusion.3.refs_1_, bf16[1024,1024]{1,0:T(8,128)(2,1)} %constant_dynamic-update-slice_fusion.6), kind=kOutput, calls=%fused_computation.106 | convolution fusion | flops 1075313664 | bytes 6295552 | tf_op jit(solution)/shard_map/dot_general | solution.py:25
  121.3 3.3 %convolution_convert_fusion.1 = bf16[512,1024]{1,0:T(8,128)(2,1)S(1)} fusion(bf16[512,1024]{1,0:T(8,128)(2,1)S(1)} %get-tuple-element.66.refs_2_, bf16[1024,1024]{1,0:T(8,128)(2,1)} %constant_dynamic-update-slice_fusion.15), kind=kOutput, calls=%fused_computation.10 | convolution fusion | flops 1074266112 | bytes 4194304 | tf_op jit(solution)/shard_map/dot_general | solution.py:29
  126.3 1.6 collective-permute-start.58
  129.1 5.6 %collective-permute-done.58.refs_4_ = bf16[128,1024]{1,0:T(8,128)(2,1)S(1)} collective-permute-done((bf16[128,1024]{1,0:T(8,128)(2,1)S(1)}, bf16[128,1024]{1,0:T(8,128)(2,1)S(1)}, u32[]{:S(2)}, u32[]{:S(2)}) %collective-permute-start.58) | collective-permute-done | bytes 262176 | tf_op jit(solution)/shard_map/ppermute | solution.py:105
  136.0 2.1 %ring_sum.16 = (bf16[256,1024]{1,0:T(8,128)(2,1)}, bf16[256,1024]{1,0:T(8,128)(2,1)}) custom-call(s32[2]{0:T(128)S(1)} %pad_add_fusion.3.owners_ref, bf16[512,1024]{1,0:T(8,128)(2,1)S(1)} %constant_dynamic-update-slice_fusion.24.refs_0_, bf16[512,1024]{1,0:T(8,128)(2,1)S(1)} %constant_dynamic-update-slice_fusion.3.refs_1_, ...), custom_call_target="tpu_custom_call" | custom-call | flops 536870912 | bytes 3145728 | tf_op jit(solution)/shard_map/ring_sum/pallas_call | solution.py:322
  145.6 3.4 %collective-permute-done.43 = bf16[128,1024]{1,0:T(8,128)(2,1)} collective-permute-done((bf16[128,1024]{1,0:T(8,128)(2,1)}, bf16[128,1024]{1,0:T(8,128)(2,1)}, u32[]{:S(2)}, u32[]{:S(2)}) %collective-permute-start.43) | collective-permute-done | bytes 262176 | tf_op jit(solution)/shard_map/ppermute | solution.py:65
  148.9 2.3 %collective-permute-done.60.refs_4_ = bf16[256,1024]{1,0:T(8,128)(2,1)} collective-permute-done((bf16[256,1024]{1,0:T(8,128)(2,1)}, bf16[256,1024]{1,0:T(8,128)(2,1)}, u32[]{:S(2)}, u32[]{:S(2)}) %collective-permute-start.60) | collective-permute-done | bytes 524320 | tf_op jit(solution)/shard_map/ppermute | solution.py:105
  153.8 2.2 %ring_sum.17 = (bf16[256,1024]{1,0:T(8,128)(2,1)S(1)}, bf16[256,1024]{1,0:T(8,128)(2,1)S(1)}) custom-call(s32[2]{0:T(128)S(1)} %pad_add_fusion.2.owners_ref, bf16[512,1024]{1,0:T(8,128)(2,1)S(1)} %constant_dynamic-update-slice_fusion.24.refs_0_, bf16[512,1024]{1,0:T(8,128)(2,1)S(1)} %constant_dynamic-update-slice_fusion.3.refs_1_, ...), custom_call_target="tpu_custom_call" | custom-call | flops 536870912 | bytes 3145728 | tf_op jit(solution)/shard_map/ring_sum/pallas_call | solution.py:322
  160.5 6.1 %attention_grad.1 = (bf16[512,768]{1,0:T(8,128)(2,1)S(1)}, f32[1,256]{1,0:T(1,128)S(1)}, f32[1,256]{1,0:T(1,128)S(1)}) custom-call(s32[4]{0:T(128)S(1)} %multiply_subtract_fusion.counts_ref, bf16[512,768]{1,0:T(8,128)(2,1)S(1)} %copy-done.1, bf16[512,768]{1,0:T(8,128)(2,1)S(1)} %copy-done.1, bf16[512,768]{1,0:T(8,128)(2,1)S(1)} %copy-done.1, ...), custom_call_target="tpu_custom_call" | custom-call | flops 671088640 | bytes 2097152 | tf_op jit(solution)/shard_map/attention_grad/pallas_call | solution.py:474
  170.7 2.3 %collective-permute-done.50.refs_4_ = bf16[80,1024]{1,0:T(8,128)(2,1)S(1)} collective-permute-done((bf16[80,1024]{1,0:T(8,128)(2,1)S(1)}, bf16[80,1024]{1,0:T(8,128)(2,1)S(1)}, u32[]{:S(2)}, u32[]{:S(2)}) %collective-permute-start.50) | collective-permute-done | bytes 163872 | tf_op jit(solution)/shard_map/ppermute | solution.py:105
  179.7 2.7 %collective-permute-done.52.refs_4_ = bf16[144,1024]{1,0:T(8,128)(2,1)S(1)} collective-permute-done((bf16[144,1024]{1,0:T(8,128)(2,1)S(1)}, bf16[144,1024]{1,0:T(8,128)(2,1)S(1)}, u32[]{:S(2)}, u32[]{:S(2)}) %collective-permute-start.52) | collective-permute-done | bytes 294944 | tf_op jit(solution)/shard_map/ppermute | solution.py:105
  189.6 5.0 %collective-permute-done.54.refs_4_ = bf16[144,1024]{1,0:T(8,128)(2,1)S(1)} collective-permute-done((bf16[144,1024]{1,0:T(8,128)(2,1)S(1)}, bf16[144,1024]{1,0:T(8,128)(2,1)S(1)}, u32[]{:S(2)}, u32[]{:S(2)}) %collective-permute-start.54) | collective-permute-done | bytes 294944 | tf_op jit(solution)/shard_map/ppermute | solution.py:105
  196.3 2.3 %collective-permute-done.65.refs_5_ = bf16[128,1024]{1,0:T(8,128)(2,1)S(1)} collective-permute-done((bf16[128,1024]{1,0:T(8,128)(2,1)S(1)}, bf16[128,1024]{1,0:T(8,128)(2,1)S(1)}, u32[]{:S(2)}, u32[]{:S(2)}) %collective-permute-start.65) | collective-permute-done | bytes 262176 | tf_op jit(solution)/shard_map/ppermute | solution.py:106
  201.4 2.1 ring_sum.19
  204.3 1.9 collective-permute-done.56.refs_4_
  206.2 2.3 %collective-permute-done.57.refs_5_ = bf16[144,1024]{1,0:T(8,128)(2,1)S(1)} collective-permute-done((bf16[144,1024]{1,0:T(8,128)(2,1)S(1)}, bf16[144,1024]{1,0:T(8,128)(2,1)S(1)}, u32[]{:S(2)}, u32[]{:S(2)}) %collective-permute-start.57) | collective-permute-done | bytes 294944 | tf_op jit(solution)/shard_map/ppermute | solution.py:106
  208.5 1.7 ring_sum.14
  (267 shorter events, 100.0 us)
Async XLA Ops:
  0.7 16.5 %collective-permute-start = (bf16[128,1024]{1,0:T(8,128)(2,1)}, bf16[128,1024]{1,0:T(8,128)(2,1)}, u32[]{:S(2)}, u32[]{:S(2)}) collective-permute-start(bf16[128,1024]{1,0:T(8,128)(2,1)} %param.18), channel_id=1, source_target_pairs={{0,1},{1,0},{2,3},{3,2},{4,5},{5,4},{6,7},{7,6},{8,9},{9,8},{10,11... | collective-permute-start | bytes 786440 | tf_op jit(solution)/shard_map/ppermute | solution.py:65
  1.3 17.5 %collective-permute-start.1 = (bf16[128,1024]{1,0:T(8,128)(2,1)}, bf16[128,1024]{1,0:T(8,128)(2,1)}, u32[]{:S(2)}, u32[]{:S(2)}) collective-permute-start(bf16[128,1024]{1,0:T(8,128)(2,1)} %param.18), channel_id=1, source_target_pairs={{0,2},{1,3},{2,0},{3,1},{4,6},{5,7},{6,4},{7,5},{8,10},{9,11},{10,... | collective-permute-start | bytes 786440 | tf_op jit(solution)/shard_map/ppermute | solution.py:65
  5.9 15.5 %collective-permute-start.3 = (bf16[128,1024]{1,0:T(8,128)(2,1)}, bf16[128,1024]{1,0:T(8,128)(2,1)}, u32[]{:S(2)}, u32[]{:S(2)}) collective-permute-start(bf16[128,1024]{1,0:T(8,128)(2,1)} %get-tuple-element.139), channel_id=1, source_target_pairs={{0,8},{8,16},{16,24},{24,28},{28,20},{20,12},{12,4},{4,0},{1,9},{9... | collective-permute-start | bytes 786440 | tf_op jit(solution)/shard_map/ppermute | solution.py:105
  7.4 17.2 %collective-permute-start.4 = (bf16[128,1024]{1,0:T(8,128)(2,1)}, bf16[128,1024]{1,0:T(8,128)(2,1)}, u32[]{:S(2)}, u32[]{:S(2)}) collective-permute-start(bf16[128,1024]{1,0:T(8,128)(2,1)} %get-tuple-element.139), channel_id=1, source_target_pairs={{8,0},{16,8},{24,16},{28,24},{20,28},{12,20},{4,12},{0,4},{9,1},{1... | collective-permute-start | bytes 786440 | tf_op jit(solution)/shard_map/ppermute | solution.py:106
  7.9 14.9 %collective-permute-start.17 = (bf16[128,1024]{1,0:T(8,128)(2,1)}, bf16[128,1024]{1,0:T(8,128)(2,1)}, u32[]{:S(2)}, u32[]{:S(2)}) collective-permute-start(bf16[128,1024]{1,0:T(8,128)(2,1)} %param.25), channel_id=1, source_target_pairs={{0,8},{8,16},{16,24},{24,28},{28,20},{20,12},{12,4},{4,0},{1,9},{9... | collective-permute-start | bytes 786440 | tf_op jit(solution)/shard_map/ppermute | solution.py:105
  17.2 9.9 %collective-permute-start.18 = (bf16[128,1024]{1,0:T(8,128)(2,1)}, bf16[128,1024]{1,0:T(8,128)(2,1)S(1)}, u32[]{:S(2)}, u32[]{:S(2)}) collective-permute-start(bf16[128,1024]{1,0:T(8,128)(2,1)} %param.25), channel_id=1, source_target_pairs={{8,0},{16,8},{24,16},{28,24},{20,28},{12,20},{4,12},{0,4},{9,1},{1... | collective-permute-start | bytes 786440 | tf_op jit(solution)/shard_map/ppermute | solution.py:106
  21.3 9.7 %collective-permute-start.26 = (bf16[128,1024]{1,0:T(8,128)(2,1)S(1)}, bf16[128,1024]{1,0:T(8,128)(2,1)S(1)}, u32[]{:S(2)}, u32[]{:S(2)}) collective-permute-start(bf16[128,1024]{1,0:T(8,128)(2,1)S(1)} %bitcast.43), channel_id=1, source_target_pairs={{8,0},{16,8},{24,16},{28,24},{20,28},{12,20},{4,12},{0,4},{9,1},{1... | collective-permute-start | bytes 786440 | tf_op jit(solution)/shard_map/ppermute | solution.py:106
  28.4 11.2 %collective-permute-start.19 = (bf16[128,1024]{1,0:T(8,128)(2,1)}, bf16[128,1024]{1,0:T(8,128)(2,1)S(1)}, u32[]{:S(2)}, u32[]{:S(2)}) collective-permute-start(bf16[128,1024]{1,0:T(8,128)(2,1)} %collective-permute-done.17), channel_id=1, source_target_pairs={{0,8},{8,16},{16,24},{24,28},{28,20},{20,12},{12,4},{4,0},{1,9},{9... | collective-permute-start | bytes 786440 | tf_op jit(solution)/shard_map/ppermute | solution.py:105
  31.1 11.2 %collective-permute-start.20 = (bf16[128,1024]{1,0:T(8,128)(2,1)S(1)}, bf16[128,1024]{1,0:T(8,128)(2,1)S(1)}, u32[]{:S(2)}, u32[]{:S(2)}) collective-permute-start(bf16[128,1024]{1,0:T(8,128)(2,1)S(1)} %collective-permute-done.18), channel_id=1, source_target_pairs={{8,0},{16,8},{24,16},{28,24},{20,28},{12,20},{4,12},{0,4},{9,1},{1... | collective-permute-start | bytes 786440 | tf_op jit(solution)/shard_map/ppermute | solution.py:106
  32.3 20.8 %collective-permute-start.27 = (bf16[128,1024]{1,0:T(8,128)(2,1)S(1)}, bf16[128,1024]{1,0:T(8,128)(2,1)S(1)}, u32[]{:S(2)}, u32[]{:S(2)}) collective-permute-start(bf16[128,1024]{1,0:T(8,128)(2,1)S(1)} %collective-permute-done.25), channel_id=1, source_target_pairs={{0,8},{8,16},{16,24},{24,28},{28,20},{20,12},{12,4},{4,0},{1,9},{9... | collective-permute-start | bytes 786440 | tf_op jit(solution)/shard_map/ppermute | solution.py:105
  34.0 16.9 %collective-permute-start.7 = (bf16[128,1024]{1,0:T(8,128)(2,1)S(1)}, bf16[128,1024]{1,0:T(8,128)(2,1)S(1)}, u32[]{:S(2)}, u32[]{:S(2)}) collective-permute-start(bf16[128,1024]{1,0:T(8,128)(2,1)S(1)} %collective-permute-done.5), channel_id=1, source_target_pairs={{0,8},{8,16},{16,24},{24,28},{28,20},{20,12},{12,4},{4,0},{1,9},{9... | collective-permute-start | bytes 786440 | tf_op jit(solution)/shard_map/ppermute | solution.py:105
  36.7 15.8 %collective-permute-start.8 = (bf16[128,1024]{1,0:T(8,128)(2,1)S(1)}, bf16[128,1024]{1,0:T(8,128)(2,1)S(1)}, u32[]{:S(2)}, u32[]{:S(2)}) collective-permute-start(bf16[128,1024]{1,0:T(8,128)(2,1)S(1)} %collective-permute-done.6), channel_id=1, source_target_pairs={{8,0},{16,8},{24,16},{28,24},{20,28},{12,20},{4,12},{0,4},{9,1},{1... | collective-permute-start | bytes 786440 | tf_op jit(solution)/shard_map/ppermute | solution.py:106
  39.6 28.3 %collective-permute-start.28 = (bf16[128,1024]{1,0:T(8,128)(2,1)S(1)}, bf16[128,1024]{1,0:T(8,128)(2,1)S(1)}, u32[]{:S(2)}, u32[]{:S(2)}) collective-permute-start(bf16[128,1024]{1,0:T(8,128)(2,1)S(1)} %collective-permute-done.26), channel_id=1, source_target_pairs={{8,0},{16,8},{24,16},{28,24},{20,28},{12,20},{4,12},{0,4},{9,1},{1... | collective-permute-start | bytes 786440 | tf_op jit(solution)/shard_map/ppermute | solution.py:106
  42.3 26.8 %collective-permute-start.21 = (bf16[128,1024]{1,0:T(8,128)(2,1)S(1)}, bf16[128,1024]{1,0:T(8,128)(2,1)S(1)}, u32[]{:S(2)}, u32[]{:S(2)}) collective-permute-start(bf16[128,1024]{1,0:T(8,128)(2,1)S(1)} %collective-permute-done.19), channel_id=1, source_target_pairs={{0,8},{8,16},{16,24},{24,28},{28,20},{20,12},{12,4},{4,0},{1,9},{9... | collective-permute-start | bytes 786440 | tf_op jit(solution)/shard_map/ppermute | solution.py:105
  53.1 18.4 %collective-permute-start.22 = (bf16[128,1024]{1,0:T(8,128)(2,1)S(1)}, bf16[128,1024]{1,0:T(8,128)(2,1)S(1)}, u32[]{:S(2)}, u32[]{:S(2)}) collective-permute-start(bf16[128,1024]{1,0:T(8,128)(2,1)S(1)} %collective-permute-done.20), channel_id=1, source_target_pairs={{8,0},{16,8},{24,16},{28,24},{20,28},{12,20},{4,12},{0,4},{9,1},{1... | collective-permute-start | bytes 786440 | tf_op jit(solution)/shard_map/ppermute | solution.py:106
  58.8 14.1 %collective-permute-start.29 = (bf16[128,1024]{1,0:T(8,128)(2,1)S(1)}, bf16[128,1024]{1,0:T(8,128)(2,1)S(1)}, u32[]{:S(2)}, u32[]{:S(2)}) collective-permute-start(bf16[128,1024]{1,0:T(8,128)(2,1)S(1)} %collective-permute-done.27), channel_id=1, source_target_pairs={{0,8},{8,16},{16,24},{24,28},{28,20},{20,12},{12,4},{4,0},{1,9},{9... | collective-permute-start | bytes 786440 | tf_op jit(solution)/shard_map/ppermute | solution.py:105
  69.1 12.4 %collective-permute-start.23 = (bf16[64,1024]{1,0:T(8,128)(2,1)S(1)}, bf16[64,1024]{1,0:T(8,128)(2,1)S(1)}, u32[]{:S(2)}, u32[]{:S(2)}) collective-permute-start(bf16[64,1024]{1,0:T(8,128)(2,1)S(1)} %slice.104), channel_id=1, source_target_pairs={{0,8},{8,16},{16,24},{24,28},{28,20},{20,12},{12,4},{4,0},{1,9},{9... | collective-permute-start | bytes 393224 | tf_op jit(solution)/shard_map/ppermute | solution.py:105
  124.8 15.3 %collective-permute-start.39 = (bf16[128,1024]{1,0:T(8,128)(2,1)S(1)}, bf16[128,1024]{1,0:T(8,128)(2,1)S(1)}, u32[]{:S(2)}, u32[]{:S(2)}) collective-permute-start(bf16[128,1024]{1,0:T(8,128)(2,1)S(1)} %get-tuple-element.132), channel_id=1, source_target_pairs={{0,1},{1,0},{2,3},{3,2},{4,5},{5,4},{6,7},{7,6},{8,9},{9,8},{10,11... | collective-permute-start | bytes 786440 | tf_op jit(solution)/shard_map/ppermute | solution.py:65
  128.4 11.7 %collective-permute-start.41 = (bf16[128,1024]{1,0:T(8,128)(2,1)S(1)}, bf16[128,1024]{1,0:T(8,128)(2,1)S(1)}, u32[]{:S(2)}, u32[]{:S(2)}) collective-permute-start(bf16[128,1024]{1,0:T(8,128)(2,1)S(1)} %add_convert_fusion.3), channel_id=1, source_target_pairs={{0,2},{1,3},{2,0},{3,1},{4,6},{5,7},{6,4},{7,5},{8,10},{9,11},{10,... | collective-permute-start | bytes 786440 | tf_op jit(solution)/shard_map/ppermute | solution.py:65
  138.1 13.2 %collective-permute-start.60 = (bf16[256,1024]{1,0:T(8,128)(2,1)}, bf16[256,1024]{1,0:T(8,128)(2,1)}, u32[]{:S(2)}, u32[]{:S(2)}) collective-permute-start(bf16[256,1024]{1,0:T(8,128)(2,1)} %get-tuple-element.90), channel_id=1, source_target_pairs={{0,8},{8,16},{16,24},{24,28},{28,20},{20,12},{12,4},{4,0},{1,9},{9... | collective-permute-start | bytes 1572872 | tf_op jit(solution)/shard_map/ppermute | solution.py:105
  139.7 12.9 %collective-permute-start.61 = (bf16[256,1024]{1,0:T(8,128)(2,1)}, bf16[256,1024]{1,0:T(8,128)(2,1)}, u32[]{:S(2)}, u32[]{:S(2)}) collective-permute-start(bf16[256,1024]{1,0:T(8,128)(2,1)} %get-tuple-element.91), channel_id=1, source_target_pairs={{8,0},{16,8},{24,16},{28,24},{20,28},{12,20},{4,12},{0,4},{9,1},{1... | collective-permute-start | bytes 1572872 | tf_op jit(solution)/shard_map/ppermute | solution.py:106
  142.1 16.0 %collective-permute-start.42 = (bf16[128,1024]{1,0:T(8,128)(2,1)}, bf16[128,1024]{1,0:T(8,128)(2,1)}, u32[]{:S(2)}, u32[]{:S(2)}) collective-permute-start(bf16[128,1024]{1,0:T(8,128)(2,1)} %convert_element_type.146), channel_id=1, source_target_pairs={{0,1},{1,0},{2,3},{3,2},{4,5},{5,4},{6,7},{7,6},{8,9},{9,8},{10,11... | collective-permute-start | bytes 786440 | tf_op jit(solution)/shard_map/ppermute | solution.py:65
  144.0 22.7 %collective-permute-start.49 = (f32[6,1024]{1,0:T(8,128)S(1)}, f32[6,1024]{1,0:T(8,128)S(1)}, u32[]{:S(2)}, u32[]{:S(2)}) collective-permute-start(f32[6,1024]{1,0:T(8,128)S(1)} %add.489.refs_4_), channel_id=1, source_target_pairs={{0,2},{1,3},{2,0},{3,1},{4,6},{5,7},{6,4},{7,5},{8,10},{9,11},{10,... | collective-permute-start | bytes 73736 | tf_op jit(solution)/shard_map/ppermute | solution.py:65
  148.9 11.1 %collective-permute-start.44 = (bf16[128,1024]{1,0:T(8,128)(2,1)}, bf16[128,1024]{1,0:T(8,128)(2,1)S(1)}, u32[]{:S(2)}, u32[]{:S(2)}) collective-permute-start(bf16[128,1024]{1,0:T(8,128)(2,1)} %collective-permute-done.43), channel_id=1, source_target_pairs={{0,1},{1,0},{2,3},{3,2},{4,5},{5,4},{6,7},{7,6},{8,9},{9,8},{10,11... | collective-permute-start | bytes 786440 | tf_op jit(solution)/shard_map/ppermute | solution.py:65
  156.0 21.7 %collective-permute-start.62 = (bf16[256,1024]{1,0:T(8,128)(2,1)S(1)}, bf16[256,1024]{1,0:T(8,128)(2,1)S(1)}, u32[]{:S(2)}, u32[]{:S(2)}) collective-permute-start(bf16[256,1024]{1,0:T(8,128)(2,1)S(1)} %get-tuple-element.92), channel_id=1, source_target_pairs={{0,8},{8,16},{16,24},{24,28},{28,20},{20,12},{12,4},{4,0},{1,9},{9... | collective-permute-start | bytes 1572872 | tf_op jit(solution)/shard_map/ppermute | solution.py:105
  157.5 20.2 %collective-permute-start.63 = (bf16[256,1024]{1,0:T(8,128)(2,1)S(1)}, bf16[256,1024]{1,0:T(8,128)(2,1)S(1)}, u32[]{:S(2)}, u32[]{:S(2)}) collective-permute-start(bf16[256,1024]{1,0:T(8,128)(2,1)S(1)} %get-tuple-element.93), channel_id=1, source_target_pairs={{8,0},{16,8},{24,16},{28,24},{20,28},{12,20},{4,12},{0,4},{9,1},{1... | collective-permute-start | bytes 1572872 | tf_op jit(solution)/shard_map/ppermute | solution.py:106
  177.6 9.8 %collective-permute-start.46 = (bf16[128,1024]{1,0:T(8,128)(2,1)S(1)}, bf16[128,1024]{1,0:T(8,128)(2,1)S(1)}, u32[]{:S(2)}, u32[]{:S(2)}) collective-permute-start(bf16[128,1024]{1,0:T(8,128)(2,1)S(1)} %get-tuple-element.131), channel_id=1, source_target_pairs={{0,1},{1,0},{2,3},{3,2},{4,5},{5,4},{6,7},{7,6},{8,9},{9,8},{10,11... | collective-permute-start | bytes 786440 | tf_op jit(solution)/shard_map/ppermute | solution.py:65
  183.9 10.7 %collective-permute-start.54 = (bf16[144,1024]{1,0:T(8,128)(2,1)S(1)}, bf16[144,1024]{1,0:T(8,128)(2,1)S(1)}, u32[]{:S(2)}, u32[]{:S(2)}) collective-permute-start(bf16[144,1024]{1,0:T(8,128)(2,1)S(1)} %get-tuple-element.78), channel_id=1, source_target_pairs={{0,8},{8,16},{16,24},{24,28},{28,20},{20,12},{12,4},{4,0},{1,9},{9... | collective-permute-start | bytes 884744 | tf_op jit(solution)/shard_map/ppermute | solution.py:105
  184.5 10.2 %collective-permute-start.55 = (bf16[144,1024]{1,0:T(8,128)(2,1)S(1)}, bf16[144,1024]{1,0:T(8,128)(2,1)S(1)}, u32[]{:S(2)}, u32[]{:S(2)}) collective-permute-start(bf16[144,1024]{1,0:T(8,128)(2,1)S(1)} %get-tuple-element.79), channel_id=1, source_target_pairs={{8,0},{16,8},{24,16},{28,24},{20,28},{12,20},{4,12},{0,4},{9,1},{1... | collective-permute-start | bytes 884744 | tf_op jit(solution)/shard_map/ppermute | solution.py:106
  186.0 12.6 %collective-permute-start.65 = (bf16[128,1024]{1,0:T(8,128)(2,1)S(1)}, bf16[128,1024]{1,0:T(8,128)(2,1)S(1)}, u32[]{:S(2)}, u32[]{:S(2)}) collective-permute-start(bf16[128,1024]{1,0:T(8,128)(2,1)S(1)} %get-tuple-element.95), channel_id=1, source_target_pairs={{8,0},{16,8},{24,16},{28,24},{20,28},{12,20},{4,12},{0,4},{9,1},{1... | collective-permute-start | bytes 786440 | tf_op jit(solution)/shard_map/ppermute | solution.py:106
  187.5 12.8 %collective-permute-start.66 = (bf16[128,1024]{1,0:T(8,128)(2,1)S(1)}, bf16[128,1024]{1,0:T(8,128)(2,1)S(1)}, u32[]{:S(2)}, u32[]{:S(2)}) collective-permute-start(bf16[128,1024]{1,0:T(8,128)(2,1)S(1)} %get-tuple-element.96), channel_id=1, source_target_pairs={{0,8},{8,16},{16,24},{24,28},{28,20},{20,12},{12,4},{4,0},{1,9},{9... | collective-permute-start | bytes 786440 | tf_op jit(solution)/shard_map/ppermute | solution.py:105
  188.3 13.1 %collective-permute-start.67 = (bf16[128,1024]{1,0:T(8,128)(2,1)S(1)}, bf16[128,1024]{1,0:T(8,128)(2,1)S(1)}, u32[]{:S(2)}, u32[]{:S(2)}) collective-permute-start(bf16[128,1024]{1,0:T(8,128)(2,1)S(1)} %get-tuple-element.97), channel_id=1, source_target_pairs={{8,0},{16,8},{24,16},{28,24},{20,28},{12,20},{4,12},{0,4},{9,1},{1... | collective-permute-start | bytes 786440 | tf_op jit(solution)/shard_map/ppermute | solution.py:106
  (62 other events, 473.5 us)

commit v3 on v2

--- a/solution.py
+++ b/solution.py
@@ -60,6 +60,60 @@
     )
 
 
+def sum_of(refs):
+    first, *others = refs
+    total = first[...].astype(F32)
+    for ref in others:
+        total = total + ref[...].astype(F32)
+    return total
+
+
+def first_norm_kernel(*refs):
+    bias, gain, shift = (ref[...] for ref in refs[4:7])
+    out_ref, normed_ref, inverse_ref, low_ref = refs[7:]
+    out, normed, inverse = norm_forward(sum_of(refs[:4]) + bias, gain, shift)
+    out_ref[...], normed_ref[...], inverse_ref[...] = out, normed, inverse
+    low_ref[...] = out.astype(BF16)
+
+
+def second_norm_kernel(*refs):
+    bias, gain, shift, upstream = (ref[...].astype(F32) for ref in refs[4:8])
+    out_ref, grad_ref, low_ref, sums_ref = refs[8:]
+    out, normed, inverse = norm_forward(sum_of(refs[:4]) + bias, gain, shift)
+    out_ref[...] = out.astype(BF16)
+    grad = norm_backward(upstream, gain, normed, inverse)
+    grad_ref[...] = grad
+    low_ref[...] = grad.astype(BF16)
+    sums_ref[0:1] = jnp.sum(upstream * normed, axis=0, keepdims=True)
+    sums_ref[1:2] = jnp.sum(upstream, axis=0, keepdims=True)
+    sums_ref[2:3] = jnp.sum(grad, axis=0, keepdims=True)
+
+
+def first_grad_kernel(*refs):
+    gain, normed, inverse = (ref[...] for ref in refs[4:7])
+    grad_ref, low_ref, sums_ref = refs[7:]
+    upstream = sum_of(refs[:4])
+    grad = norm_backward(upstream, gain, normed, inverse)
+    grad_ref[...] = grad
+    low_ref[...] = grad.astype(BF16)
+    sums_ref[0:1] = jnp.sum(upstream * normed, axis=0, keepdims=True)
+    sums_ref[1:2] = jnp.sum(upstream, axis=0, keepdims=True)
+    sums_ref[2:3] = jnp.sum(grad, axis=0, keepdims=True)
+
+
+def norm_stage(kernel, operands, outs):
+    vmem = pl.BlockSpec(memory_space=pltpu.VMEM)
+    size = operands[0].size
+    return pl.pallas_call(
+        kernel,
+        in_specs=[vmem] * len(operands),
+        out_specs=[vmem] * len(outs),
+        out_shape=[jax.ShapeDtypeStruct(shape, dtype) for shape, dtype in outs],
+        cost_estimate=pl.CostEstimate(flops=20 * size, bytes_accessed=16 * size, transcendentals=0),
+        compiler_params=pltpu.CompilerParams(vmem_limit_bytes=KERNEL_VMEM),
+    )(*(array.reshape(1, -1) if array.ndim == 1 else array for array in operands))
+
+
 def swap(array, axis, bit):
     size = lax.axis_size(axis)
     return lax.ppermute(array, axis, [(i, i ^ bit) for i in range(size)])
@@ -69,11 +123,7 @@
     far = swap(block, "tensor", 2)
     other_core = swap(block, "tensor", 1)
     far_core = swap(far, "tensor", 1)
-    rows = block.shape[0]
-    whole = jnp.zeros((4 * rows, block.shape[1]), block.dtype)
-    for i, part in enumerate((block, other_core, far, far_core)):
-        whole = lax.dynamic_update_slice_in_dim(whole, part, i * rows, 0)
-    return lax.optimization_barrier(whole)
+    return jnp.concatenate([block, other_core, far, far_core], axis=0)
 
 
 def scatter_rows(partial):
@@ -82,7 +132,7 @@
     far_sum = (far.astype(F32) + swap(far_core, "tensor", 1).astype(F32)).astype(BF16)
     from_far = swap(far_sum, "tensor", 2)
     from_core = swap(other_core, "tensor", 1)
-    return own.astype(F32) + from_core.astype(F32) + from_far.astype(F32)
+    return own, from_core, from_far
 
 
 class Ring:
@@ -535,23 +585,23 @@
     qkv_bias = jnp.concatenate([query_bias, jnp.zeros_like(query_bias), value_bias])
     qkv_low = (matmul(hidden_full, qkv_full) + qkv_bias).astype(BF16)
     context, log_total = attention(qkv_low, counts, local_width, score_scale)
-    attn_rows = scatter_rows(matmul_nt(context, output_turned).astype(BF16))
-    first_sum = hidden_in.astype(F32) + attn_rows + output_bias
-    first_out, first_normed, first_inverse = norm_forward(first_sum, first_gain, first_shift)
-    normed_full = gather_rows(first_out.astype(BF16))
+    block, column, total = hidden_in.shape, (local_rows, 1), (3, hidden_in.shape[1])
+    attn_parts = scatter_rows(matmul_nt(context, output_turned).astype(BF16))
+    first_out, first_normed, first_inverse, first_low = norm_stage(
+        first_norm_kernel,
+        [hidden_in, *attn_parts, output_bias, first_gain, first_shift],
+        [(block, F32), (block, F32), (column, F32), (block, BF16)],
+    )
+    normed_full = gather_rows(first_low)
     pre_act = matmul(normed_full, up_full) + up_bias
     activated, slope = lax.optimization_barrier((gelu_value(pre_act).astype(BF16), gelu_slope(pre_act)))
-    mlp_rows = scatter_rows(matmul_nt(activated, down_turned).astype(BF16))
-    second_sum = first_out + mlp_rows + down_bias
-    second_out, second_normed, second_inverse = norm_forward(second_sum, second_gain, second_shift)
-    hidden_out = second_out.astype(BF16)
-
-    upstream = cotangent.astype(F32)
-    grad_second_gain = jnp.sum(upstream * second_normed, axis=0)
-    grad_second_shift = jnp.sum(upstream, axis=0)
-    second_grad = norm_backward(upstream, second_gain, second_normed, second_inverse)
-    grad_down_bias = jnp.sum(second_grad, axis=0)
-    second_full = gather_rows(second_grad.astype(BF16))
+    mlp_parts = scatter_rows(matmul_nt(activated, down_turned).astype(BF16))
+    hidden_out, second_grad, second_low, second_sums = norm_stage(
+        second_norm_kernel,
+        [first_out, *mlp_parts, down_bias, second_gain, second_shift, cotangent],
+        [(block, BF16), (block, F32), (block, BF16), (total, F32)],
+    )
+    second_full = gather_rows(second_low)
     pre_grad = matmul(second_full, down_turned) * slope
     grad_up_bias, pre_low = lax.optimization_barrier((jnp.sum(pre_grad, axis=0), pre_grad.astype(BF16)))
     partial = matmul_nt(pre_low, up_full).astype(BF16)
@@ -559,17 +609,15 @@
         [[(normed_full, pre_low)], [(second_full, activated)]],
         ((0, 0, up_weight.shape[1], False), (1, 0, down_weight.shape[0], True)),
     )
-    first_grad_in = second_grad + scatter_rows(partial)
-    grad_first_gain = jnp.sum(first_grad_in * first_normed, axis=0)
-    grad_first_shift = jnp.sum(first_grad_in, axis=0)
-    first_grad = norm_backward(first_grad_in, first_gain, first_normed, first_inverse)
-    grad_output_bias = jnp.sum(first_grad, axis=0)
-    attn_grad_full = gather_rows(first_grad.astype(BF16))
+    first_grad, first_grad_low, first_sums = norm_stage(
+        first_grad_kernel,
+        [second_grad, *scatter_rows(partial), first_gain, first_normed, first_inverse],
+        [(block, F32), (block, BF16), (total, F32)],
+    )
+    attn_grad_full = lax.optimization_barrier(gather_rows(first_grad_low))
     context_grad = matmul(attn_grad_full, output_turned).astype(BF16)
 
-    everywhere = jnp.stack(
-        [grad_second_gain, grad_second_shift, grad_down_bias, grad_first_gain, grad_first_shift, grad_output_bias]
-    )
+    everywhere = jnp.concatenate([second_sums, first_sums], axis=0)
     everywhere = everywhere + swap(everywhere, "tensor", 1)
     everywhere_far = swap(everywhere, "tensor", 2)
 
@@ -583,8 +631,8 @@
     )
     sums = [vector.reshape(-1) for vector in sums]
     back = matmul_nt(low, qkv_full).astype(BF16)
-    back = scatter_rows(back)
-    grad_in = (first_grad + back).astype(BF16)
+    back_parts = scatter_rows(back)
+    grad_in = (first_grad + sum(part.astype(F32) for part in back_parts)).astype(BF16)
     return (
         hidden_out,
         grad_in,

time: 211 us -> 206 us (0.976)
  local copies, waits for them, and re-layouts: 29.2 us -> 25.4 us
  other arithmetic: 6.14 us -> 2.36 us
  starting transfers between devices: 54 us -> 56.7 us
    ppermute x26, waiting for transfers between devices: 26.7 us -> 33.2 us  [swap(): return lax.ppermute(array, axis, [(i, i ^ bit) for i in range(size)])]
    dynamic_update_slice x16 -> x0, local copies, waits for them, and re-layouts: 6.37 us -> none  [gather_rows(): whole = lax.dynamic_update_slice_in_dim(whole, part, i * rows, 0)]
    ppermute x21, waiting for transfers between devices: 34.4 us -> 30.3 us  [step(): going_up = lax.ppermute(going_up, 'dp', self.up)]
    reduce_sum x8 -> x0, other arithmetic: 2.82 us -> none  [the longest x1 0.96 us: layer(): grad_down_bias = jnp.sum(second_grad, axis=0)]
    unnamed x54 -> x41, local copies, waits for them, and re-layouts: 2.42 us -> 4.87 us
    ppermute x21, starting transfers between devices: 15.8 us -> 18.2 us  [step(): going_down = lax.ppermute(going_down, 'dp', self.down)]
  transfers between devices with their start and end apart: 68 -> 68, of which waited for: 30 -> 33; matrix products, arithmetic and copies ran while one was open for 17% -> 15% of each run, Pallas kernels for 11% -> 11%
where the time goes in v3:
time: 206 us
  waiting for transfers between devices  78 us (38%)
  starting transfers between devices  56.7 us (28%)
  Pallas kernels  26 us (13%)
  local copies, waits for them, and re-layouts  25.4 us (12%)
  matrix products  15 us (7%)
  between operations  2.37 us (1%)
  other arithmetic  2.36 us (1%)
    ppermute x26, waiting for transfers between devices, swap(): return lax.ppermute(array, axis, [(i, i ^ bit) for i in range(size)])  33.2 us
    ppermute x21, waiting for transfers between devices, step(): going_up = lax.ppermute(going_up, 'dp', self.up)  30.3 us
    ppermute x21, starting transfers between devices, step(): going_up = lax.ppermute(going_up, 'dp', self.up)  28.9 us
    ppermute x21, starting transfers between devices, step(): going_down = lax.ppermute(going_down, 'dp', self.down)  18.2 us
    dynamic_update_slice x26, local copies, waits for them, and re-layouts, put(): lax.dynamic_update_slice_in_dim(wholes[i], part[low - first:high - first]...  16.8 us
    ppermute x21, waiting for transfers between devices, step(): going_down = lax.ppermute(going_down, 'dp', self.down)  14.5 us
    pallas_call x10, Pallas kernels, ring_sum(): pl.pallas_call(functools.partial(ring_sum_kernel, places, stage, shapes,...  12.8 us
    ppermute x26, starting transfers between devices, swap(): return lax.ppermute(array, axis, [(i, i ^ bit) for i in range(size)])  9.57 us
  transfers between devices with their start and end apart: 68, of which 33 were waited for; matrix products, arithmetic and copies ran while one was open for 15% of the time, Pallas kernels for 11%

profile of v3, /device:TPU:0, one launch (start us, length us, event | category | flops | bytes accessed | tf_op | source)
XLA Modules:
  0.0 205.8 jit_solution(4897976038876390649)
XLA Ops:
  1.3 2.6 %collective-permute-start.1 = (bf16[128,1024]{1,0:T(8,128)(2,1)}, bf16[128,1024]{1,0:T(8,128)(2,1)}, u32[]{:S(2)}, u32[]{:S(2)}) collective-permute-start(bf16[128,1024]{1,0:T(8,128)(2,1)} %refs_0_.1), channel_id=1, source_target_pairs={{0,2},{1,3},{2,0},{3,1},{4,6},{5,7},{6,4},{7,5},{8,10},{9,11},{10,... | collective-permute-start | bytes 786440 | tf_op jit(solution)/shard_map/ppermute | solution.py:119
  9.5 1.8 copy.36
  15.2 1.7 constant_dynamic-update-slice_fusion.29
  19.2 1.6 collective-permute-start.25
  23.4 1.7 constant_dynamic-update-slice_fusion.28
  47.9 3.3 %collective-permute-done.7 = bf16[128,1024]{1,0:T(8,128)(2,1)S(1)} collective-permute-done((bf16[128,1024]{1,0:T(8,128)(2,1)S(1)}, bf16[128,1024]{1,0:T(8,128)(2,1)S(1)}, u32[]{:S(2)}, u32[]{:S(2)}) %collective-permute-start.7) | collective-permute-done | bytes 262176 | tf_op jit(solution)/shard_map/ppermute | solution.py:155
  51.3 1.6 collective-permute-start.9
  54.6 1.6 collective-permute-start.29
  56.3 3.5 %collective-permute-done.9 = bf16[64,1024]{1,0:T(8,128)(2,1)S(1)} collective-permute-done((bf16[64,1024]{1,0:T(8,128)(2,1)S(1)}, bf16[64,1024]{1,0:T(8,128)(2,1)S(1)}, u32[]{:S(2)}, u32[]{:S(2)}) %collective-permute-start.9) | collective-permute-done | bytes 131104 | tf_op jit(solution)/shard_map/ppermute | solution.py:155
  63.5 5.1 %attention.1 = (bf16[512,256]{1,0:T(8,128)(2,1)S(1)}, f32[2,2,512]{2,1,0:T(2,128)S(1)}) custom-call(s32[4]{0:T(128)S(1)} %multiply_subtract_fusion.counts_ref, bf16[512,768]{1,0:T(8,128)(2,1)S(1)} %add_convert_fusion.query_ref.key_ref.value_ref, bf16[512,768]{1,0:T(8,128)(2,1)S(1)} %add_convert_fusion.query_ref.key_ref.value_ref, ...), custom_call_target="tpu_custom_call" | custom-call | flops 268435456 | bytes 1048576 | tf_op jit(solution)/shard_map/attention/pallas_call | solution.py:438
  70.0 1.6 collective-permute-start.23
  78.8 3.7 %collective-permute-done.13.refs_3_ = bf16[128,1024]{1,0:T(8,128)(2,1)S(1)} collective-permute-done((bf16[128,1024]{1,0:T(8,128)(2,1)S(1)}, bf16[128,1024]{1,0:T(8,128)(2,1)S(1)}, u32[]{:S(2)}, u32[]{:S(2)}) %collective-permute-start.13) | collective-permute-done | bytes 262176 | tf_op jit(solution)/shard_map/ppermute | solution.py:119
  85.5 5.3 %collective-permute-done.15 = bf16[128,1024]{1,0:T(8,128)(2,1)S(1)} collective-permute-done((bf16[128,1024]{1,0:T(8,128)(2,1)S(1)}, bf16[128,1024]{1,0:T(8,128)(2,1)S(1)}, u32[]{:S(2)}, u32[]{:S(2)}) %collective-permute-start.15) | collective-permute-done | bytes 262176 | tf_op jit(solution)/shard_map/ppermute | solution.py:119
  92.3 3.4 %fusion.3 = (f32[512,1024]{1,0:T(8,128)S(1)}, bf16[512,1024]{1,0:T(8,128)(2,1)S(1)}) fusion(f32[1024]{0:T(1024)S(1)} %copy-done.14, bf16[512,1024]{1,0:T(8,128)(2,1)S(1)} %constant_dynamic-update-slice_fusion.4.refs_0_, bf16[1024,1024]{1,0:T(8,128)(2,1)} %constant_dynamic-update-slice_fusion.21), kind=kOutput, calls=%fused_computation.4 | convolution fusion | flops 1080033280 | bytes 6295552 | tf_op jit(solution)/shard_map/dot_general | solution.py:25
  95.8 2.9 %convolution_convert_fusion.2 = bf16[512,1024]{1,0:T(8,128)(2,1)S(1)} fusion(bf16[512,1024]{1,0:T(8,128)(2,1)S(1)} %get-tuple-element.77.refs_3_, bf16[1024,1024]{1,0:T(8,128)(2,1)} %constant_dynamic-update-slice_fusion.12), kind=kOutput, calls=%fused_computation.11 | convolution fusion | flops 1074266112 | bytes 4194304 | tf_op jit(solution)/shard_map/dot_general | solution.py:29
  101.0 7.8 %collective-permute-done.35.refs_3_ = bf16[128,1024]{1,0:T(8,128)(2,1)S(1)} collective-permute-done((bf16[128,1024]{1,0:T(8,128)(2,1)S(1)}, bf16[128,1024]{1,0:T(8,128)(2,1)S(1)}, u32[]{:S(2)}, u32[]{:S(2)}) %collective-permute-start.35) | collective-permute-done | bytes 262176 | tf_op jit(solution)/shard_map/ppermute | solution.py:119
  110.5 7.0 %collective-permute-done.37 = bf16[128,1024]{1,0:T(8,128)(2,1)S(1)} collective-permute-done((bf16[128,1024]{1,0:T(8,128)(2,1)S(1)}, bf16[128,1024]{1,0:T(8,128)(2,1)S(1)}, u32[]{:S(2)}, u32[]{:S(2)}) %collective-permute-start.37) | collective-permute-done | bytes 262176 | tf_op jit(solution)/shard_map/ppermute | solution.py:119
  119.1 2.9 %fusion.9 = (bf16[512,1024]{1,0:T(8,128)(2,1)S(1)}, f32[1024]{0:T(1024)S(1)}) fusion(f32[512,1024]{1,0:T(8,128)S(1)} %get-tuple-element.81, bf16[512,1024]{1,0:T(8,128)(2,1)S(1)} %constant_dynamic-update-slice_fusion.8.refs_1_, bf16[1024,1024]{1,0:T(8,128)(2,1)} %constant_dynamic-update-slice_fusion.12), kind=kOutput, calls=%fused_computation.73 | convolution fusion | flops 1075313664 | bytes 6295552 | tf_op jit(solution)/shard_map/dot_general | solution.py:25
  122.0 2.9 %convolution_convert_fusion.1 = bf16[512,1024]{1,0:T(8,128)(2,1)S(1)} fusion(bf16[512,1024]{1,0:T(8,128)(2,1)S(1)} %get-tuple-element.82.refs_2_, bf16[1024,1024]{1,0:T(8,128)(2,1)} %constant_dynamic-update-slice_fusion.21), kind=kOutput, calls=%fused_computation.10 | convolution fusion | flops 1074266112 | bytes 4194304 | tf_op jit(solution)/shard_map/dot_general | solution.py:29
  129.4 5.6 %collective-permute-done.58.refs_4_ = bf16[128,1024]{1,0:T(8,128)(2,1)S(1)} collective-permute-done((bf16[128,1024]{1,0:T(8,128)(2,1)S(1)}, bf16[128,1024]{1,0:T(8,128)(2,1)S(1)}, u32[]{:S(2)}, u32[]{:S(2)}) %collective-permute-start.58) | collective-permute-done | bytes 262176 | tf_op jit(solution)/shard_map/ppermute | solution.py:155
  137.6 1.7 collective-permute-start.60
  141.4 5.4 %collective-permute-done.43 = bf16[128,1024]{1,0:T(8,128)(2,1)S(1)} collective-permute-done((bf16[128,1024]{1,0:T(8,128)(2,1)S(1)}, bf16[128,1024]{1,0:T(8,128)(2,1)S(1)}, u32[]{:S(2)}, u32[]{:S(2)}) %collective-permute-start.43) | collective-permute-done | bytes 262176 | tf_op jit(solution)/shard_map/ppermute | solution.py:119
  147.4 3.0 %collective-permute-done.60.refs_4_ = bf16[256,1024]{1,0:T(8,128)(2,1)S(1)} collective-permute-done((bf16[256,1024]{1,0:T(8,128)(2,1)S(1)}, bf16[256,1024]{1,0:T(8,128)(2,1)S(1)}, u32[]{:S(2)}, u32[]{:S(2)}) %collective-permute-start.60) | collective-permute-done | bytes 524320 | tf_op jit(solution)/shard_map/ppermute | solution.py:155
  155.8 6.2 %attention_grad.1 = (bf16[512,768]{1,0:T(8,128)(2,1)S(1)}, f32[1,256]{1,0:T(1,128)S(1)}, f32[1,256]{1,0:T(1,128)S(1)}) custom-call(s32[4]{0:T(128)S(1)} %multiply_subtract_fusion.counts_ref, bf16[512,768]{1,0:T(8,128)(2,1)S(1)} %add_convert_fusion.query_ref.key_ref.value_ref, bf16[512,768]{1,0:T(8,128)(2,1)S(1)} %add_convert_fusion.query_ref.key_ref.value_ref, ...), custom_call_target="tpu_custom_call" | custom-call | flops 671088640 | bytes 2097152 | tf_op jit(solution)/shard_map/attention_grad/pallas_call | solution.py:524
  166.0 2.4 %collective-permute-done.50.refs_4_ = bf16[80,1024]{1,0:T(8,128)(2,1)S(1)} collective-permute-done((bf16[80,1024]{1,0:T(8,128)(2,1)S(1)}, bf16[80,1024]{1,0:T(8,128)(2,1)S(1)}, u32[]{:S(2)}, u32[]{:S(2)}) %collective-permute-start.50) | collective-permute-done | bytes 163872 | tf_op jit(solution)/shard_map/ppermute | solution.py:155
  175.1 2.7 %collective-permute-done.52.refs_4_ = bf16[144,1024]{1,0:T(8,128)(2,1)S(1)} collective-permute-done((bf16[144,1024]{1,0:T(8,128)(2,1)S(1)}, bf16[144,1024]{1,0:T(8,128)(2,1)S(1)}, u32[]{:S(2)}, u32[]{:S(2)}) %collective-permute-start.52) | collective-permute-done | bytes 294944 | tf_op jit(solution)/shard_map/ppermute | solution.py:155
  184.8 5.0 %collective-permute-done.54.refs_4_ = bf16[144,1024]{1,0:T(8,128)(2,1)S(1)} collective-permute-done((bf16[144,1024]{1,0:T(8,128)(2,1)S(1)}, bf16[144,1024]{1,0:T(8,128)(2,1)S(1)}, u32[]{:S(2)}, u32[]{:S(2)}) %collective-permute-start.54) | collective-permute-done | bytes 294944 | tf_op jit(solution)/shard_map/ppermute | solution.py:155
  191.5 2.6 %collective-permute-done.65.refs_5_ = bf16[128,1024]{1,0:T(8,128)(2,1)S(1)} collective-permute-done((bf16[128,1024]{1,0:T(8,128)(2,1)S(1)}, bf16[128,1024]{1,0:T(8,128)(2,1)S(1)}, u32[]{:S(2)}, u32[]{:S(2)}) %collective-permute-start.65) | collective-permute-done | bytes 262176 | tf_op jit(solution)/shard_map/ppermute | solution.py:156
  196.9 2.1 ring_sum.19
  199.8 1.7 collective-permute-done.56.refs_4_
  201.5 2.4 %collective-permute-done.57.refs_5_ = bf16[144,1024]{1,0:T(8,128)(2,1)S(1)} collective-permute-done((bf16[144,1024]{1,0:T(8,128)(2,1)S(1)}, bf16[144,1024]{1,0:T(8,128)(2,1)S(1)}, u32[]{:S(2)}, u32[]{:S(2)}) %collective-permute-start.57) | collective-permute-done | bytes 294944 | tf_op jit(solution)/shard_map/ppermute | solution.py:156
  203.9 1.7 ring_sum.14
  (227 shorter events, 98.9 us)
Async XLA Ops:
  0.7 17.0 %collective-permute-start = (bf16[128,1024]{1,0:T(8,128)(2,1)}, bf16[128,1024]{1,0:T(8,128)(2,1)}, u32[]{:S(2)}, u32[]{:S(2)}) collective-permute-start(bf16[128,1024]{1,0:T(8,128)(2,1)} %refs_0_.1), channel_id=1, source_target_pairs={{0,1},{1,0},{2,3},{3,2},{4,5},{5,4},{6,7},{7,6},{8,9},{9,8},{10,11... | collective-permute-start | bytes 786440 | tf_op jit(solution)/shard_map/ppermute | solution.py:119
  1.3 17.9 %collective-permute-start.1 = (bf16[128,1024]{1,0:T(8,128)(2,1)}, bf16[128,1024]{1,0:T(8,128)(2,1)}, u32[]{:S(2)}, u32[]{:S(2)}) collective-permute-start(bf16[128,1024]{1,0:T(8,128)(2,1)} %refs_0_.1), channel_id=1, source_target_pairs={{0,2},{1,3},{2,0},{3,1},{4,6},{5,7},{6,4},{7,5},{8,10},{9,11},{10,... | collective-permute-start | bytes 786440 | tf_op jit(solution)/shard_map/ppermute | solution.py:119
  5.8 16.0 %collective-permute-start.3 = (bf16[128,1024]{1,0:T(8,128)(2,1)}, bf16[128,1024]{1,0:T(8,128)(2,1)}, u32[]{:S(2)}, u32[]{:S(2)}) collective-permute-start(bf16[128,1024]{1,0:T(8,128)(2,1)} %get-tuple-element.146), channel_id=1, source_target_pairs={{0,8},{8,16},{16,24},{24,28},{28,20},{20,12},{12,4},{4,0},{1,9},{9... | collective-permute-start | bytes 786440 | tf_op jit(solution)/shard_map/ppermute | solution.py:155
  7.4 17.6 %collective-permute-start.4 = (bf16[128,1024]{1,0:T(8,128)(2,1)}, bf16[128,1024]{1,0:T(8,128)(2,1)}, u32[]{:S(2)}, u32[]{:S(2)}) collective-permute-start(bf16[128,1024]{1,0:T(8,128)(2,1)} %get-tuple-element.146), channel_id=1, source_target_pairs={{8,0},{16,8},{24,16},{28,24},{20,28},{12,20},{4,12},{0,4},{9,1},{1... | collective-permute-start | bytes 786440 | tf_op jit(solution)/shard_map/ppermute | solution.py:156
  7.9 15.4 %collective-permute-start.17 = (bf16[128,1024]{1,0:T(8,128)(2,1)}, bf16[128,1024]{1,0:T(8,128)(2,1)}, u32[]{:S(2)}, u32[]{:S(2)}) collective-permute-start(bf16[128,1024]{1,0:T(8,128)(2,1)} %param.25), channel_id=1, source_target_pairs={{0,8},{8,16},{16,24},{24,28},{28,20},{20,12},{12,4},{4,0},{1,9},{9... | collective-permute-start | bytes 786440 | tf_op jit(solution)/shard_map/ppermute | solution.py:155
  17.7 9.9 %collective-permute-start.18 = (bf16[128,1024]{1,0:T(8,128)(2,1)}, bf16[128,1024]{1,0:T(8,128)(2,1)S(1)}, u32[]{:S(2)}, u32[]{:S(2)}) collective-permute-start(bf16[128,1024]{1,0:T(8,128)(2,1)} %param.25), channel_id=1, source_target_pairs={{8,0},{16,8},{24,16},{28,24},{20,28},{12,20},{4,12},{0,4},{9,1},{1... | collective-permute-start | bytes 786440 | tf_op jit(solution)/shard_map/ppermute | solution.py:156
  21.8 9.8 %collective-permute-start.26 = (bf16[128,1024]{1,0:T(8,128)(2,1)}, bf16[128,1024]{1,0:T(8,128)(2,1)S(1)}, u32[]{:S(2)}, u32[]{:S(2)}) collective-permute-start(bf16[128,1024]{1,0:T(8,128)(2,1)} %bitcast.50), channel_id=1, source_target_pairs={{8,0},{16,8},{24,16},{28,24},{20,28},{12,20},{4,12},{0,4},{9,1},{1... | collective-permute-start | bytes 786440 | tf_op jit(solution)/shard_map/ppermute | solution.py:156
  28.8 11.2 %collective-permute-start.19 = (bf16[128,1024]{1,0:T(8,128)(2,1)}, bf16[128,1024]{1,0:T(8,128)(2,1)S(1)}, u32[]{:S(2)}, u32[]{:S(2)}) collective-permute-start(bf16[128,1024]{1,0:T(8,128)(2,1)} %collective-permute-done.17), channel_id=1, source_target_pairs={{0,8},{8,16},{16,24},{24,28},{28,20},{20,12},{12,4},{4,0},{1,9},{9... | collective-permute-start | bytes 786440 | tf_op jit(solution)/shard_map/ppermute | solution.py:155
  31.6 11.2 %collective-permute-start.20 = (bf16[128,1024]{1,0:T(8,128)(2,1)S(1)}, bf16[128,1024]{1,0:T(8,128)(2,1)S(1)}, u32[]{:S(2)}, u32[]{:S(2)}) collective-permute-start(bf16[128,1024]{1,0:T(8,128)(2,1)S(1)} %collective-permute-done.18), channel_id=1, source_target_pairs={{8,0},{16,8},{24,16},{28,24},{20,28},{12,20},{4,12},{0,4},{9,1},{1... | collective-permute-start | bytes 786440 | tf_op jit(solution)/shard_map/ppermute | solution.py:156
  32.7 12.9 %collective-permute-start.27 = (bf16[128,1024]{1,0:T(8,128)(2,1)S(1)}, bf16[128,1024]{1,0:T(8,128)(2,1)S(1)}, u32[]{:S(2)}, u32[]{:S(2)}) collective-permute-start(bf16[128,1024]{1,0:T(8,128)(2,1)S(1)} %collective-permute-done.25), channel_id=1, source_target_pairs={{0,8},{8,16},{16,24},{24,28},{28,20},{20,12},{12,4},{4,0},{1,9},{9... | collective-permute-start | bytes 786440 | tf_op jit(solution)/shard_map/ppermute | solution.py:155
  34.4 20.2 %collective-permute-start.28 = (bf16[128,1024]{1,0:T(8,128)(2,1)S(1)}, bf16[128,1024]{1,0:T(8,128)(2,1)S(1)}, u32[]{:S(2)}, u32[]{:S(2)}) collective-permute-start(bf16[128,1024]{1,0:T(8,128)(2,1)S(1)} %collective-permute-done.26), channel_id=1, source_target_pairs={{8,0},{16,8},{24,16},{28,24},{20,28},{12,20},{4,12},{0,4},{9,1},{1... | collective-permute-start | bytes 786440 | tf_op jit(solution)/shard_map/ppermute | solution.py:156
  37.2 14.1 %collective-permute-start.7 = (bf16[128,1024]{1,0:T(8,128)(2,1)S(1)}, bf16[128,1024]{1,0:T(8,128)(2,1)S(1)}, u32[]{:S(2)}, u32[]{:S(2)}) collective-permute-start(bf16[128,1024]{1,0:T(8,128)(2,1)S(1)} %collective-permute-done.5), channel_id=1, source_target_pairs={{0,8},{8,16},{16,24},{24,28},{28,20},{20,12},{12,4},{4,0},{1,9},{9... | collective-permute-start | bytes 786440 | tf_op jit(solution)/shard_map/ppermute | solution.py:155
  40.1 14.0 %collective-permute-start.8 = (bf16[128,1024]{1,0:T(8,128)(2,1)S(1)}, bf16[128,1024]{1,0:T(8,128)(2,1)S(1)}, u32[]{:S(2)}, u32[]{:S(2)}) collective-permute-start(bf16[128,1024]{1,0:T(8,128)(2,1)S(1)} %collective-permute-done.6), channel_id=1, source_target_pairs={{8,0},{16,8},{24,16},{28,24},{20,28},{12,20},{4,12},{0,4},{9,1},{1... | collective-permute-start | bytes 786440 | tf_op jit(solution)/shard_map/ppermute | solution.py:156
  42.8 27.2 %collective-permute-start.21 = (bf16[128,1024]{1,0:T(8,128)(2,1)S(1)}, bf16[128,1024]{1,0:T(8,128)(2,1)S(1)}, u32[]{:S(2)}, u32[]{:S(2)}) collective-permute-start(bf16[128,1024]{1,0:T(8,128)(2,1)S(1)} %collective-permute-done.19), channel_id=1, source_target_pairs={{0,8},{8,16},{16,24},{24,28},{28,20},{20,12},{12,4},{4,0},{1,9},{9... | collective-permute-start | bytes 786440 | tf_op jit(solution)/shard_map/ppermute | solution.py:155
  45.7 26.0 %collective-permute-start.22 = (bf16[128,1024]{1,0:T(8,128)(2,1)S(1)}, bf16[128,1024]{1,0:T(8,128)(2,1)S(1)}, u32[]{:S(2)}, u32[]{:S(2)}) collective-permute-start(bf16[128,1024]{1,0:T(8,128)(2,1)S(1)} %collective-permute-done.20), channel_id=1, source_target_pairs={{8,0},{16,8},{24,16},{28,24},{20,28},{12,20},{4,12},{0,4},{9,1},{1... | collective-permute-start | bytes 786440 | tf_op jit(solution)/shard_map/ppermute | solution.py:156
  54.6 19.1 %collective-permute-start.29 = (bf16[128,1024]{1,0:T(8,128)(2,1)S(1)}, bf16[128,1024]{1,0:T(8,128)(2,1)S(1)}, u32[]{:S(2)}, u32[]{:S(2)}) collective-permute-start(bf16[128,1024]{1,0:T(8,128)(2,1)S(1)} %collective-permute-done.27), channel_id=1, source_target_pairs={{0,8},{8,16},{16,24},{24,28},{28,20},{20,12},{12,4},{4,0},{1,9},{9... | collective-permute-start | bytes 786440 | tf_op jit(solution)/shard_map/ppermute | solution.py:155
  59.7 15.3 %collective-permute-start.30 = (bf16[128,1024]{1,0:T(8,128)(2,1)S(1)}, bf16[128,1024]{1,0:T(8,128)(2,1)S(1)}, u32[]{:S(2)}, u32[]{:S(2)}) collective-permute-start(bf16[128,1024]{1,0:T(8,128)(2,1)S(1)} %collective-permute-done.28), channel_id=1, source_target_pairs={{8,0},{16,8},{24,16},{28,24},{20,28},{12,20},{4,12},{0,4},{9,1},{1... | collective-permute-start | bytes 786440 | tf_op jit(solution)/shard_map/ppermute | solution.py:156
  71.6 11.8 %collective-permute-start.24 = (bf16[64,1024]{1,0:T(8,128)(2,1)S(1)}, bf16[64,1024]{1,0:T(8,128)(2,1)S(1)}, u32[]{:S(2)}, u32[]{:S(2)}) collective-permute-start(bf16[64,1024]{1,0:T(8,128)(2,1)S(1)} %slice.105), channel_id=1, source_target_pairs={{8,0},{16,8},{24,16},{28,24},{20,28},{12,20},{4,12},{0,4},{9,1},{1... | collective-permute-start | bytes 393224 | tf_op jit(solution)/shard_map/ppermute | solution.py:156
  125.2 14.5 %collective-permute-start.39 = (bf16[128,1024]{1,0:T(8,128)(2,1)S(1)}, bf16[128,1024]{1,0:T(8,128)(2,1)S(1)}, u32[]{:S(2)}, u32[]{:S(2)}) collective-permute-start(bf16[128,1024]{1,0:T(8,128)(2,1)S(1)} %get-tuple-element.138), channel_id=1, source_target_pairs={{0,1},{1,0},{2,3},{3,2},{4,5},{5,4},{6,7},{7,6},{8,9},{9,8},{10,11... | collective-permute-start | bytes 786440 | tf_op jit(solution)/shard_map/ppermute | solution.py:119
  128.8 10.9 %collective-permute-start.41 = (bf16[128,1024]{1,0:T(8,128)(2,1)S(1)}, bf16[128,1024]{1,0:T(8,128)(2,1)S(1)}, u32[]{:S(2)}, u32[]{:S(2)}) collective-permute-start(bf16[128,1024]{1,0:T(8,128)(2,1)S(1)} %add_convert_fusion.3), channel_id=1, source_target_pairs={{0,2},{1,3},{2,0},{3,1},{4,6},{5,7},{6,4},{7,5},{8,10},{9,11},{10,... | collective-permute-start | bytes 786440 | tf_op jit(solution)/shard_map/ppermute | solution.py:119
  137.6 12.9 %collective-permute-start.60 = (bf16[256,1024]{1,0:T(8,128)(2,1)S(1)}, bf16[256,1024]{1,0:T(8,128)(2,1)S(1)}, u32[]{:S(2)}, u32[]{:S(2)}) collective-permute-start(bf16[256,1024]{1,0:T(8,128)(2,1)S(1)} %get-tuple-element.112), channel_id=1, source_target_pairs={{0,8},{8,16},{16,24},{24,28},{28,20},{20,12},{12,4},{4,0},{1,9},{9... | collective-permute-start | bytes 1572872 | tf_op jit(solution)/shard_map/ppermute | solution.py:155
  139.3 12.5 %collective-permute-start.61 = (bf16[256,1024]{1,0:T(8,128)(2,1)S(1)}, bf16[256,1024]{1,0:T(8,128)(2,1)S(1)}, u32[]{:S(2)}, u32[]{:S(2)}) collective-permute-start(bf16[256,1024]{1,0:T(8,128)(2,1)S(1)} %get-tuple-element.113), channel_id=1, source_target_pairs={{8,0},{16,8},{24,16},{28,24},{20,28},{12,20},{4,12},{0,4},{9,1},{1... | collective-permute-start | bytes 1572872 | tf_op jit(solution)/shard_map/ppermute | solution.py:156
  140.9 14.3 %collective-permute-start.42 = (bf16[128,1024]{1,0:T(8,128)(2,1)S(1)}, bf16[128,1024]{1,0:T(8,128)(2,1)S(1)}, u32[]{:S(2)}, u32[]{:S(2)}) collective-permute-start(bf16[128,1024]{1,0:T(8,128)(2,1)S(1)} %get-tuple-element.86), channel_id=1, source_target_pairs={{0,1},{1,0},{2,3},{3,2},{4,5},{5,4},{6,7},{7,6},{8,9},{9,8},{10,11... | collective-permute-start | bytes 786440 | tf_op jit(solution)/shard_map/ppermute | solution.py:119
  146.9 15.1 %collective-permute-start.49 = (f32[6,1024]{1,0:T(8,128)S(1)}, f32[6,1024]{1,0:T(8,128)S(1)}, u32[]{:S(2)}, u32[]{:S(2)}) collective-permute-start(f32[6,1024]{1,0:T(8,128)S(1)} %fusion.8.refs_4_), channel_id=1, source_target_pairs={{0,2},{1,3},{2,0},{3,1},{4,6},{5,7},{6,4},{7,5},{8,10},{9,11},{10,... | collective-permute-start | bytes 73736 | tf_op jit(solution)/shard_map/ppermute | solution.py:119
  153.2 19.8 %collective-permute-start.62 = (bf16[256,1024]{1,0:T(8,128)(2,1)S(1)}, bf16[256,1024]{1,0:T(8,128)(2,1)S(1)}, u32[]{:S(2)}, u32[]{:S(2)}) collective-permute-start(bf16[256,1024]{1,0:T(8,128)(2,1)S(1)} %get-tuple-element.114), channel_id=1, source_target_pairs={{0,8},{8,16},{16,24},{24,28},{28,20},{20,12},{12,4},{4,0},{1,9},{9... | collective-permute-start | bytes 1572872 | tf_op jit(solution)/shard_map/ppermute | solution.py:155
  154.7 18.3 %collective-permute-start.63 = (bf16[256,1024]{1,0:T(8,128)(2,1)S(1)}, bf16[256,1024]{1,0:T(8,128)(2,1)S(1)}, u32[]{:S(2)}, u32[]{:S(2)}) collective-permute-start(bf16[256,1024]{1,0:T(8,128)(2,1)S(1)} %get-tuple-element.115), channel_id=1, source_target_pairs={{8,0},{16,8},{24,16},{28,24},{20,28},{12,20},{4,12},{0,4},{9,1},{1... | collective-permute-start | bytes 1572872 | tf_op jit(solution)/shard_map/ppermute | solution.py:156
  172.9 9.8 %collective-permute-start.46 = (bf16[128,1024]{1,0:T(8,128)(2,1)S(1)}, bf16[128,1024]{1,0:T(8,128)(2,1)S(1)}, u32[]{:S(2)}, u32[]{:S(2)}) collective-permute-start(bf16[128,1024]{1,0:T(8,128)(2,1)S(1)} %get-tuple-element.136), channel_id=1, source_target_pairs={{0,1},{1,0},{2,3},{3,2},{4,5},{5,4},{6,7},{7,6},{8,9},{9,8},{10,11... | collective-permute-start | bytes 786440 | tf_op jit(solution)/shard_map/ppermute | solution.py:119
  179.4 10.5 %collective-permute-start.54 = (bf16[144,1024]{1,0:T(8,128)(2,1)S(1)}, bf16[144,1024]{1,0:T(8,128)(2,1)S(1)}, u32[]{:S(2)}, u32[]{:S(2)}) collective-permute-start(bf16[144,1024]{1,0:T(8,128)(2,1)S(1)} %get-tuple-element.100), channel_id=1, source_target_pairs={{0,8},{8,16},{16,24},{24,28},{28,20},{20,12},{12,4},{4,0},{1,9},{9... | collective-permute-start | bytes 884744 | tf_op jit(solution)/shard_map/ppermute | solution.py:155
  180.0 9.9 %collective-permute-start.55 = (bf16[144,1024]{1,0:T(8,128)(2,1)S(1)}, bf16[144,1024]{1,0:T(8,128)(2,1)S(1)}, u32[]{:S(2)}, u32[]{:S(2)}) collective-permute-start(bf16[144,1024]{1,0:T(8,128)(2,1)S(1)} %get-tuple-element.101), channel_id=1, source_target_pairs={{8,0},{16,8},{24,16},{28,24},{20,28},{12,20},{4,12},{0,4},{9,1},{1... | collective-permute-start | bytes 884744 | tf_op jit(solution)/shard_map/ppermute | solution.py:156
  181.4 12.6 %collective-permute-start.65 = (bf16[128,1024]{1,0:T(8,128)(2,1)S(1)}, bf16[128,1024]{1,0:T(8,128)(2,1)S(1)}, u32[]{:S(2)}, u32[]{:S(2)}) collective-permute-start(bf16[128,1024]{1,0:T(8,128)(2,1)S(1)} %get-tuple-element.117), channel_id=1, source_target_pairs={{8,0},{16,8},{24,16},{28,24},{20,28},{12,20},{4,12},{0,4},{9,1},{1... | collective-permute-start | bytes 786440 | tf_op jit(solution)/shard_map/ppermute | solution.py:156
  182.7 12.8 %collective-permute-start.66 = (bf16[128,1024]{1,0:T(8,128)(2,1)S(1)}, bf16[128,1024]{1,0:T(8,128)(2,1)S(1)}, u32[]{:S(2)}, u32[]{:S(2)}) collective-permute-start(bf16[128,1024]{1,0:T(8,128)(2,1)S(1)} %get-tuple-element.118), channel_id=1, source_target_pairs={{0,8},{8,16},{16,24},{24,28},{28,20},{20,12},{12,4},{4,0},{1,9},{9... | collective-permute-start | bytes 786440 | tf_op jit(solution)/shard_map/ppermute | solution.py:155
  183.5 13.3 %collective-permute-start.67 = (bf16[128,1024]{1,0:T(8,128)(2,1)S(1)}, bf16[128,1024]{1,0:T(8,128)(2,1)S(1)}, u32[]{:S(2)}, u32[]{:S(2)}) collective-permute-start(bf16[128,1024]{1,0:T(8,128)(2,1)S(1)} %get-tuple-element.119), channel_id=1, source_target_pairs={{8,0},{16,8},{24,16},{28,24},{20,28},{12,20},{4,12},{0,4},{9,1},{1... | collective-permute-start | bytes 786440 | tf_op jit(solution)/shard_map/ppermute | solution.py:156
  (51 other events, 375.5 us)

commit v4 on v3

--- a/solution.py
+++ b/solution.py
@@ -123,12 +123,16 @@
     far = swap(block, "tensor", 2)
     other_core = swap(block, "tensor", 1)
     far_core = swap(far, "tensor", 1)
-    return jnp.concatenate([block, other_core, far, far_core], axis=0)
-
-
-def scatter_rows(partial):
-    rows = partial.shape[0] // 4
-    own, other_core, far, far_core = (partial[i * rows : (i + 1) * rows] for i in range(4))
+    return jnp.concatenate([block, other_core], axis=0), jnp.concatenate([far, far_core], axis=0)
+
+
+def halves(array):
+    return jnp.split(array, 2, axis=0)
+
+
+def scatter_rows(near, distant):
+    own, other_core = halves(near)
+    far, far_core = halves(distant)
     far_sum = (far.astype(F32) + swap(far_core, "tensor", 1).astype(F32)).astype(BF16)
     from_far = swap(far_sum, "tensor", 2)
     from_core = swap(other_core, "tensor", 1)
@@ -198,8 +202,8 @@
         if not self.small:
             owned = []
             for row in layout:
-                for left, right in row:
-                    whole = matmul_tn(left, right).astype(BF16)
+                for lefts, rights in row:
+                    whole = sum(matmul_tn(left, right) for left, right in zip(lefts, rights)).astype(BF16)
                     owned.append(lax.psum_scatter(whole, "dp", scatter_dimension=0, tiled=True).astype(F32))
             outs = []
             for term, start, stop, turned in shapes:
@@ -237,29 +241,26 @@
 VECTOR_ROWS = 8
 
 
-def split_low(value):
-    high = value.astype(BF16)
-    return high, (value - high.astype(F32)).astype(BF16)
-
-
-def ring_sum_kernel(places, stage, shapes, has_vectors, owners_ref, *refs):
-    count = len(places)
-    lefts, rights, rest = refs[:count], refs[count : 2 * count], refs[2 * count :]
+def ring_sum_kernel(places, counts, stage, shapes, has_vectors, owners_ref, *refs):
+    pairs, used = [], 0
+    for count in counts:
+        pairs.append((refs[used : used + count], refs[used + count : used + 2 * count]))
+        used += 2 * count
+    rest = refs[used:]
     rows = places[0][2]
     total = max(place[0] for place in places) + rows
     half = total // 2
-    extra = 2 * VECTOR_ROWS if has_vectors else 0
+    extra = VECTOR_ROWS if has_vectors else 0
 
     def term(i, direction):
-        start = pl.multiple_of(owners_ref[direction] * rows, rows)
-        return matmul_tn(lefts[i][:, pl.ds(start, rows)], rights[i][...])
+        columns = pl.ds(pl.multiple_of(owners_ref[direction] * rows, rows), rows)
+        products = [matmul_tn(left[:, columns], right[...]) for left, right in zip(*pairs[i])]
+        return sum(products[1:], products[0])
 
     by_row = stage != FIRST and not has_vectors and len(rest) == (4 + len(shapes) if stage == LAST else 6)
 
     def vectors_in(ref):
-        first = ref.shape[0] - extra
-        high = ref[first : first + VECTOR_ROWS].astype(F32)
-        return high + ref[first + VECTOR_ROWS : first + extra].astype(F32)
+        return ref[ref.shape[0] - extra :].astype(F32)
 
     if has_vectors and stage == FIRST:
         partial_ref, other_ref, *single_refs = rest[:5]
@@ -274,11 +275,8 @@
                 row, column = row + 1, 0
             sum_ref[row : row + 1, column : column + width] = ref[...]
             column += width
-        high, low = split_low(sum_ref[...])
         for target in rest[:2]:
-            first = target.shape[0] - extra
-            target[first : first + VECTOR_ROWS] = high
-            target[first + VECTOR_ROWS : first + extra] = low
+            target[target.shape[0] - extra :] = sum_ref[...].astype(BF16)
     elif has_vectors and stage == STEP:
         rest[5][...] = rest[2][...] + vectors_in(rest[0]) + vectors_in(rest[1])
         for arrived, target in zip(rest[:2], rest[3:5]):
@@ -339,18 +337,19 @@
 
 def ring_sum(layout, owners, arrived, stage, shapes, vectors, apart=False):
     size = lax.axis_size("dp")
-    places, lefts, rights, row = [], [], [], 0
+    places, counts, operands, row = [], [], [], 0
     for terms in layout:
         column = 0
-        for left, right in terms:
-            rows = left.shape[1] // size
-            places.append((row, column, rows, right.shape[1]))
-            lefts.append(left)
-            rights.append(right)
-            column += right.shape[1]
+        for lefts, rights in terms:
+            rows, width = lefts[0].shape[1] // size, rights[0].shape[1]
+            places.append((row, column, rows, width))
+            counts.append(len(lefts))
+            operands += [*lefts, *rights]
+            column += width
         row += rows
-    extra = 2 * VECTOR_ROWS if vectors else 0
-    operands = [*lefts, *rights, *arrived]
+    extra = VECTOR_ROWS if vectors else 0
+    depth = sum(array.shape[0] for array in layout[0][0][0])
+    operands += arrived
     out_shape = []
     if stage == LAST:
         for term, start, stop, turned in shapes:
@@ -370,12 +369,12 @@
             operands += vectors
     vmem = pl.BlockSpec(memory_space=pltpu.VMEM)
     return pl.pallas_call(
-        functools.partial(ring_sum_kernel, places, stage, shapes, bool(vectors)),
+        functools.partial(ring_sum_kernel, places, counts, stage, shapes, bool(vectors)),
         in_specs=[pl.BlockSpec(memory_space=pltpu.SMEM)] + [vmem] * len(operands),
         out_specs=[vmem] * len(out_shape),
         out_shape=out_shape,
         cost_estimate=pl.CostEstimate(
-            flops=4 * row * column * lefts[0].shape[0],
+            flops=4 * row * column * depth,
             bytes_accessed=12 * row * column,
             transcendentals=0,
         ),
@@ -576,7 +575,7 @@
 
     packed = row_major(jnp.concatenate([query_weight, key_weight, value_weight, output_weight.T], axis=1))
     (packed_full,) = ring.gather(packed, (packed.shape[0],))
-    hidden_full = gather_rows(hidden_in)
+    hidden_full = jnp.concatenate(gather_rows(hidden_in), axis=0)
     (up_full,) = ring.gather(up_weight, (up_weight.shape[0],))
     (down_turned,) = ring.gather(row_major(down_weight.T), (down_weight.shape[1],))
     qkv_full = packed_full[:, : 3 * local_width]
@@ -586,35 +585,41 @@
     qkv_low = (matmul(hidden_full, qkv_full) + qkv_bias).astype(BF16)
     context, log_total = attention(qkv_low, counts, local_width, score_scale)
     block, column, total = hidden_in.shape, (local_rows, 1), (3, hidden_in.shape[1])
-    attn_parts = scatter_rows(matmul_nt(context, output_turned).astype(BF16))
+    attn_parts = scatter_rows(*halves(matmul_nt(context, output_turned).astype(BF16)))
     first_out, first_normed, first_inverse, first_low = norm_stage(
         first_norm_kernel,
         [hidden_in, *attn_parts, output_bias, first_gain, first_shift],
         [(block, F32), (block, F32), (column, F32), (block, BF16)],
     )
-    normed_full = gather_rows(first_low)
-    pre_act = matmul(normed_full, up_full) + up_bias
-    activated, slope = lax.optimization_barrier((gelu_value(pre_act).astype(BF16), gelu_slope(pre_act)))
-    mlp_parts = scatter_rows(matmul_nt(activated, down_turned).astype(BF16))
+    normed = gather_rows(first_low)
+    activated, slope, mlp = [None] * 2, [None] * 2, [None] * 2
+    for i in (1, 0):
+        pre_act = matmul(normed[i], up_full) + up_bias
+        activated[i], slope[i] = lax.optimization_barrier((gelu_value(pre_act).astype(BF16), gelu_slope(pre_act)))
+        mlp[i] = matmul_nt(activated[i], down_turned).astype(BF16)
+    mlp_parts = scatter_rows(*mlp)
     hidden_out, second_grad, second_low, second_sums = norm_stage(
         second_norm_kernel,
         [first_out, *mlp_parts, down_bias, second_gain, second_shift, cotangent],
         [(block, BF16), (block, F32), (block, BF16), (total, F32)],
     )
-    second_full = gather_rows(second_low)
-    pre_grad = matmul(second_full, down_turned) * slope
-    grad_up_bias, pre_low = lax.optimization_barrier((jnp.sum(pre_grad, axis=0), pre_grad.astype(BF16)))
-    partial = matmul_nt(pre_low, up_full).astype(BF16)
+    second = gather_rows(second_low)
+    pre_low, up_sums, partial = [None] * 2, [None] * 2, [None] * 2
+    for i in (0, 1):
+        pre_grad = matmul(second[i], down_turned) * slope[i]
+        up_sums[i], pre_low[i] = lax.optimization_barrier((jnp.sum(pre_grad, axis=0), pre_grad.astype(BF16)))
+        partial[i] = matmul_nt(pre_low[i], up_full).astype(BF16)
+    grad_up_bias = up_sums[0] + up_sums[1]
     up_owned, down_owned = ring.scatter(
-        [[(normed_full, pre_low)], [(second_full, activated)]],
+        [[(normed, pre_low)], [(second, activated)]],
         ((0, 0, up_weight.shape[1], False), (1, 0, down_weight.shape[0], True)),
     )
     first_grad, first_grad_low, first_sums = norm_stage(
         first_grad_kernel,
-        [second_grad, *scatter_rows(partial), first_gain, first_normed, first_inverse],
+        [second_grad, *scatter_rows(*partial), first_gain, first_normed, first_inverse],
         [(block, F32), (block, BF16), (total, F32)],
     )
-    attn_grad_full = lax.optimization_barrier(gather_rows(first_grad_low))
+    attn_grad_full = lax.optimization_barrier(jnp.concatenate(gather_rows(first_grad_low), axis=0))
     context_grad = matmul(attn_grad_full, output_turned).astype(BF16)
 
     everywhere = jnp.concatenate([second_sums, first_sums], axis=0)
@@ -625,13 +630,13 @@
         qkv_low, context_grad, log_total, counts, local_width, score_scale
     )
     query_owned, key_owned, value_owned, output_owned, *sums = ring.scatter(
-        [[(hidden_full, low), (attn_grad_full, context)]],
+        [[((hidden_full,), (low,)), ((attn_grad_full,), (context,))]],
         tuple((0, i * local_width, (i + 1) * local_width, False) for i in range(3)) + ((1, 0, local_width, True),),
         (everywhere, everywhere_far, grad_up_bias.reshape(1, -1), query_sum, value_sum),
     )
     sums = [vector.reshape(-1) for vector in sums]
     back = matmul_nt(low, qkv_full).astype(BF16)
-    back_parts = scatter_rows(back)
+    back_parts = scatter_rows(*halves(back))
     grad_in = (first_grad + sum(part.astype(F32) for part in back_parts)).astype(BF16)
     return (
         hidden_out,

time: 206 us -> 203 us (0.985)
  local copies, waits for them, and re-layouts: 25.4 us -> 20.1 us
  waiting for transfers between devices: 78 us -> 81.7 us
  starting transfers between devices: 56.7 us -> 54 us
    ppermute x21, waiting for transfers between devices: 14.5 us -> 23.9 us  [step(): going_down = lax.ppermute(going_down, 'dp', self.down)]
    ppermute x21, waiting for transfers between devices: 30.3 us -> 23.4 us  [step(): going_up = lax.ppermute(going_up, 'dp', self.up)]
    dynamic_update_slice x26, local copies, waits for them, and re-layouts: 16.8 us -> 12.1 us  [put(): lax.dynamic_update_slice_in_dim(wholes[i], part[low - first:high - first]...]
    ppermute x21, starting transfers between devices: 18.2 us -> 15 us  [step(): going_down = lax.ppermute(going_down, 'dp', self.down)]
    unnamed x41 -> x43, local copies, waits for them, and re-layouts: 4.87 us -> 5.61 us
    dot_general x4 -> x6, matrix products: 7.75 us -> 8.37 us  [matmul(): return jnp.dot(left_side, right_side, preferred_element_type=F32)]
    dot_general x4 -> x6, matrix products: 7.26 us -> 7.75 us  [matmul_nt(): lax.dot_general(left_side, right_side, (((1,), (1,)), ((), ())), preferre...]
  transfers between devices with their start and end apart: 68 -> 68, of which waited for: 33 -> 31; matrix products, arithmetic and copies ran while one was open for 15% -> 14% of each run, Pallas kernels for 11% -> 11%
where the time goes in v4:
time: 203 us
  waiting for transfers between devices  81.7 us (40%)
  starting transfers between devices  54 us (27%)
  Pallas kernels  26 us (13%)
  local copies, waits for them, and re-layouts  20.1 us (10%)
  matrix products  16.1 us (8%)
  between operations  2.58 us (1%)
  other arithmetic  2.38 us (1%)
    ppermute x26, waiting for transfers between devices, swap(): return lax.ppermute(array, axis, [(i, i ^ bit) for i in range(size)])  34.4 us
    ppermute x21, starting transfers between devices, step(): going_up = lax.ppermute(going_up, 'dp', self.up)  30 us
    ppermute x21, waiting for transfers between devices, step(): going_down = lax.ppermute(going_down, 'dp', self.down)  23.9 us
    ppermute x21, waiting for transfers between devices, step(): going_up = lax.ppermute(going_up, 'dp', self.up)  23.4 us
    ppermute x21, starting transfers between devices, step(): going_down = lax.ppermute(going_down, 'dp', self.down)  15 us
    pallas_call x10, Pallas kernels, ring_sum(): pl.pallas_call(functools.partial(ring_sum_kernel, places, counts, stage,...  12.8 us
    dynamic_update_slice x26, local copies, waits for them, and re-layouts, put(): lax.dynamic_update_slice_in_dim(wholes[i], part[low - first:high - first]...  12.1 us
    ppermute x26, starting transfers between devices, swap(): return lax.ppermute(array, axis, [(i, i ^ bit) for i in range(size)])  9.09 us
  transfers between devices with their start and end apart: 68, of which 31 were waited for; matrix products, arithmetic and copies ran while one was open for 14% of the time, Pallas kernels for 11%

profile of v4, /device:TPU:0, one launch (start us, length us, event | category | flops | bytes accessed | tf_op | source)
XLA Modules:
  0.0 202.9 jit_solution(9098041727379020075)
XLA Ops:
  2.8 3.1 %collective-permute-start.3 = (bf16[128,1024]{1,0:T(8,128)(2,1)}, bf16[128,1024]{1,0:T(8,128)(2,1)}, u32[]{:S(2)}, u32[]{:S(2)}) collective-permute-start(bf16[128,1024]{1,0:T(8,128)(2,1)} %get-tuple-element.156), channel_id=1, source_target_pairs={{0,8},{8,16},{16,24},{24,28},{28,20},{20,12},{12,4},{4,0},{1,9},{9... | collective-permute-start | bytes 786440 | tf_op jit(solution)/shard_map/ppermute | solution.py:159
  5.9 2.0 collective-permute-start.1
  9.5 1.8 copy.36
  13.8 1.7 constant_dynamic-update-slice_fusion.29
  21.0 1.7 constant_dynamic-update-slice_fusion.37
  24.2 1.7 constant_dynamic-update-slice_fusion.36
  26.3 1.8 constant_dynamic-update-slice_fusion.28
  34.1 2.9 %collective-permute-done.6 = bf16[128,1024]{1,0:T(8,128)(2,1)S(1)} collective-permute-done((bf16[128,1024]{1,0:T(8,128)(2,1)}, bf16[128,1024]{1,0:T(8,128)(2,1)S(1)}, u32[]{:S(2)}, u32[]{:S(2)}) %collective-permute-start.6) | collective-permute-done | bytes 262176 | tf_op jit(solution)/shard_map/ppermute | solution.py:160
  40.4 2.3 %collective-permute-done.18 = bf16[128,1024]{1,0:T(8,128)(2,1)S(1)} collective-permute-done((bf16[128,1024]{1,0:T(8,128)(2,1)S(1)}, bf16[128,1024]{1,0:T(8,128)(2,1)S(1)}, u32[]{:S(2)}, u32[]{:S(2)}) %collective-permute-start.18) | collective-permute-done | bytes 262176 | tf_op jit(solution)/shard_map/ppermute | solution.py:160
  45.5 2.8 %collective-permute-done.26 = bf16[128,1024]{1,0:T(8,128)(2,1)S(1)} collective-permute-done((bf16[128,1024]{1,0:T(8,128)(2,1)S(1)}, bf16[128,1024]{1,0:T(8,128)(2,1)S(1)}, u32[]{:S(2)}, u32[]{:S(2)}) %collective-permute-start.26) | collective-permute-done | bytes 262176 | tf_op jit(solution)/shard_map/ppermute | solution.py:160
  51.6 2.3 %collective-permute-done.8 = bf16[128,1024]{1,0:T(8,128)(2,1)S(1)} collective-permute-done((bf16[128,1024]{1,0:T(8,128)(2,1)S(1)}, bf16[128,1024]{1,0:T(8,128)(2,1)S(1)}, u32[]{:S(2)}, u32[]{:S(2)}) %collective-permute-start.8) | collective-permute-done | bytes 262176 | tf_op jit(solution)/shard_map/ppermute | solution.py:160
  56.5 3.0 %collective-permute-done.20 = bf16[128,1024]{1,0:T(8,128)(2,1)S(1)} collective-permute-done((bf16[128,1024]{1,0:T(8,128)(2,1)S(1)}, bf16[128,1024]{1,0:T(8,128)(2,1)S(1)}, u32[]{:S(2)}, u32[]{:S(2)}) %collective-permute-start.20) | collective-permute-done | bytes 262176 | tf_op jit(solution)/shard_map/ppermute | solution.py:160
  66.2 5.1 %attention.1 = (bf16[512,256]{1,0:T(8,128)(2,1)S(1)}, f32[2,2,512]{2,1,0:T(2,128)S(1)}) custom-call(s32[4]{0:T(128)S(1)} %multiply_subtract_fusion.counts_ref, bf16[512,768]{1,0:T(8,128)(2,1)S(1)} %add_convert_fusion.query_ref.key_ref.value_ref, bf16[512,768]{1,0:T(8,128)(2,1)S(1)} %add_convert_fusion.query_ref.key_ref.value_ref, ...), custom_call_target="tpu_custom_call" | custom-call | flops 268435456 | bytes 1048576 | tf_op jit(solution)/shard_map/attention/pallas_call | solution.py:437
  76.4 6.1 %collective-permute-done.13.refs_3_ = bf16[128,1024]{1,0:T(8,128)(2,1)S(1)} collective-permute-done((bf16[128,1024]{1,0:T(8,128)(2,1)S(1)}, bf16[128,1024]{1,0:T(8,128)(2,1)S(1)}, u32[]{:S(2)}, u32[]{:S(2)}) %collective-permute-start.13) | collective-permute-done | bytes 262176 | tf_op jit(solution)/shard_map/ppermute | solution.py:119
  83.5 6.8 %collective-permute-done.32 = bf16[128,1024]{1,0:T(8,128)(2,1)S(1)} collective-permute-done((bf16[128,1024]{1,0:T(8,128)(2,1)S(1)}, bf16[128,1024]{1,0:T(8,128)(2,1)S(1)}, u32[]{:S(2)}, u32[]{:S(2)}) %collective-permute-start.32) | collective-permute-done | bytes 262176 | tf_op jit(solution)/shard_map/ppermute | solution.py:119
  90.3 2.7 %fusion.5 = (f32[256,1024]{1,0:T(8,128)S(1)}, bf16[256,1024]{1,0:T(8,128)(2,1)S(1)}) fusion(f32[1024]{0:T(1024)S(1)} %copy-done.16, bf16[256,1024]{1,0:T(8,128)(2,1)S(1)} %constant_dynamic-update-slice_fusion.4.refs_0_, bf16[1024,1024]{1,0:T(8,128)(2,1)} %constant_dynamic-update-slice_fusion.21), kind=kOutput, calls=%fused_computation.19 | convolution fusion | flops 540016640 | bytes 4198400 | tf_op jit(solution)/shard_map/dot_general | solution.py:25
  93.1 2.7 %fusion.9 = (f32[256,1024]{1,0:T(8,128)S(1)}, bf16[256,1024]{1,0:T(8,128)(2,1)S(1)}) fusion(f32[1024]{0:T(1024)S(1)} %copy-done.16, bf16[256,1024]{1,0:T(8,128)(2,1)S(1)} %constant_dynamic-update-slice_fusion.6.refs_1_, bf16[1024,1024]{1,0:T(8,128)(2,1)} %constant_dynamic-update-slice_fusion.21), kind=kOutput, calls=%fused_computation.23 | convolution fusion | flops 540016640 | bytes 4198400 | tf_op jit(solution)/shard_map/dot_general | solution.py:25
  99.6 7.5 %collective-permute-done.35.refs_3_ = bf16[128,1024]{1,0:T(8,128)(2,1)S(1)} collective-permute-done((bf16[128,1024]{1,0:T(8,128)(2,1)S(1)}, bf16[128,1024]{1,0:T(8,128)(2,1)S(1)}, u32[]{:S(2)}, u32[]{:S(2)}) %collective-permute-start.35) | collective-permute-done | bytes 262176 | tf_op jit(solution)/shard_map/ppermute | solution.py:119
  110.6 6.5 %collective-permute-done.38 = bf16[128,1024]{1,0:T(8,128)(2,1)S(1)} collective-permute-done((bf16[128,1024]{1,0:T(8,128)(2,1)S(1)}, bf16[128,1024]{1,0:T(8,128)(2,1)S(1)}, u32[]{:S(2)}, u32[]{:S(2)}) %collective-permute-start.38) | collective-permute-done | bytes 262176 | tf_op jit(solution)/shard_map/ppermute | solution.py:119
  117.1 2.4 %convolution_convert_fusion.3 = bf16[256,1024]{1,0:T(8,128)(2,1)S(1)} fusion(bf16[256,1024]{1,0:T(8,128)(2,1)S(1)} %get-tuple-element.87.refs_2_, bf16[1024,1024]{1,0:T(8,128)(2,1)} %constant_dynamic-update-slice_fusion.21), kind=kOutput, calls=%fused_computation.12 | convolution fusion | flops 537133056 | bytes 3145728 | tf_op jit(solution)/shard_map/dot_general | solution.py:29
  120.3 2.4 %convolution_convert_fusion.2 = bf16[256,1024]{1,0:T(8,128)(2,1)S(1)} fusion(bf16[256,1024]{1,0:T(8,128)(2,1)S(1)} %get-tuple-element.89.refs_3_, bf16[1024,1024]{1,0:T(8,128)(2,1)} %constant_dynamic-update-slice_fusion.21), kind=kOutput, calls=%fused_computation.11 | convolution fusion | flops 537133056 | bytes 3145728 | tf_op jit(solution)/shard_map/dot_general | solution.py:29
  127.3 6.0 %collective-permute-done.58.refs_8_ = bf16[128,1024]{1,0:T(8,128)(2,1)S(1)} collective-permute-done((bf16[128,1024]{1,0:T(8,128)(2,1)S(1)}, bf16[128,1024]{1,0:T(8,128)(2,1)S(1)}, u32[]{:S(2)}, u32[]{:S(2)}) %collective-permute-start.58) | collective-permute-done | bytes 262176 | tf_op jit(solution)/shard_map/ppermute | solution.py:159
  139.7 5.7 %collective-permute-done.43 = bf16[128,1024]{1,0:T(8,128)(2,1)S(1)} collective-permute-done((bf16[128,1024]{1,0:T(8,128)(2,1)S(1)}, bf16[128,1024]{1,0:T(8,128)(2,1)S(1)}, u32[]{:S(2)}, u32[]{:S(2)}) %collective-permute-start.43) | collective-permute-done | bytes 262176 | tf_op jit(solution)/shard_map/ppermute | solution.py:119
  146.1 3.0 %collective-permute-done.60.refs_8_ = bf16[256,1024]{1,0:T(8,128)(2,1)S(1)} collective-permute-done((bf16[256,1024]{1,0:T(8,128)(2,1)S(1)}, bf16[256,1024]{1,0:T(8,128)(2,1)S(1)}, u32[]{:S(2)}, u32[]{:S(2)}) %collective-permute-start.60) | collective-permute-done | bytes 524320 | tf_op jit(solution)/shard_map/ppermute | solution.py:159
  154.2 6.2 %attention_grad.1 = (bf16[512,768]{1,0:T(8,128)(2,1)S(1)}, f32[1,256]{1,0:T(1,128)S(1)}, f32[1,256]{1,0:T(1,128)S(1)}) custom-call(s32[4]{0:T(128)S(1)} %multiply_subtract_fusion.counts_ref, bf16[512,768]{1,0:T(8,128)(2,1)S(1)} %add_convert_fusion.query_ref.key_ref.value_ref, bf16[512,768]{1,0:T(8,128)(2,1)S(1)} %add_convert_fusion.query_ref.key_ref.value_ref, ...), custom_call_target="tpu_custom_call" | custom-call | flops 671088640 | bytes 2097152 | tf_op jit(solution)/shard_map/attention_grad/pallas_call | solution.py:523
  164.4 2.4 %collective-permute-done.50.refs_4_ = bf16[72,1024]{1,0:T(8,128)(2,1)S(1)} collective-permute-done((bf16[72,1024]{1,0:T(8,128)(2,1)S(1)}, bf16[72,1024]{1,0:T(8,128)(2,1)S(1)}, u32[]{:S(2)}, u32[]{:S(2)}) %collective-permute-start.50) | collective-permute-done | bytes 147488 | tf_op jit(solution)/shard_map/ppermute | solution.py:159
  173.3 2.4 %collective-permute-done.52.refs_4_ = bf16[136,1024]{1,0:T(8,128)(2,1)S(1)} collective-permute-done((bf16[136,1024]{1,0:T(8,128)(2,1)S(1)}, bf16[136,1024]{1,0:T(8,128)(2,1)S(1)}, u32[]{:S(2)}, u32[]{:S(2)}) %collective-permute-start.52) | collective-permute-done | bytes 278560 | tf_op jit(solution)/shard_map/ppermute | solution.py:159
  182.9 4.9 %collective-permute-done.54.refs_4_ = bf16[136,1024]{1,0:T(8,128)(2,1)S(1)} collective-permute-done((bf16[136,1024]{1,0:T(8,128)(2,1)S(1)}, bf16[136,1024]{1,0:T(8,128)(2,1)S(1)}, u32[]{:S(2)}, u32[]{:S(2)}) %collective-permute-start.54) | collective-permute-done | bytes 278560 | tf_op jit(solution)/shard_map/ppermute | solution.py:159
  189.4 2.5 %collective-permute-done.65.refs_9_ = bf16[128,1024]{1,0:T(8,128)(2,1)S(1)} collective-permute-done((bf16[128,1024]{1,0:T(8,128)(2,1)S(1)}, bf16[128,1024]{1,0:T(8,128)(2,1)S(1)}, u32[]{:S(2)}, u32[]{:S(2)}) %collective-permute-start.65) | collective-permute-done | bytes 262176 | tf_op jit(solution)/shard_map/ppermute | solution.py:160
  194.7 2.1 %ring_sum.19 = (f32[128,1024]{1,0:T(8,128)}, f32[1024,128]{1,0:T(8,128)}) custom-call(s32[2]{0:T(128)S(1)} %pad_add_fusion.owners_ref, bf16[256,1024]{1,0:T(8,128)(2,1)S(1)} %constant_dynamic-update-slice_fusion.4.refs_0_, bf16[256,1024]{1,0:T(8,128)(2,1)S(1)} %constant_dynamic-update-slice_fusion.6.refs_1_, ...), custom_call_target="tpu_custom_call" | custom-call | flops 536870912 | bytes 3145728 | tf_op jit(solution)/shard_map/ring_sum/pallas_call | solution.py:371
  198.9 2.2 %collective-permute-done.57.refs_5_ = bf16[136,1024]{1,0:T(8,128)(2,1)S(1)} collective-permute-done((bf16[136,1024]{1,0:T(8,128)(2,1)S(1)}, bf16[136,1024]{1,0:T(8,128)(2,1)S(1)}, u32[]{:S(2)}, u32[]{:S(2)}) %collective-permute-start.57) | collective-permute-done | bytes 278560 | tf_op jit(solution)/shard_map/ppermute | solution.py:160
  201.1 1.7 ring_sum.14
  (238 shorter events, 92.1 us)
Async XLA Ops:
  2.8 17.6 %collective-permute-start.3 = (bf16[128,1024]{1,0:T(8,128)(2,1)}, bf16[128,1024]{1,0:T(8,128)(2,1)}, u32[]{:S(2)}, u32[]{:S(2)}) collective-permute-start(bf16[128,1024]{1,0:T(8,128)(2,1)} %get-tuple-element.156), channel_id=1, source_target_pairs={{0,8},{8,16},{16,24},{24,28},{28,20},{20,12},{12,4},{4,0},{1,9},{9... | collective-permute-start | bytes 786440 | tf_op jit(solution)/shard_map/ppermute | solution.py:159
  5.9 16.8 %collective-permute-start.4 = (bf16[128,1024]{1,0:T(8,128)(2,1)}, bf16[128,1024]{1,0:T(8,128)(2,1)}, u32[]{:S(2)}, u32[]{:S(2)}) collective-permute-start(bf16[128,1024]{1,0:T(8,128)(2,1)} %get-tuple-element.156), channel_id=1, source_target_pairs={{8,0},{16,8},{24,16},{28,24},{20,28},{12,20},{4,12},{0,4},{9,1},{1... | collective-permute-start | bytes 786440 | tf_op jit(solution)/shard_map/ppermute | solution.py:160
  5.9 12.0 %collective-permute-start.1 = (bf16[128,1024]{1,0:T(8,128)(2,1)S(1)}, bf16[128,1024]{1,0:T(8,128)(2,1)}, u32[]{:S(2)}, u32[]{:S(2)}) collective-permute-start(bf16[128,1024]{1,0:T(8,128)(2,1)S(1)} %copy-done), channel_id=1, source_target_pairs={{0,2},{1,3},{2,0},{3,1},{4,6},{5,7},{6,4},{7,5},{8,10},{9,11},{10,... | collective-permute-start | bytes 786440 | tf_op jit(solution)/shard_map/ppermute | solution.py:119
  7.9 18.0 %collective-permute-start.15 = (bf16[128,1024]{1,0:T(8,128)(2,1)}, bf16[128,1024]{1,0:T(8,128)(2,1)}, u32[]{:S(2)}, u32[]{:S(2)}) collective-permute-start(bf16[128,1024]{1,0:T(8,128)(2,1)} %param.25), channel_id=1, source_target_pairs={{0,8},{8,16},{16,24},{24,28},{28,20},{20,12},{12,4},{4,0},{1,9},{9... | collective-permute-start | bytes 786440 | tf_op jit(solution)/shard_map/ppermute | solution.py:159
  16.4 11.8 %collective-permute-start.16 = (bf16[128,1024]{1,0:T(8,128)(2,1)}, bf16[128,1024]{1,0:T(8,128)(2,1)S(1)}, u32[]{:S(2)}, u32[]{:S(2)}) collective-permute-start(bf16[128,1024]{1,0:T(8,128)(2,1)} %param.25), channel_id=1, source_target_pairs={{8,0},{16,8},{24,16},{28,24},{20,28},{12,20},{4,12},{0,4},{9,1},{1... | collective-permute-start | bytes 786440 | tf_op jit(solution)/shard_map/ppermute | solution.py:160
  17.9 11.0 %collective-permute-start.23 = (bf16[128,1024]{1,0:T(8,128)(2,1)}, bf16[128,1024]{1,0:T(8,128)(2,1)S(1)}, u32[]{:S(2)}, u32[]{:S(2)}) collective-permute-start(bf16[128,1024]{1,0:T(8,128)(2,1)} %bitcast.57), channel_id=1, source_target_pairs={{0,8},{8,16},{16,24},{24,28},{28,20},{20,12},{12,4},{4,0},{1,9},{9... | collective-permute-start | bytes 786440 | tf_op jit(solution)/shard_map/ppermute | solution.py:159
  25.9 11.2 %collective-permute-start.6 = (bf16[128,1024]{1,0:T(8,128)(2,1)}, bf16[128,1024]{1,0:T(8,128)(2,1)S(1)}, u32[]{:S(2)}, u32[]{:S(2)}) collective-permute-start(bf16[128,1024]{1,0:T(8,128)(2,1)} %collective-permute-done.4), channel_id=1, source_target_pairs={{8,0},{16,8},{24,16},{28,24},{20,28},{12,20},{4,12},{0,4},{9,1},{1... | collective-permute-start | bytes 786440 | tf_op jit(solution)/shard_map/ppermute | solution.py:160
  31.5 11.2 %collective-permute-start.18 = (bf16[128,1024]{1,0:T(8,128)(2,1)S(1)}, bf16[128,1024]{1,0:T(8,128)(2,1)S(1)}, u32[]{:S(2)}, u32[]{:S(2)}) collective-permute-start(bf16[128,1024]{1,0:T(8,128)(2,1)S(1)} %collective-permute-done.16), channel_id=1, source_target_pairs={{8,0},{16,8},{24,16},{28,24},{20,28},{12,20},{4,12},{0,4},{9,1},{1... | collective-permute-start | bytes 786440 | tf_op jit(solution)/shard_map/ppermute | solution.py:160
  31.9 13.1 %collective-permute-start.25 = (bf16[128,1024]{1,0:T(8,128)(2,1)S(1)}, bf16[128,1024]{1,0:T(8,128)(2,1)S(1)}, u32[]{:S(2)}, u32[]{:S(2)}) collective-permute-start(bf16[128,1024]{1,0:T(8,128)(2,1)S(1)} %collective-permute-done.23), channel_id=1, source_target_pairs={{0,8},{8,16},{16,24},{24,28},{28,20},{20,12},{12,4},{4,0},{1,9},{9... | collective-permute-start | bytes 786440 | tf_op jit(solution)/shard_map/ppermute | solution.py:159
  33.6 14.7 %collective-permute-start.26 = (bf16[128,1024]{1,0:T(8,128)(2,1)S(1)}, bf16[128,1024]{1,0:T(8,128)(2,1)S(1)}, u32[]{:S(2)}, u32[]{:S(2)}) collective-permute-start(bf16[128,1024]{1,0:T(8,128)(2,1)S(1)} %collective-permute-done.24), channel_id=1, source_target_pairs={{8,0},{16,8},{24,16},{28,24},{20,28},{12,20},{4,12},{0,4},{9,1},{1... | collective-permute-start | bytes 786440 | tf_op jit(solution)/shard_map/ppermute | solution.py:160
  37.1 12.9 %collective-permute-start.7 = (bf16[128,1024]{1,0:T(8,128)(2,1)S(1)}, bf16[128,1024]{1,0:T(8,128)(2,1)S(1)}, u32[]{:S(2)}, u32[]{:S(2)}) collective-permute-start(bf16[128,1024]{1,0:T(8,128)(2,1)S(1)} %collective-permute-done.5), channel_id=1, source_target_pairs={{0,8},{8,16},{16,24},{24,28},{28,20},{20,12},{12,4},{4,0},{1,9},{9... | collective-permute-start | bytes 786440 | tf_op jit(solution)/shard_map/ppermute | solution.py:159
  38.7 15.2 %collective-permute-start.8 = (bf16[128,1024]{1,0:T(8,128)(2,1)S(1)}, bf16[128,1024]{1,0:T(8,128)(2,1)S(1)}, u32[]{:S(2)}, u32[]{:S(2)}) collective-permute-start(bf16[128,1024]{1,0:T(8,128)(2,1)S(1)} %collective-permute-done.6), channel_id=1, source_target_pairs={{8,0},{16,8},{24,16},{28,24},{20,28},{12,20},{4,12},{0,4},{9,1},{1... | collective-permute-start | bytes 786440 | tf_op jit(solution)/shard_map/ppermute | solution.py:160
  42.7 12.4 %collective-permute-start.19 = (bf16[128,1024]{1,0:T(8,128)(2,1)S(1)}, bf16[128,1024]{1,0:T(8,128)(2,1)S(1)}, u32[]{:S(2)}, u32[]{:S(2)}) collective-permute-start(bf16[128,1024]{1,0:T(8,128)(2,1)S(1)} %collective-permute-done.17), channel_id=1, source_target_pairs={{0,8},{8,16},{16,24},{24,28},{28,20},{20,12},{12,4},{4,0},{1,9},{9... | collective-permute-start | bytes 786440 | tf_op jit(solution)/shard_map/ppermute | solution.py:159
  45.0 14.5 %collective-permute-start.20 = (bf16[128,1024]{1,0:T(8,128)(2,1)S(1)}, bf16[128,1024]{1,0:T(8,128)(2,1)S(1)}, u32[]{:S(2)}, u32[]{:S(2)}) collective-permute-start(bf16[128,1024]{1,0:T(8,128)(2,1)S(1)} %collective-permute-done.18), channel_id=1, source_target_pairs={{8,0},{16,8},{24,16},{28,24},{20,28},{12,20},{4,12},{0,4},{9,1},{1... | collective-permute-start | bytes 786440 | tf_op jit(solution)/shard_map/ppermute | solution.py:160
  48.3 12.8 %collective-permute-start.27 = (bf16[128,1024]{1,0:T(8,128)(2,1)S(1)}, bf16[128,1024]{1,0:T(8,128)(2,1)S(1)}, u32[]{:S(2)}, u32[]{:S(2)}) collective-permute-start(bf16[128,1024]{1,0:T(8,128)(2,1)S(1)} %collective-permute-done.25), channel_id=1, source_target_pairs={{0,8},{8,16},{16,24},{24,28},{28,20},{20,12},{12,4},{4,0},{1,9},{9... | collective-permute-start | bytes 786440 | tf_op jit(solution)/shard_map/ppermute | solution.py:159
  50.0 13.6 %collective-permute-start.9 = (bf16[64,1024]{1,0:T(8,128)(2,1)S(1)}, bf16[64,1024]{1,0:T(8,128)(2,1)S(1)}, u32[]{:S(2)}, u32[]{:S(2)}) collective-permute-start(bf16[64,1024]{1,0:T(8,128)(2,1)S(1)} %slice.40), channel_id=1, source_target_pairs={{0,8},{8,16},{16,24},{24,28},{28,20},{20,12},{12,4},{4,0},{1,9},{9... | collective-permute-start | bytes 393224 | tf_op jit(solution)/shard_map/ppermute | solution.py:159
  53.9 11.3 %collective-permute-start.10 = (bf16[64,1024]{1,0:T(8,128)(2,1)S(1)}, bf16[64,1024]{1,0:T(8,128)(2,1)S(1)}, u32[]{:S(2)}, u32[]{:S(2)}) collective-permute-start(bf16[64,1024]{1,0:T(8,128)(2,1)S(1)} %slice.41), channel_id=1, source_target_pairs={{8,0},{16,8},{24,16},{28,24},{20,28},{12,20},{4,12},{0,4},{9,1},{1... | collective-permute-start | bytes 393224 | tf_op jit(solution)/shard_map/ppermute | solution.py:160
  55.1 19.0 %collective-permute-start.28 = (bf16[128,1024]{1,0:T(8,128)(2,1)S(1)}, bf16[128,1024]{1,0:T(8,128)(2,1)S(1)}, u32[]{:S(2)}, u32[]{:S(2)}) collective-permute-start(bf16[128,1024]{1,0:T(8,128)(2,1)S(1)} %collective-permute-done.26), channel_id=1, source_target_pairs={{8,0},{16,8},{24,16},{28,24},{20,28},{12,20},{4,12},{0,4},{9,1},{1... | collective-permute-start | bytes 786440 | tf_op jit(solution)/shard_map/ppermute | solution.py:160
  59.5 15.2 %collective-permute-start.21 = (bf16[64,1024]{1,0:T(8,128)(2,1)S(1)}, bf16[64,1024]{1,0:T(8,128)(2,1)S(1)}, u32[]{:S(2)}, u32[]{:S(2)}) collective-permute-start(bf16[64,1024]{1,0:T(8,128)(2,1)S(1)} %slice.44), channel_id=1, source_target_pairs={{0,8},{8,16},{16,24},{24,28},{28,20},{20,12},{12,4},{4,0},{1,9},{9... | collective-permute-start | bytes 393224 | tf_op jit(solution)/shard_map/ppermute | solution.py:159
  61.2 14.6 %collective-permute-start.22 = (bf16[64,1024]{1,0:T(8,128)(2,1)S(1)}, bf16[64,1024]{1,0:T(8,128)(2,1)S(1)}, u32[]{:S(2)}, u32[]{:S(2)}) collective-permute-start(bf16[64,1024]{1,0:T(8,128)(2,1)S(1)} %slice.45), channel_id=1, source_target_pairs={{8,0},{16,8},{24,16},{28,24},{20,28},{12,20},{4,12},{0,4},{9,1},{1... | collective-permute-start | bytes 393224 | tf_op jit(solution)/shard_map/ppermute | solution.py:160
  63.6 19.8 %collective-permute-start.29 = (bf16[64,1024]{1,0:T(8,128)(2,1)S(1)}, bf16[64,1024]{1,0:T(8,128)(2,1)S(1)}, u32[]{:S(2)}, u32[]{:S(2)}) collective-permute-start(bf16[64,1024]{1,0:T(8,128)(2,1)S(1)} %slice.46), channel_id=1, source_target_pairs={{0,8},{8,16},{16,24},{24,28},{28,20},{20,12},{12,4},{4,0},{1,9},{9... | collective-permute-start | bytes 393224 | tf_op jit(solution)/shard_map/ppermute | solution.py:159
  123.3 14.6 %collective-permute-start.37 = (bf16[128,1024]{1,0:T(8,128)(2,1)S(1)}, bf16[128,1024]{1,0:T(8,128)(2,1)S(1)}, u32[]{:S(2)}, u32[]{:S(2)}) collective-permute-start(bf16[128,1024]{1,0:T(8,128)(2,1)S(1)} %get-tuple-element.152), channel_id=1, source_target_pairs={{0,1},{1,0},{2,3},{3,2},{4,5},{5,4},{6,7},{7,6},{8,9},{9,8},{10,11... | collective-permute-start | bytes 786440 | tf_op jit(solution)/shard_map/ppermute | solution.py:119
  126.6 11.3 %collective-permute-start.41 = (bf16[128,1024]{1,0:T(8,128)(2,1)S(1)}, bf16[128,1024]{1,0:T(8,128)(2,1)S(1)}, u32[]{:S(2)}, u32[]{:S(2)}) collective-permute-start(bf16[128,1024]{1,0:T(8,128)(2,1)S(1)} %add_convert_fusion.3), channel_id=1, source_target_pairs={{0,2},{1,3},{2,0},{3,1},{4,6},{5,7},{6,4},{7,5},{8,10},{9,11},{10,... | collective-permute-start | bytes 786440 | tf_op jit(solution)/shard_map/ppermute | solution.py:119
  135.8 13.2 %collective-permute-start.60 = (bf16[256,1024]{1,0:T(8,128)(2,1)S(1)}, bf16[256,1024]{1,0:T(8,128)(2,1)S(1)}, u32[]{:S(2)}, u32[]{:S(2)}) collective-permute-start(bf16[256,1024]{1,0:T(8,128)(2,1)S(1)} %get-tuple-element.120), channel_id=1, source_target_pairs={{0,8},{8,16},{16,24},{24,28},{28,20},{20,12},{12,4},{4,0},{1,9},{9... | collective-permute-start | bytes 1572872 | tf_op jit(solution)/shard_map/ppermute | solution.py:159
  137.4 12.9 %collective-permute-start.61 = (bf16[256,1024]{1,0:T(8,128)(2,1)S(1)}, bf16[256,1024]{1,0:T(8,128)(2,1)S(1)}, u32[]{:S(2)}, u32[]{:S(2)}) collective-permute-start(bf16[256,1024]{1,0:T(8,128)(2,1)S(1)} %get-tuple-element.121), channel_id=1, source_target_pairs={{8,0},{16,8},{24,16},{28,24},{20,28},{12,20},{4,12},{0,4},{9,1},{1... | collective-permute-start | bytes 1572872 | tf_op jit(solution)/shard_map/ppermute | solution.py:160
  139.2 14.5 %collective-permute-start.42 = (bf16[128,1024]{1,0:T(8,128)(2,1)S(1)}, bf16[128,1024]{1,0:T(8,128)(2,1)S(1)}, u32[]{:S(2)}, u32[]{:S(2)}) collective-permute-start(bf16[128,1024]{1,0:T(8,128)(2,1)S(1)} %get-tuple-element.93), channel_id=1, source_target_pairs={{0,1},{1,0},{2,3},{3,2},{4,5},{5,4},{6,7},{7,6},{8,9},{9,8},{10,11... | collective-permute-start | bytes 786440 | tf_op jit(solution)/shard_map/ppermute | solution.py:119
  145.5 15.0 %collective-permute-start.49 = (f32[6,1024]{1,0:T(8,128)S(1)}, f32[6,1024]{1,0:T(8,128)S(1)}, u32[]{:S(2)}, u32[]{:S(2)}) collective-permute-start(f32[6,1024]{1,0:T(8,128)S(1)} %fusion.12.refs_4_), channel_id=1, source_target_pairs={{0,2},{1,3},{2,0},{3,1},{4,6},{5,7},{6,4},{7,5},{8,10},{9,11},{10,... | collective-permute-start | bytes 73736 | tf_op jit(solution)/shard_map/ppermute | solution.py:119
  151.6 19.6 %collective-permute-start.62 = (bf16[256,1024]{1,0:T(8,128)(2,1)S(1)}, bf16[256,1024]{1,0:T(8,128)(2,1)S(1)}, u32[]{:S(2)}, u32[]{:S(2)}) collective-permute-start(bf16[256,1024]{1,0:T(8,128)(2,1)S(1)} %get-tuple-element.122), channel_id=1, source_target_pairs={{0,8},{8,16},{16,24},{24,28},{28,20},{20,12},{12,4},{4,0},{1,9},{9... | collective-permute-start | bytes 1572872 | tf_op jit(solution)/shard_map/ppermute | solution.py:159
  153.0 18.2 %collective-permute-start.63 = (bf16[256,1024]{1,0:T(8,128)(2,1)S(1)}, bf16[256,1024]{1,0:T(8,128)(2,1)S(1)}, u32[]{:S(2)}, u32[]{:S(2)}) collective-permute-start(bf16[256,1024]{1,0:T(8,128)(2,1)S(1)} %get-tuple-element.123), channel_id=1, source_target_pairs={{8,0},{16,8},{24,16},{28,24},{20,28},{12,20},{4,12},{0,4},{9,1},{1... | collective-permute-start | bytes 1572872 | tf_op jit(solution)/shard_map/ppermute | solution.py:160
  179.4 12.5 %collective-permute-start.65 = (bf16[128,1024]{1,0:T(8,128)(2,1)S(1)}, bf16[128,1024]{1,0:T(8,128)(2,1)S(1)}, u32[]{:S(2)}, u32[]{:S(2)}) collective-permute-start(bf16[128,1024]{1,0:T(8,128)(2,1)S(1)} %get-tuple-element.125), channel_id=1, source_target_pairs={{8,0},{16,8},{24,16},{28,24},{20,28},{12,20},{4,12},{0,4},{9,1},{1... | collective-permute-start | bytes 786440 | tf_op jit(solution)/shard_map/ppermute | solution.py:160
  180.8 12.6 %collective-permute-start.66 = (bf16[128,1024]{1,0:T(8,128)(2,1)S(1)}, bf16[128,1024]{1,0:T(8,128)(2,1)S(1)}, u32[]{:S(2)}, u32[]{:S(2)}) collective-permute-start(bf16[128,1024]{1,0:T(8,128)(2,1)S(1)} %get-tuple-element.126), channel_id=1, source_target_pairs={{0,8},{8,16},{16,24},{24,28},{28,20},{20,12},{12,4},{4,0},{1,9},{9... | collective-permute-start | bytes 786440 | tf_op jit(solution)/shard_map/ppermute | solution.py:159
  181.8 12.9 %collective-permute-start.67 = (bf16[128,1024]{1,0:T(8,128)(2,1)S(1)}, bf16[128,1024]{1,0:T(8,128)(2,1)S(1)}, u32[]{:S(2)}, u32[]{:S(2)}) collective-permute-start(bf16[128,1024]{1,0:T(8,128)(2,1)S(1)} %get-tuple-element.127), channel_id=1, source_target_pairs={{8,0},{16,8},{24,16},{28,24},{20,28},{12,20},{4,12},{0,4},{9,1},{1... | collective-permute-start | bytes 786440 | tf_op jit(solution)/shard_map/ppermute | solution.py:160
  (53 other events, 367.1 us)
